TPU v7x, 32 devices: a whole 2x2x4 slice. The times are simulated.
32 devices in a mesh: rows: 16 (over z, y, x), chip: 2 (over core).
Axes of the slice: x: 2, y: 2, z: 4, core: 2. Of those that a mesh axis runs over, the one named last changes fastest.
Arguments:
- hamiltonian: float32 [24576, 24576], P(('rows', 'chip')), may hold values from -1 to 4, as said below
- vectors: float32 [24576, 256], P(('rows', 'chip')), may hold values from -6 to 6
Outputs:
- ritz_block: float32 [24576, 256], P(('rows', 'chip'))
- projected: float32 [256, 256], replicated
Inputs may be any that keep to these rules, and one draw needn't show every extreme that they name: hamiltonian is symmetric and positive definite.
All inputs are finite; a program needn't handle non-finite values.
Results may differ from a plain program's by a relative error of at most 0.003.
Values may be sent and summed in bfloat16 or wider, within the bound.
No kernel may reach another device: no remote copies, remote signals or barrier semaphores. Data moves between devices by JAX's collectives and lax.ppermute only.
A program may use at most 128 MiB of HBM per device.

v0:
```python
import jax
import jax.numpy as jnp
from jax import lax
from jax.experimental import pallas as pl
from jax.experimental.pallas import tpu as pltpu
from jax.sharding import PartitionSpec as P


AXES = ("rows", "chip")
F32 = jnp.float32
BF16 = jnp.bfloat16
NN = (((1,), (0,)), ((), ()))
NT = (((1,), (1,)), ((), ()))


def shards_plain(hamiltonian, vectors):
    highest = lax.Precision.HIGHEST
    basis = vectors.astype(BF16)
    widened = basis.astype(F32)
    correlation_part = jnp.dot(basis.T, basis, preferred_element_type=F32)
    whole = lax.all_gather(basis, AXES, axis=0, tiled=True)
    product = jnp.dot(hamiltonian, whole.astype(F32), precision=highest)
    coupling_part = jnp.dot(widened.T, product, precision=highest)
    gram_part = jnp.dot(product.T, product, precision=highest)
    correlation, coupling, gram = lax.psum((correlation_part, coupling_part, gram_part), AXES)
    symmetric = 0.5 * (coupling + coupling.T)
    lower = jnp.linalg.cholesky(correlation)
    half = lax.linalg.triangular_solve(lower, symmetric, left_side=True, lower=True)
    projected = lax.linalg.triangular_solve(lower, half.T, left_side=True, lower=True)
    factor = jnp.linalg.cholesky(gram)
    rotated = lax.linalg.triangular_solve(factor, product.T, left_side=True, lower=True)
    return (rotated.T * jnp.sqrt(F32(hamiltonian.shape[1])), projected)


def split(a):
    high = a.astype(BF16)
    return high, (a - high.astype(F32)).astype(BF16)


def dot1(a, b, dims=NN):
    return lax.dot_general(a, b, dims, preferred_element_type=F32)


def dot3(a, b, dims=NN):
    ah, al = split(a)
    bh, bl = split(b)
    return dot1(ah, bh, dims) + (dot1(ah, bl, dims) + dot1(al, bh, dims))


def stage_call(hamiltonian, units, places, acc):
    n = len(units)
    rows, _ = hamiltonian.shape
    width = sum(a.shape[0] for a in units[0])
    nvec = units[0][0].shape[1]
    first = acc is None
    nbuf = min(3, n)
    pieces = []
    for i, unit in enumerate(units):
        at = 0
        for a in unit:
            pieces.append((i, at, a))
            at += a.shape[0]
    count = len(pieces)

    def body(places_ref, h_ref, *rest):
        piece_refs = rest[:count]
        rest = rest[count:]
        acc_refs = ()
        if not first:
            acc_refs, rest = rest[:2], rest[2:]
        out_ref, corr_ref, hbuf, ubuf, hsem, usem = rest

        def hcopy(i, slot):
            at = pl.multiple_of(places_ref[i] * width, 128)
            return pltpu.make_async_copy(h_ref.at[:, pl.ds(at, width)], hbuf.at[slot], hsem.at[slot])

        for i in range(nbuf):
            hcopy(i, i).start()
        for (i, at, a), ref in zip(pieces, piece_refs):
            pltpu.make_async_copy(ref, ubuf.at[i, pl.ds(at, a.shape[0]), :], usem.at[i]).start()
        if first:
            out_ref[...] = jnp.zeros_like(out_ref)
            corr_ref[...] = jnp.zeros_like(corr_ref)
        else:
            out_ref[...] = acc_refs[0][...]
            corr_ref[...] = acc_refs[1][...]

        def step(i, _):
            slot = lax.rem(i, nbuf)
            pltpu.make_async_copy(ubuf.at[i], ubuf.at[i], usem.at[i]).wait()
            u = ubuf[i]
            corr_ref[...] += lax.dot_general(u, u, (((0,), (0,)), ((), ())), preferred_element_type=F32)
            hcopy(i, slot).wait()
            high, low = split(hbuf[slot])
            out_ref[...] += dot1(high, u) + dot1(low, u)

            @pl.when(i + nbuf < n)
            def _():
                hcopy(i + nbuf, slot).start()

            return 0

        lax.fori_loop(0, n, step, 0)

    any_spec = pl.BlockSpec(memory_space=pl.ANY)
    vmem = pl.BlockSpec(memory_space=pltpu.VMEM)
    operands = [places, hamiltonian, *(a for _, _, a in pieces)]
    in_specs = [pl.BlockSpec(memory_space=pltpu.SMEM), any_spec] + [any_spec] * count
    aliases = {}
    if not first:
        aliases = {len(operands): 0, len(operands) + 1: 1}
        operands += list(acc)
        in_specs += [vmem, vmem]
    return pl.pallas_call(
        body,
        name="stage_product",
        out_shape=(jax.ShapeDtypeStruct((rows, nvec), F32), jax.ShapeDtypeStruct((nvec, nvec), F32)),
        in_specs=in_specs,
        out_specs=(vmem, vmem),
        scratch_shapes=[
            pltpu.VMEM((nbuf, rows, width), F32),
            pltpu.VMEM((n, width, nvec), BF16),
            pltpu.SemaphoreType.DMA((nbuf,)),
            pltpu.SemaphoreType.DMA((n,)),
        ],
        input_output_aliases=aliases,
        cost_estimate=pl.CostEstimate(
            flops=4 * n * rows * width * nvec, transcendentals=0, bytes_accessed=4 * n * rows * width
        ),
        compiler_params=pltpu.CompilerParams(vmem_limit_bytes=48 << 20),
    )(*operands)


def parts_call(product, basis, own):
    _, nvec = product.shape
    half = nvec // 2
    total = 6 * half
    piece = total // 8

    def body(own_ref, p_ref, b_ref, keep_ref, send_ref, buf):
        p = p_ref[...]
        pt_high, pt_low = split(p.T)
        bt = b_ref[...].astype(F32).T.astype(BF16)
        p_high, p_low = split(p)
        cross = dot1(pt_high, p_low)
        gram = dot1(pt_high, p_high) + (cross + dot1(pt_low, p_high))
        coupling = dot1(bt, p_high) + dot1(bt, p_low)
        coupling = 0.5 * (coupling + coupling.T)
        at = 0
        for a in (gram, coupling):
            for i, j in ((0, 0), (1, 0), (1, 1)):
                buf[at * half:(at + 1) * half, :] = a[i * half:(i + 1) * half, j * half:(j + 1) * half]
                at += 1
        own = own_ref[0]
        for m in range(4):
            keep_ref[m] = buf[pl.ds(pl.multiple_of((own ^ m) * piece, 8), piece), :]
            send_ref[m] = buf[pl.ds(pl.multiple_of((own ^ (m + 4)) * piece, 8), piece), :]

    vmem = pl.BlockSpec(memory_space=pltpu.VMEM)
    shape = jax.ShapeDtypeStruct((4, piece, half), F32)
    return pl.pallas_call(
        body,
        name="partial_sums",
        out_shape=(shape, shape),
        in_specs=[pl.BlockSpec(memory_space=pltpu.SMEM), vmem, vmem],
        out_specs=(vmem, vmem),
        scratch_shapes=[pltpu.VMEM((total, half), F32)],
        compiler_params=pltpu.CompilerParams(vmem_limit_bytes=48 << 20),
    )(own, product, basis)


def inverse_factor(a, out_ref, work_a, work_w):
    n = a.shape[0]
    i = lax.broadcasted_iota(jnp.int32, (n, n), 0)
    j = lax.broadcasted_iota(jnp.int32, (n, n), 1)
    eye = jnp.where(i == j, 1.0, 0.0).astype(F32)
    weight = jnp.where(i > j, 1.0, jnp.where(i == j, 0.5, 0.0)).astype(F32)
    diagonal = jnp.where(i == j, a, 0.0)
    scale_row = lax.rsqrt(jnp.sum(diagonal, axis=0, keepdims=True))
    scale_col = lax.rsqrt(jnp.sum(diagonal, axis=1, keepdims=True))
    k = a * scale_row * scale_col
    e = k - eye
    x = (e * weight).astype(BF16)
    x = (e - dot1(x, x, NT)) * weight
    xh = x.astype(BF16)
    m = eye - x + dot1(xh, xh) * jnp.where(i >= j, 1.0, 0.0)

    def residual(m):
        return dot3(dot3(m, k), m, NT) - eye

    m = m - dot3(residual(m) * weight, m)
    e = residual(m)
    norm = jnp.max(jnp.sum(jnp.abs(e), axis=1))
    m = m - dot3(e * weight, m)
    out_ref[...] = m * scale_row

    @pl.when(jnp.logical_not(norm < 3e-3))
    def _():
        work_a[...] = a
        work_w[...] = eye
        lane = lax.broadcasted_iota(jnp.int32, (1, n), 1)
        row = lax.broadcasted_iota(jnp.int32, (n, 1), 0)

        def column(s, _):
            top = work_a[pl.ds(s, 1), :]
            top_w = work_w[pl.ds(s, 1), :]
            inverse = 1.0 / jnp.sum(jnp.where(lane == s, top, 0.0), axis=1, keepdims=True)
            at = work_a[...]
            col = jnp.sum(jnp.where(lane == s, at, 0.0), axis=1, keepdims=True)
            col = jnp.where(row > s, col * inverse, 0.0)
            work_a[...] = at - col * top
            work_w[...] = work_w[...] - col * top_w
            return 0

        lax.fori_loop(0, n, column, 0)
        pivots = jnp.sum(jnp.where(i == j, work_a[...], 0.0), axis=1, keepdims=True)
        out_ref[...] = work_w[...] * lax.rsqrt(pivots)


def inverse_call(a):
    vmem = pl.BlockSpec(memory_space=pltpu.VMEM)
    square = pltpu.VMEM(a.shape, F32)

    def body(a_ref, out_ref, work_a, work_w):
        inverse_factor(a_ref[...], out_ref, work_a, work_w)

    return pl.pallas_call(
        body,
        name="inverse_factor",
        out_shape=jax.ShapeDtypeStruct(a.shape, F32),
        in_specs=[vmem],
        out_specs=vmem,
        scratch_shapes=[square, square],
        cost_estimate=pl.CostEstimate(flops=60 * a.shape[0] ** 3, transcendentals=0, bytes_accessed=0),
    )(a)


def finish_call(product, mine, other, low, own, scale):
    rows, nvec = product.shape
    half = nvec // 2
    _, piece, _ = mine.shape

    def body(own_ref, p_ref, mine_ref, other_ref, low_ref, ritz_ref, projected_ref, buf, whole, inv, work_a, work_w):
        own = own_ref[0]
        for m in range(4):
            buf[pl.ds(pl.multiple_of((own ^ m) * piece, 8), piece), :] = mine_ref[m]
            buf[pl.ds(pl.multiple_of((own ^ (m + 4)) * piece, 8), piece), :] = other_ref[m]
        for q in range(2):
            at = 3 * q * half
            corner = buf[at + half:at + 2 * half, :]
            whole[q, :half, :half] = buf[at:at + half, :]
            whole[q, half:, :half] = corner
            whole[q, :half, half:] = corner.T
            whole[q, half:, half:] = buf[at + 2 * half:at + 3 * half, :]
        inverse_factor(whole[0], inv, work_a, work_w)
        ritz_ref[...] = dot3(p_ref[...], inv[...] * scale, NT)
        low = low_ref[...]
        projected_ref[...] = dot3(dot3(low, whole[1]), low, NT)

    vmem = pl.BlockSpec(memory_space=pltpu.VMEM)
    square = pltpu.VMEM((nvec, nvec), F32)
    return pl.pallas_call(
        body,
        name="finish",
        out_shape=(jax.ShapeDtypeStruct((rows, nvec), F32), jax.ShapeDtypeStruct((nvec, nvec), F32)),
        in_specs=[pl.BlockSpec(memory_space=pltpu.SMEM), vmem, vmem, vmem, vmem],
        out_specs=(vmem, vmem),
        scratch_shapes=[
            pltpu.VMEM((6 * half, half), F32),
            pltpu.VMEM((2, nvec, nvec), F32),
            square,
            square,
            square,
        ],
        compiler_params=pltpu.CompilerParams(vmem_limit_bytes=48 << 20),
    )(own, product, mine, other, low)


WHOLE = (0, 8)
STAGES = (
    ((4, ((0, 4, WHOLE),)), (1, ((0, 1, WHOLE),)), (2, ((0, 2, WHOLE),))),
    ((5, ((4, 1, WHOLE),)), (6, ((4, 2, WHOLE),)), (8, ((0, 8, WHOLE),)), (3, ((2, 1, WHOLE),))),
    ((7, ((5, 2, WHOLE),)),),
    ((12, ((8, 4, WHOLE),)), (9, ((8, 1, WHOLE),)), (10, ((8, 2, WHOLE),))),
    ((14, ((12, 2, WHOLE),)), (13, ((9, 4, WHOLE),)), (11, ((10, 1, WHOLE),))),
    ((15, ((14, 1, (0, 4)), (13, 2, (4, 8)))),),
)
TURNS = (
    ((0,), ()),
    ((4, 1, 2), (0,)),
    ((5, 6), (4, 1, 2)),
    ((8, 3, 7), (5, 6)),
    ((12, 9, 10), (8, 3, 7)),
    ((14, 13, 11), (12, 9, 10)),
    ((15,), (14, 13, 11)),
    ((), (15,)),
)


def shards_pairs(hamiltonian, vectors):
    chips = lax.axis_size("rows")
    here = lax.axis_index("rows")
    core = lax.axis_index("chip")
    width = vectors.shape[0]

    def from_chip(a, m):
        return lax.ppermute(a, "rows", [(s, s ^ m) for s in range(chips)])

    def from_core(a):
        return lax.ppermute(a, "chip", [(0, 1), (1, 0)])

    basis = vectors.astype(BF16)
    mine = {0: (basis,)}
    acc = None
    other = {}
    for t, (near, far) in enumerate(TURNS):
        if 0 < t <= len(STAGES):
            for m, parts in STAGES[t - 1]:
                got = []
                for source, step, (lo, hi) in parts:
                    a = mine[source][0]
                    if (lo, hi) != WHOLE:
                        a = a[lo * width // 8:hi * width // 8]
                    got.append(from_chip(a, step))
                mine[m] = tuple(got)
        for m in near:
            other[m] = tuple(from_core(a) for a in mine[m])
        units = [mine[m] for m in near] + [other[m] for m in far]
        ids = jnp.array([2 * m for m in near] + [2 * m + 1 for m in far], jnp.int32)
        acc = stage_call(hamiltonian, units, (2 * here + core) ^ ids, acc)
    product, correlation = acc
    own = (core * 4 + here % 4).astype(jnp.int32).reshape(1)
    keep, send = parts_call(product, basis, own)
    a = keep + from_core(send)
    b = a[0] + from_chip(a[1], 1) + from_chip(a[2], 2) + from_chip(a[3], 3)
    b = b + from_chip(b, 4) + from_chip(b, 8) + from_chip(b, 12)
    mine4 = jnp.stack([b, from_chip(b, 1), from_chip(b, 2), from_chip(b, 3)])
    other4 = from_core(mine4)
    low = inverse_call(correlation)
    scale = float(hamiltonian.shape[1]) ** 0.5
    return finish_call(product, mine4, other4, low, own, scale)


def solution(mesh):
    in_specs = (P(AXES, None), P(AXES, None))
    out_specs = (P(AXES, None), P())
    pairs = mesh.shape["rows"] == 16 and mesh.shape["chip"] == 2
    body = shards_pairs if pairs else shards_plain
    return jax.shard_map(body, mesh=mesh, in_specs=in_specs, out_specs=out_specs, check_vma=False)
```

profile of v0, /device:TPU:0, one launch (start us, length us, event | category | flops | bytes accessed | tf_op | source)
XLA Modules:
  0.0 223.5 jit_solution(4966599147963590259)
XLA Ops:
  1.9 3.1 %collective-permute-start.21 = (bf16[768,256]{1,0:T(8,128)(2,1)S(1)}, bf16[768,256]{1,0:T(8,128)(2,1)S(1)}, u32[]{:S(2)}, u32[]{:S(2)}) collective-permute-start(bf16[768,256]{1,0:T(8,128)(2,1)S(1)} %convert_element_type.3.rest_0_.b_ref), channel_id=1, source_target_pairs={{0,8},{2,10},{4,12},{6,14},{8,0},{10,2},{12,4},{14,6},{16,24},{18,... | collective-permute-start | bytes 1179656 | tf_op jit(solution)/shard_map/ppermute | solution.py:307
  8.0 2.6 %collective-permute-start = (bf16[768,256]{1,0:T(8,128)(2,1)S(1)}, bf16[768,256]{1,0:T(8,128)(2,1)S(1)}, u32[]{:S(2)}, u32[]{:S(2)}) collective-permute-start(bf16[768,256]{1,0:T(8,128)(2,1)S(1)} %convert_element_type.3.rest_0_.b_ref), channel_id=1, source_target_pairs={{0,16},{2,18},{4,20},{6,22},{8,24},{10,26},{12,28},{14,30},{16,0},... | collective-permute-start | bytes 1179656 | tf_op jit(solution)/shard_map/ppermute | solution.py:307
  10.6 7.9 %collective-permute-done.21.rest_0_ = bf16[768,256]{1,0:T(8,128)(2,1)S(1)} collective-permute-done((bf16[768,256]{1,0:T(8,128)(2,1)S(1)}, bf16[768,256]{1,0:T(8,128)(2,1)S(1)}, u32[]{:S(2)}, u32[]{:S(2)}) %collective-permute-start.21) | collective-permute-done | bytes 393248 | tf_op jit(solution)/shard_map/ppermute | solution.py:307
  18.5 2.6 %collective-permute-start.22 = (bf16[768,256]{1,0:T(8,128)(2,1)S(1)}, bf16[768,256]{1,0:T(8,128)(2,1)S(1)}, u32[]{:S(2)}, u32[]{:S(2)}) collective-permute-start(bf16[768,256]{1,0:T(8,128)(2,1)S(1)} %collective-permute-done.21.rest_0_), channel_id=1, source_target_pairs={{0,2},{2,0},{4,6},{6,4},{8,10},{10,8},{12,14},{14,12},{16,18},{18,... | collective-permute-start | bytes 1179656 | tf_op jit(solution)/shard_map/ppermute | solution.py:307
  21.1 2.6 %stage_product.8 = (f32[768,256]{1,0:T(8,128)S(1)}, f32[256,256]{1,0:T(8,128)S(1)}) custom-call(s32[1]{0:T(128)} %bitcast.1.places_ref, f32[768,24576]{1,0:T(8,128)} %h_ref.15, bf16[768,256]{1,0:T(8,128)(2,1)S(1)} %convert_element_type.3.rest_0_.b_ref), custom_call_target="tpu_custom_call" | custom-call | flops 603979776 | bytes 2359296 | tf_op jit(solution)/shard_map/stage_product/pallas_call | solution.py:114
  23.7 2.6 %collective-permute-start.26 = (bf16[768,256]{1,0:T(8,128)(2,1)S(1)}, bf16[768,256]{1,0:T(8,128)(2,1)S(1)}, u32[]{:S(2)}, u32[]{:S(2)}) collective-permute-start(bf16[768,256]{1,0:T(8,128)(2,1)S(1)} %collective-permute-done.21.rest_0_), channel_id=1, source_target_pairs={{0,4},{2,6},{4,0},{6,2},{8,12},{10,14},{12,8},{14,10},{16,20},{18,... | collective-permute-start | bytes 1179656 | tf_op jit(solution)/shard_map/ppermute | solution.py:307
  29.5 4.8 %collective-permute-done.26.rest_1_ = bf16[768,256]{1,0:T(8,128)(2,1)S(1)} collective-permute-done((bf16[768,256]{1,0:T(8,128)(2,1)S(1)}, bf16[768,256]{1,0:T(8,128)(2,1)S(1)}, u32[]{:S(2)}, u32[]{:S(2)}) %collective-permute-start.26) | collective-permute-done | bytes 393248 | tf_op jit(solution)/shard_map/ppermute | solution.py:307
  36.3 4.6 %collective-permute-done.19.rest_1_ = bf16[768,256]{1,0:T(8,128)(2,1)S(1)} collective-permute-done((bf16[768,256]{1,0:T(8,128)(2,1)S(1)}, bf16[768,256]{1,0:T(8,128)(2,1)S(1)}, u32[]{:S(2)}, u32[]{:S(2)}) %collective-permute-start.19) | collective-permute-done | bytes 393248 | tf_op jit(solution)/shard_map/ppermute | solution.py:307
  43.4 2.4 %collective-permute-done.11.rest_2_ = bf16[768,256]{1,0:T(8,128)(2,1)S(1)} collective-permute-done((bf16[768,256]{1,0:T(8,128)(2,1)S(1)}, bf16[768,256]{1,0:T(8,128)(2,1)S(1)}, u32[]{:S(2)}, u32[]{:S(2)}) %collective-permute-start.11) | collective-permute-done | bytes 393248 | tf_op jit(solution)/shard_map/ppermute | solution.py:307
  45.9 2.2 collective-permute-done.5.rest_1_
  48.7 3.8 %collective-permute-done.23.rest_2_ = bf16[768,256]{1,0:T(8,128)(2,1)S(1)} collective-permute-done((bf16[768,256]{1,0:T(8,128)(2,1)S(1)}, bf16[768,256]{1,0:T(8,128)(2,1)S(1)}, u32[]{:S(2)}, u32[]{:S(2)}) %collective-permute-start.23) | collective-permute-done | bytes 393248 | tf_op jit(solution)/shard_map/ppermute | solution.py:307
  52.6 3.1 %collective-permute-start.6 = (bf16[768,256]{1,0:T(8,128)(2,1)S(1)}, bf16[768,256]{1,0:T(8,128)(2,1)S(1)}, u32[]{:S(2)}, u32[]{:S(2)}) collective-permute-start(bf16[768,256]{1,0:T(8,128)(2,1)S(1)} %collective-permute-done.5.rest_1_), channel_id=1, source_target_pairs={{0,8},{2,10},{4,12},{6,14},{8,0},{10,2},{12,4},{14,6},{16,24},{18,... | collective-permute-start | bytes 1179656 | tf_op jit(solution)/shard_map/ppermute | solution.py:307
  55.7 7.0 %stage_product.9 = (f32[768,256]{1,0:T(8,128)S(1)}, f32[256,256]{1,0:T(8,128)S(1)}) custom-call(s32[4]{0:T(128)S(1)} %broadcast_xor_fusion.4.places_ref, f32[768,24576]{1,0:T(8,128)} %h_ref.15, bf16[768,256]{1,0:T(8,128)(2,1)S(1)} %collective-permute-done.21.rest_0_, ...), custom_call_target="tpu_custom_call", output_to_operand_aliasing={{0}: (6, {}), {1}: (7, {})} | custom-call | flops 2415919104 | bytes 9437184 | tf_op jit(solution)/shard_map/stage_product/pallas_call | solution.py:114
  65.1 8.3 %stage_product.10 = (f32[768,256]{1,0:T(8,128)S(1)}, f32[256,256]{1,0:T(8,128)S(1)}) custom-call(s32[5]{0:T(128)S(1)} %broadcast_xor_fusion.places_ref, f32[768,24576]{1,0:T(8,128)} %h_ref.15, bf16[768,256]{1,0:T(8,128)(2,1)S(1)} %collective-permute-done.22.rest_0_, ...), custom_call_target="tpu_custom_call", output_to_operand_aliasing={{0}: (7, {}), {1}: (8, {})} | custom-call | flops 3019898880 | bytes 11796480 | tf_op jit(solution)/shard_map/stage_product/pallas_call | solution.py:114
  73.4 8.3 %stage_product.11 = (f32[768,256]{1,0:T(8,128)S(1)}, f32[256,256]{1,0:T(8,128)S(1)}) custom-call(s32[5]{0:T(128)S(1)} %broadcast_xor_fusion.1.places_ref, f32[768,24576]{1,0:T(8,128)} %h_ref.15, bf16[768,256]{1,0:T(8,128)(2,1)S(1)} %collective-permute-done.rest_0_, ...), custom_call_target="tpu_custom_call", output_to_operand_aliasing={{0}: (7, {}), {1}: (8, {})} | custom-call | flops 3019898880 | bytes 11796480 | tf_op jit(solution)/shard_map/stage_product/pallas_call | solution.py:114
  84.3 9.5 %stage_product.12 = (f32[768,256]{1,0:T(8,128)S(1)}, f32[256,256]{1,0:T(8,128)S(1)}) custom-call(s32[6]{0:T(128)S(1)} %broadcast_xor_fusion.2.places_ref, f32[768,24576]{1,0:T(8,128)} %h_ref.15, bf16[768,256]{1,0:T(8,128)(2,1)S(1)} %collective-permute-done.1.rest_0_, ...), custom_call_target="tpu_custom_call", output_to_operand_aliasing={{0}: (8, {}), {1}: (9, {})} | custom-call | flops 3623878656 | bytes 14155776 | tf_op jit(solution)/shard_map/stage_product/pallas_call | solution.py:114
  94.5 9.5 %stage_product.13 = (f32[768,256]{1,0:T(8,128)S(1)}, f32[256,256]{1,0:T(8,128)S(1)}) custom-call(s32[6]{0:T(128)S(1)} %broadcast_xor_fusion.3.places_ref, f32[768,24576]{1,0:T(8,128)} %h_ref.15, bf16[768,256]{1,0:T(8,128)(2,1)S(1)} %collective-permute-done.2.rest_0_, ...), custom_call_target="tpu_custom_call", output_to_operand_aliasing={{0}: (8, {}), {1}: (9, {})} | custom-call | flops 3623878656 | bytes 14155776 | tf_op jit(solution)/shard_map/stage_product/pallas_call | solution.py:114
  104.1 7.0 %stage_product.14 = (f32[768,256]{1,0:T(8,128)S(1)}, f32[256,256]{1,0:T(8,128)S(1)}) custom-call(s32[4]{0:T(128)S(1)} %broadcast_xor_fusion.5.places_ref, f32[768,24576]{1,0:T(8,128)} %h_ref.15, bf16[384,256]{1,0:T(8,128)(2,1)S(1)} %collective-permute-done.3.rest_0_, ...), custom_call_target="tpu_custom_call", output_to_operand_aliasing={{0}: (7, {}), {1}: (8, {})} | custom-call | flops 2415919104 | bytes 9437184 | tf_op jit(solution)/shard_map/stage_product/pallas_call | solution.py:114
  111.1 2.6 %stage_product.15 = (f32[768,256]{1,0:T(8,128)S(1)}, f32[256,256]{1,0:T(8,128)S(1)}) custom-call(s32[1]{0:T(128)S(6)} %xor.41.places_ref, f32[768,24576]{1,0:T(8,128)} %h_ref.15, bf16[384,256]{1,0:T(8,128)(2,1)S(1)} %collective-permute-done.4.rest_0_, ...), custom_call_target="tpu_custom_call", output_to_operand_aliasing={{0}: (4, {}), {1}: (5, {})} | custom-call | flops 603979776 | bytes 2359296 | tf_op jit(solution)/shard_map/stage_product/pallas_call | solution.py:114
  120.4 2.3 %collective-permute-done.35 = f32[96,128]{1,0:T(8,128)S(1)} collective-permute-done((f32[96,128]{1,0:T(8,128)S(1)}, f32[96,128]{1,0:T(8,128)S(1)}, u32[]{:S(2)}, u32[]{:S(2)}) %collective-permute-start.35) | collective-permute-done | bytes 49184 | tf_op jit(solution)/shard_map/ppermute | solution.py:307
  123.5 3.0 %collective-permute-start.38 = (f32[96,128]{1,0:T(8,128)S(1)}, f32[96,128]{1,0:T(8,128)S(1)}, u32[]{:S(2)}, u32[]{:S(2)}) collective-permute-start(f32[96,128]{1,0:T(8,128)S(1)} %fusion.2), channel_id=1, source_target_pairs={{0,16},{2,18},{4,20},{6,22},{8,24},{10,26},{12,28},{14,30},{16,0},... | collective-permute-start | bytes 147464 | tf_op jit(solution)/shard_map/ppermute | solution.py:307
  128.6 3.8 %collective-permute-done.39 = f32[96,128]{1,0:T(8,128)S(1)} collective-permute-done((f32[96,128]{1,0:T(8,128)S(1)}, f32[96,128]{1,0:T(8,128)S(1)}, u32[]{:S(2)}, u32[]{:S(2)}) %collective-permute-start.39) | collective-permute-done | bytes 49184 | tf_op jit(solution)/shard_map/ppermute | solution.py:307
  139.5 41.5 %inverse_factor.1.low_ref = f32[256,256]{1,0:T(8,128)} custom-call(f32[256,256]{1,0:T(8,128)} %copy-done), custom_call_target="tpu_custom_call" | custom-call | flops 1006632960 | tf_op jit(solution)/shard_map/inverse_factor/pallas_call | solution.py:227
  181.9 41.6 %finish.1 = (f32[768,256]{1,0:T(8,128)}, f32[256,256]{1,0:T(8,128)}) custom-call(s32[1]{0:T(128)} %bitcast.own_ref, f32[768,256]{1,0:T(8,128)S(1)} %get-tuple-element.34.p_ref, f32[4,96,128]{2,1,0:T(8,128)S(1)} %pad_maximum_fusion.mine_ref, f32[4,96,128]{2,1,0:T(8,128)S(1)} %collective-permute-done.43.other_ref, f32[256,256]{1,0:T(8,128)S(1)} %copy-done.1), custom_call_target="tpu_custom_call" | custom-call | tf_op jit(solution)/shard_map/finish/pallas_call | solution.py:262
  (105 shorter events, 35.8 us)
Async XLA Ops:
  1.9 16.6 %collective-permute-start.21 = (bf16[768,256]{1,0:T(8,128)(2,1)S(1)}, bf16[768,256]{1,0:T(8,128)(2,1)S(1)}, u32[]{:S(2)}, u32[]{:S(2)}) collective-permute-start(bf16[768,256]{1,0:T(8,128)(2,1)S(1)} %convert_element_type.3.rest_0_.b_ref), channel_id=1, source_target_pairs={{0,8},{2,10},{4,12},{6,14},{8,0},{10,2},{12,4},{14,6},{16,24},{18,... | collective-permute-start | bytes 1179656 | tf_op jit(solution)/shard_map/ppermute | solution.py:307
  5.0 18.7 %collective-permute-start.18 = (bf16[768,256]{1,0:T(8,128)(2,1)S(1)}, bf16[768,256]{1,0:T(8,128)(2,1)S(1)}, u32[]{:S(2)}, u32[]{:S(2)}) collective-permute-start(bf16[768,256]{1,0:T(8,128)(2,1)S(1)} %convert_element_type.3.rest_0_.b_ref), channel_id=1, source_target_pairs={{0,4},{2,6},{4,0},{6,2},{8,12},{10,14},{12,8},{14,10},{16,20},{18,... | collective-permute-start | bytes 1179656 | tf_op jit(solution)/shard_map/ppermute | solution.py:307
  6.5 19.8 %collective-permute-start.29 = (bf16[768,256]{1,0:T(8,128)(2,1)S(1)}, bf16[768,256]{1,0:T(8,128)(2,1)S(1)}, u32[]{:S(2)}, u32[]{:S(2)}) collective-permute-start(bf16[768,256]{1,0:T(8,128)(2,1)S(1)} %convert_element_type.3.rest_0_.b_ref), channel_id=1, source_target_pairs={{0,2},{2,0},{4,6},{6,4},{8,10},{10,8},{12,14},{14,12},{16,18},{18,... | collective-permute-start | bytes 1179656 | tf_op jit(solution)/shard_map/ppermute | solution.py:307
  8.0 18.3 %collective-permute-start.32 = (bf16[768,256]{1,0:T(8,128)(2,1)S(1)}, bf16[768,256]{1,0:T(8,128)(2,1)}, u32[]{:S(2)}, u32[]{:S(2)}) collective-permute-start(bf16[768,256]{1,0:T(8,128)(2,1)S(1)} %convert_element_type.3.rest_0_.b_ref), channel_id=1, source_target_pairs={{0,1},{1,0},{2,3},{3,2},{4,5},{5,4},{6,7},{7,6},{8,9},{9,8},{10,11... | collective-permute-start | bytes 1179656 | tf_op jit(solution)/shard_map/ppermute | solution.py:310
  8.0 20.9 %collective-permute-start = (bf16[768,256]{1,0:T(8,128)(2,1)S(1)}, bf16[768,256]{1,0:T(8,128)(2,1)S(1)}, u32[]{:S(2)}, u32[]{:S(2)}) collective-permute-start(bf16[768,256]{1,0:T(8,128)(2,1)S(1)} %convert_element_type.3.rest_0_.b_ref), channel_id=1, source_target_pairs={{0,16},{2,18},{4,20},{6,22},{8,24},{10,26},{12,28},{14,30},{16,0},... | collective-permute-start | bytes 1179656 | tf_op jit(solution)/shard_map/ppermute | solution.py:307
  28.9 12.0 %collective-permute-start.19 = (bf16[768,256]{1,0:T(8,128)(2,1)S(1)}, bf16[768,256]{1,0:T(8,128)(2,1)S(1)}, u32[]{:S(2)}, u32[]{:S(2)}) collective-permute-start(bf16[768,256]{1,0:T(8,128)(2,1)S(1)} %collective-permute-done.18.rest_2_), channel_id=1, source_target_pairs={{0,2},{2,0},{4,6},{6,4},{8,10},{10,8},{12,14},{14,12},{16,18},{18,... | collective-permute-start | bytes 1179656 | tf_op jit(solution)/shard_map/ppermute | solution.py:307
  36.0 12.0 %collective-permute-start.5 = (bf16[768,256]{1,0:T(8,128)(2,1)S(1)}, bf16[768,256]{1,0:T(8,128)(2,1)S(1)}, u32[]{:S(2)}, u32[]{:S(2)}) collective-permute-start(bf16[768,256]{1,0:T(8,128)(2,1)S(1)} %collective-permute-done.rest_0_), channel_id=1, source_target_pairs={{0,2},{2,0},{4,6},{6,4},{8,10},{10,8},{12,14},{14,12},{16,18},{18,... | collective-permute-start | bytes 1179656 | tf_op jit(solution)/shard_map/ppermute | solution.py:307
  43.4 19.3 %collective-permute-start.25 = (bf16[768,256]{1,0:T(8,128)(2,1)S(1)}, bf16[768,256]{1,0:T(8,128)(2,1)S(1)}, u32[]{:S(2)}, u32[]{:S(2)}) collective-permute-start(bf16[768,256]{1,0:T(8,128)(2,1)S(1)} %collective-permute-done.22.rest_0_), channel_id=1, source_target_pairs={{0,1},{1,0},{2,3},{3,2},{4,5},{5,4},{6,7},{7,6},{8,9},{9,8},{10,11... | collective-permute-start | bytes 1179656 | tf_op jit(solution)/shard_map/ppermute | solution.py:310
  45.9 16.9 %collective-permute-start.27 = (bf16[768,256]{1,0:T(8,128)(2,1)S(1)}, bf16[768,256]{1,0:T(8,128)(2,1)S(1)}, u32[]{:S(2)}, u32[]{:S(2)}) collective-permute-start(bf16[768,256]{1,0:T(8,128)(2,1)S(1)} %collective-permute-done.26.rest_1_), channel_id=1, source_target_pairs={{0,1},{1,0},{2,3},{3,2},{4,5},{5,4},{6,7},{7,6},{8,9},{9,8},{10,11... | collective-permute-start | bytes 1179656 | tf_op jit(solution)/shard_map/ppermute | solution.py:310
  48.0 15.3 %collective-permute-start.20 = (bf16[768,256]{1,0:T(8,128)(2,1)S(1)}, bf16[768,256]{1,0:T(8,128)(2,1)S(1)}, u32[]{:S(2)}, u32[]{:S(2)}) collective-permute-start(bf16[768,256]{1,0:T(8,128)(2,1)S(1)} %collective-permute-done.19.rest_1_), channel_id=1, source_target_pairs={{0,1},{1,0},{2,3},{3,2},{4,5},{5,4},{6,7},{7,6},{8,9},{9,8},{10,11... | collective-permute-start | bytes 1179656 | tf_op jit(solution)/shard_map/ppermute | solution.py:310
  48.0 16.6 %collective-permute-start.2 = (bf16[768,256]{1,0:T(8,128)(2,1)S(1)}, bf16[768,256]{1,0:T(8,128)(2,1)S(1)}, u32[]{:S(2)}, u32[]{:S(2)}) collective-permute-start(bf16[768,256]{1,0:T(8,128)(2,1)S(1)} %collective-permute-done.1.rest_0_), channel_id=1, source_target_pairs={{0,4},{2,6},{4,0},{6,2},{8,12},{10,14},{12,8},{14,10},{16,20},{18,... | collective-permute-start | bytes 1179656 | tf_op jit(solution)/shard_map/ppermute | solution.py:307
  52.6 12.0 %collective-permute-start.6 = (bf16[768,256]{1,0:T(8,128)(2,1)S(1)}, bf16[768,256]{1,0:T(8,128)(2,1)S(1)}, u32[]{:S(2)}, u32[]{:S(2)}) collective-permute-start(bf16[768,256]{1,0:T(8,128)(2,1)S(1)} %collective-permute-done.5.rest_1_), channel_id=1, source_target_pairs={{0,8},{2,10},{4,12},{6,14},{8,0},{10,2},{12,4},{14,6},{16,24},{18,... | collective-permute-start | bytes 1179656 | tf_op jit(solution)/shard_map/ppermute | solution.py:307
  62.7 19.8 %collective-permute-start.14 = (bf16[768,256]{1,0:T(8,128)(2,1)S(1)}, bf16[768,256]{1,0:T(8,128)(2,1)S(1)}, u32[]{:S(2)}, u32[]{:S(2)}) collective-permute-start(bf16[768,256]{1,0:T(8,128)(2,1)S(1)} %collective-permute-done.1.rest_0_), channel_id=1, source_target_pairs={{0,1},{1,0},{2,3},{3,2},{4,5},{5,4},{6,7},{7,6},{8,9},{9,8},{10,11... | collective-permute-start | bytes 1179656 | tf_op jit(solution)/shard_map/ppermute | solution.py:310
  62.8 20.9 %collective-permute-start.15 = (bf16[768,256]{1,0:T(8,128)(2,1)S(1)}, bf16[768,256]{1,0:T(8,128)(2,1)S(1)}, u32[]{:S(2)}, u32[]{:S(2)}) collective-permute-start(bf16[768,256]{1,0:T(8,128)(2,1)S(1)} %collective-permute-done.5.rest_1_), channel_id=1, source_target_pairs={{0,1},{1,0},{2,3},{3,2},{4,5},{5,4},{6,7},{7,6},{8,9},{9,8},{10,11... | collective-permute-start | bytes 1179656 | tf_op jit(solution)/shard_map/ppermute | solution.py:310
  63.3 18.4 %collective-permute-start.12 = (bf16[768,256]{1,0:T(8,128)(2,1)S(1)}, bf16[768,256]{1,0:T(8,128)(2,1)S(1)}, u32[]{:S(2)}, u32[]{:S(2)}) collective-permute-start(bf16[768,256]{1,0:T(8,128)(2,1)S(1)} %collective-permute-done.11.rest_2_), channel_id=1, source_target_pairs={{0,2},{2,0},{4,6},{6,4},{8,10},{10,8},{12,14},{14,12},{16,18},{18,... | collective-permute-start | bytes 1179656 | tf_op jit(solution)/shard_map/ppermute | solution.py:307
  64.6 19.1 %collective-permute-start.16 = (bf16[768,256]{1,0:T(8,128)(2,1)S(1)}, bf16[768,256]{1,0:T(8,128)(2,1)S(1)}, u32[]{:S(2)}, u32[]{:S(2)}) collective-permute-start(bf16[768,256]{1,0:T(8,128)(2,1)S(1)} %collective-permute-done.11.rest_2_), channel_id=1, source_target_pairs={{0,1},{1,0},{2,3},{3,2},{4,5},{5,4},{6,7},{7,6},{8,9},{9,8},{10,11... | collective-permute-start | bytes 1179656 | tf_op jit(solution)/shard_map/ppermute | solution.py:310
  64.6 19.6 %collective-permute-start.24 = (bf16[768,256]{1,0:T(8,128)(2,1)S(1)}, bf16[768,256]{1,0:T(8,128)(2,1)S(1)}, u32[]{:S(2)}, u32[]{:S(2)}) collective-permute-start(bf16[768,256]{1,0:T(8,128)(2,1)S(1)} %collective-permute-done.23.rest_2_), channel_id=1, source_target_pairs={{0,1},{1,0},{2,3},{3,2},{4,5},{5,4},{6,7},{7,6},{8,9},{9,8},{10,11... | collective-permute-start | bytes 1179656 | tf_op jit(solution)/shard_map/ppermute | solution.py:310
  81.7 12.1 %collective-permute-start.3 = (bf16[384,256]{1,0:T(8,128)(2,1)S(1)}, bf16[384,256]{1,0:T(8,128)(2,1)S(1)}, u32[]{:S(2)}, u32[]{:S(2)}) collective-permute-start(bf16[384,256]{1,0:T(8,128)(2,1)S(1)} %slice.24), channel_id=1, source_target_pairs={{0,2},{2,0},{4,6},{6,4},{8,10},{10,8},{12,14},{14,12},{16,18},{18,... | collective-permute-start | bytes 589832 | tf_op jit(solution)/shard_map/ppermute | solution.py:307
  83.7 20.3 %collective-permute-start.10 = (bf16[768,256]{1,0:T(8,128)(2,1)S(1)}, bf16[768,256]{1,0:T(8,128)(2,1)S(1)}, u32[]{:S(2)}, u32[]{:S(2)}) collective-permute-start(bf16[768,256]{1,0:T(8,128)(2,1)S(1)} %collective-permute-done.6.rest_1_), channel_id=1, source_target_pairs={{0,1},{1,0},{2,3},{3,2},{4,5},{5,4},{6,7},{7,6},{8,9},{9,8},{10,11... | collective-permute-start | bytes 1179656 | tf_op jit(solution)/shard_map/ppermute | solution.py:310
  83.7 20.3 %collective-permute-start.9 = (bf16[768,256]{1,0:T(8,128)(2,1)S(1)}, bf16[768,256]{1,0:T(8,128)(2,1)S(1)}, u32[]{:S(2)}, u32[]{:S(2)}) collective-permute-start(bf16[768,256]{1,0:T(8,128)(2,1)S(1)} %collective-permute-done.2.rest_0_), channel_id=1, source_target_pairs={{0,1},{1,0},{2,3},{3,2},{4,5},{5,4},{6,7},{7,6},{8,9},{9,8},{10,11... | collective-permute-start | bytes 1179656 | tf_op jit(solution)/shard_map/ppermute | solution.py:310
  84.2 19.8 %collective-permute-start.13 = (bf16[768,256]{1,0:T(8,128)(2,1)S(1)}, bf16[768,256]{1,0:T(8,128)(2,1)S(1)}, u32[]{:S(2)}, u32[]{:S(2)}) collective-permute-start(bf16[768,256]{1,0:T(8,128)(2,1)S(1)} %collective-permute-done.12.rest_2_), channel_id=1, source_target_pairs={{0,1},{1,0},{2,3},{3,2},{4,5},{5,4},{6,7},{7,6},{8,9},{9,8},{10,11... | collective-permute-start | bytes 1179656 | tf_op jit(solution)/shard_map/ppermute | solution.py:310
  93.9 17.2 %collective-permute-start.4 = (bf16[384,256]{1,0:T(8,128)(2,1)S(1)}, bf16[384,256]{1,0:T(8,128)(2,1)S(1)}, u32[]{:S(2)}, u32[]{:S(2)}) collective-permute-start(bf16[384,256]{1,0:T(8,128)(2,1)S(1)} %collective-permute-done.3.rest_0_), channel_id=1, source_target_pairs={{0,1},{1,0},{2,3},{3,2},{4,5},{5,4},{6,7},{7,6},{8,9},{9,8},{10,11... | collective-permute-start | bytes 589832 | tf_op jit(solution)/shard_map/ppermute | solution.py:310
  94.4 16.7 %collective-permute-start.8 = (bf16[384,256]{1,0:T(8,128)(2,1)S(1)}, bf16[384,256]{1,0:T(8,128)(2,1)S(1)}, u32[]{:S(2)}, u32[]{:S(2)}) collective-permute-start(bf16[384,256]{1,0:T(8,128)(2,1)S(1)} %collective-permute-done.7.rest_1_), channel_id=1, source_target_pairs={{0,1},{1,0},{2,3},{3,2},{4,5},{5,4},{6,7},{7,6},{8,9},{9,8},{10,11... | collective-permute-start | bytes 589832 | tf_op jit(solution)/shard_map/ppermute | solution.py:310
  139.4 41.6 %collective-permute-start.43 = (f32[4,96,128]{2,1,0:T(8,128)S(1)}, f32[4,96,128]{2,1,0:T(8,128)S(1)}, u32[]{:S(2)}, u32[]{:S(2)}) collective-permute-start(f32[4,96,128]{2,1,0:T(8,128)S(1)} %pad_maximum_fusion.mine_ref), channel_id=1, source_target_pairs={{0,1},{1,0},{2,3},{3,2},{4,5},{5,4},{6,7},{7,6},{8,9},{9,8},{10,11... | collective-permute-start | bytes 589832 | tf_op jit(solution)/shard_map/ppermute | solution.py:310
  (28 other events, 390.1 us)
where the time goes:
time: 224 us
  Pallas kernels  139 us (62%)
  waiting for transfers between devices  42.5 us (19%)
  starting transfers between devices  39 us (17%)
    pallas_call x8, Pallas kernels, stage_call(): pl.pallas_call(body, name='stage_product', out_shape=(jax.ShapeDtypeStruc...  54.7 us
    pallas_call x1, Pallas kernels, finish_call(): pl.pallas_call(body, name='finish', out_shape=(jax.ShapeDtypeStruct((rows...  41.6 us
    pallas_call x1, Pallas kernels, inverse_call(): pl.pallas_call(body, name='inverse_factor', out_shape=jax.ShapeDtypeStruc...  41.5 us
    ppermute x25, waiting for transfers between devices, from_chip(): return lax.ppermute(a, 'rows', [(s, s ^ m) for s in range(chips)])  41.3 us
    ppermute x25, starting transfers between devices, from_chip(): return lax.ppermute(a, 'rows', [(s, s ^ m) for s in range(chips)])  35.7 us
  transfers between devices with their start and end apart: 44, of which 17 were waited for; matrix products, arithmetic and copies ran while one was open for 0% of the time, Pallas kernels for 42%

commit v1 on v0

v1 whole, which is shorter than its diff:
```python
import jax
import jax.numpy as jnp
from jax import lax
from jax.experimental import pallas as pl
from jax.experimental.pallas import tpu as pltpu
from jax.sharding import PartitionSpec as P


AXES = ("rows", "chip")
F32 = jnp.float32
BF16 = jnp.bfloat16
NN = (((1,), (0,)), ((), ()))
NT = (((1,), (1,)), ((), ()))


def shards_plain(hamiltonian, vectors):
    highest = lax.Precision.HIGHEST
    basis = vectors.astype(BF16)
    widened = basis.astype(F32)
    correlation_part = jnp.dot(basis.T, basis, preferred_element_type=F32)
    whole = lax.all_gather(basis, AXES, axis=0, tiled=True)
    product = jnp.dot(hamiltonian, whole.astype(F32), precision=highest)
    coupling_part = jnp.dot(widened.T, product, precision=highest)
    gram_part = jnp.dot(product.T, product, precision=highest)
    correlation, coupling, gram = lax.psum((correlation_part, coupling_part, gram_part), AXES)
    symmetric = 0.5 * (coupling + coupling.T)
    lower = jnp.linalg.cholesky(correlation)
    half = lax.linalg.triangular_solve(lower, symmetric, left_side=True, lower=True)
    projected = lax.linalg.triangular_solve(lower, half.T, left_side=True, lower=True)
    factor = jnp.linalg.cholesky(gram)
    rotated = lax.linalg.triangular_solve(factor, product.T, left_side=True, lower=True)
    return (rotated.T * jnp.sqrt(F32(hamiltonian.shape[1])), projected)


def split(a):
    high = a.astype(BF16)
    return high, (a - high.astype(F32)).astype(BF16)


def dot1(a, b, dims=NN):
    return lax.dot_general(a, b, dims, preferred_element_type=F32)


def dot3(a, b, dims=NN):
    ah, al = split(a)
    bh, bl = split(b)
    return dot1(ah, bh, dims) + (dot1(ah, bl, dims) + dot1(al, bh, dims))


def piece_at(quarter, core, slot):
    step = (0, 2 - core, 1 + core, 3)[slot]
    return 4 * core + (quarter ^ step)


def cut_pieces(p, b, quarter, core, buf, keep_ref, send_ref):
    half = p.shape[1] // 2
    piece = buf.shape[0] // 8
    pt_high, pt_low = split(p.T)
    bt = b.astype(F32).T.astype(BF16)
    p_high, p_low = split(p)
    cross = dot1(pt_high, p_low)
    gram = dot1(pt_high, p_high) + (cross + dot1(pt_low, p_high))
    coupling = dot1(bt, p_high) + dot1(bt, p_low)
    coupling = 0.5 * (coupling + coupling.T)
    correlation = dot1(bt, b)
    at = 0
    for a in (gram, coupling, correlation):
        for i, j in ((0, 0), (1, 0), (1, 1)):
            buf[at * half:(at + 1) * half, :] = a[i * half:(i + 1) * half, j * half:(j + 1) * half]
            at += 1
    for slot in range(4):
        at = pl.multiple_of(piece_at(quarter, core, slot) * piece, 8)
        keep_ref[slot] = buf[pl.ds(at, piece), :]
        at = pl.multiple_of(piece_at(quarter, 1 - core, slot) * piece, 8)
        send_ref[slot] = buf[pl.ds(at, piece), :]


def stage_call(hamiltonian, units, places, offset, acc, basis=None):
    n = len(units)
    rows, _ = hamiltonian.shape
    width = sum(a.shape[0] for a in units[0])
    nvec = units[0][0].shape[1]
    half = nvec // 2
    first = acc is None
    last = basis is not None
    nbuf = min(5, n)
    pieces = []
    for i, unit in enumerate(units):
        at = 0
        for a in unit:
            pieces.append((i, at, a))
            at += a.shape[0]
    count = len(pieces)
    tail = places.shape[0] - 2

    def body(places_ref, h_ref, *rest):
        piece_refs, rest = rest[:count], rest[count:]
        if not first:
            acc_ref, rest = rest[0], rest[1:]
        if last:
            b_ref, out_ref, keep_ref, send_ref, hbuf, ubuf, hsem, usem, buf = rest
        else:
            out_ref, hbuf, ubuf, hsem, usem = rest

        def hcopy(i, slot):
            at = pl.multiple_of(places_ref[offset + i] * width, 128)
            return pltpu.make_async_copy(h_ref.at[:, pl.ds(at, width)], hbuf.at[slot], hsem.at[slot])

        for i in range(nbuf):
            hcopy(i, i).start()
            for (k, at, a), ref in zip(pieces, piece_refs):
                if k == i or (k > i and i == nbuf - 1):
                    pltpu.make_async_copy(ref, ubuf.at[k, pl.ds(at, a.shape[0]), :], usem.at[k]).start()
        if first:
            out_ref[...] = jnp.zeros_like(out_ref)
        else:
            out_ref[...] = acc_ref[...]

        def step(i, _):
            slot = lax.rem(i, nbuf)
            pltpu.make_async_copy(ubuf.at[i], ubuf.at[i], usem.at[i]).wait()
            hcopy(i, slot).wait()
            high, low = split(hbuf[slot])
            u = ubuf[i]
            out_ref[...] += dot1(high, u) + dot1(low, u)

            @pl.when(i + nbuf < n)
            def _():
                hcopy(i + nbuf, slot).start()

            return 0

        lax.fori_loop(0, n, step, 0)
        if last:
            cut_pieces(out_ref[...], b_ref[...], places_ref[tail], places_ref[tail + 1], buf, keep_ref, send_ref)

    any_spec = pl.BlockSpec(memory_space=pl.ANY)
    vmem = pl.BlockSpec(memory_space=pltpu.VMEM)
    operands = [places, hamiltonian, *(a for _, _, a in pieces)]
    in_specs = [pl.BlockSpec(memory_space=pltpu.SMEM), any_spec] + [any_spec] * count
    aliases = {}
    if not first:
        aliases = {len(operands): 0}
        operands.append(acc)
        in_specs.append(vmem)
    out_shape = [jax.ShapeDtypeStruct((rows, nvec), F32)]
    scratch = [
        pltpu.VMEM((nbuf, rows, width), F32),
        pltpu.VMEM((n, width, nvec), BF16),
        pltpu.SemaphoreType.DMA((nbuf,)),
        pltpu.SemaphoreType.DMA((n,)),
    ]
    if last:
        operands.append(basis)
        in_specs.append(vmem)
        out_shape += [jax.ShapeDtypeStruct((4, 9 * half // 8, half), F32)] * 2
        scratch.append(pltpu.VMEM((9 * half, half), F32))
    return pl.pallas_call(
        body,
        name="stage_product",
        out_shape=tuple(out_shape),
        in_specs=in_specs,
        out_specs=(vmem,) * len(out_shape),
        scratch_shapes=scratch,
        input_output_aliases=aliases,
        cost_estimate=pl.CostEstimate(
            flops=4 * n * rows * width * nvec, transcendentals=0, bytes_accessed=4 * n * rows * width
        ),
        compiler_params=pltpu.CompilerParams(vmem_limit_bytes=48 << 20),
    )(*operands)


def refine(a):
    n = a.shape[0]
    i = lax.broadcasted_iota(jnp.int32, (n, n), 0)
    j = lax.broadcasted_iota(jnp.int32, (n, n), 1)
    eye = jnp.where(i == j, 1.0, 0.0).astype(F32)
    weight = jnp.where(i > j, 1.0, jnp.where(i == j, 0.5, 0.0)).astype(F32)
    diagonal = jnp.where(i == j, a, 0.0)
    scale_row = lax.rsqrt(jnp.sum(diagonal, axis=0, keepdims=True))
    scale_col = lax.rsqrt(jnp.sum(diagonal, axis=1, keepdims=True))
    k = a * scale_row * scale_col
    e = k - eye
    x = (e * weight).astype(BF16)
    x = (e - dot1(x, x, NT)) * weight
    xh = x.astype(BF16)
    m = eye - x + dot1(xh, xh) * jnp.where(i >= j, 1.0, 0.0)

    def residual(m):
        return dot3(dot3(m, k), m, NT) - eye

    m = m - dot3(residual(m) * weight, m)
    e = residual(m)
    norm = jnp.max(jnp.sum(jnp.abs(e), axis=1))
    m = m - dot3(e * weight, m)
    return m * scale_row, norm


def eliminate(a, out_ref, work_a, work_w):
    n = a.shape[0]
    i = lax.broadcasted_iota(jnp.int32, (n, n), 0)
    j = lax.broadcasted_iota(jnp.int32, (n, n), 1)
    work_a[...] = a
    work_w[...] = jnp.where(i == j, 1.0, 0.0).astype(F32)
    lane = lax.broadcasted_iota(jnp.int32, (1, n), 1)
    row = lax.broadcasted_iota(jnp.int32, (n, 1), 0)

    def column(s, _):
        top = work_a[pl.ds(s, 1), :]
        top_w = work_w[pl.ds(s, 1), :]
        inverse = 1.0 / jnp.sum(jnp.where(lane == s, top, 0.0), axis=1, keepdims=True)
        at = work_a[...]
        col = jnp.sum(jnp.where(lane == s, at, 0.0), axis=1, keepdims=True)
        col = jnp.where(row > s, col * inverse, 0.0)
        work_a[...] = at - col * top
        work_w[...] = work_w[...] - col * top_w
        return 0

    lax.fori_loop(0, n, column, 0)
    pivots = jnp.sum(jnp.where(i == j, work_a[...], 0.0), axis=1, keepdims=True)
    out_ref[...] = work_w[...] * lax.rsqrt(pivots)


def finish_call(product, mine, other, places, scale):
    rows, nvec = product.shape
    half = nvec // 2
    _, piece, _ = mine.shape
    tail = places.shape[0] - 2

    def body(places_ref, p_ref, mine_ref, other_ref, ritz_ref, projected_ref, pbuf, buf, whole, inv, work_a, work_w, sem):
        copy = pltpu.make_async_copy(p_ref, pbuf, sem)
        copy.start()
        quarter = places_ref[tail]
        core = places_ref[tail + 1]
        for slot in range(4):
            buf[pl.ds(pl.multiple_of(piece_at(quarter, core, slot) * piece, 8), piece), :] = mine_ref[slot]
            buf[pl.ds(pl.multiple_of(piece_at(quarter, 1 - core, slot) * piece, 8), piece), :] = other_ref[slot]
        for q in range(3):
            at = 3 * q * half
            corner = buf[at + half:at + 2 * half, :]
            whole[q, :half, :half] = buf[at:at + half, :]
            whole[q, half:, :half] = corner
            whole[q, :half, half:] = corner.T
            whole[q, half:, half:] = buf[at + 2 * half:at + 3 * half, :]
        inv[0], gram_norm = refine(whole[0])
        inv[1], correlation_norm = refine(whole[2])
        for at, source, norm in ((0, 0, gram_norm), (1, 2, correlation_norm)):
            @pl.when(jnp.logical_not(norm < 3e-3))
            def _():
                eliminate(whole[source], inv.at[at], work_a, work_w)
        copy.wait()
        ritz_ref[...] = dot3(pbuf[...], inv[0] * scale, NT)
        low = inv[1]
        projected_ref[...] = dot3(dot3(low, whole[1]), low, NT)

    vmem = pl.BlockSpec(memory_space=pltpu.VMEM)
    square = pltpu.VMEM((nvec, nvec), F32)
    return pl.pallas_call(
        body,
        name="finish",
        out_shape=(jax.ShapeDtypeStruct((rows, nvec), F32), jax.ShapeDtypeStruct((nvec, nvec), F32)),
        in_specs=[pl.BlockSpec(memory_space=pltpu.SMEM), pl.BlockSpec(memory_space=pl.ANY), vmem, vmem],
        out_specs=(vmem, vmem),
        scratch_shapes=[
            pltpu.VMEM((rows, nvec), F32),
            pltpu.VMEM((9 * half, half), F32),
            pltpu.VMEM((3, nvec, nvec), F32),
            pltpu.VMEM((2, nvec, nvec), F32),
            square,
            square,
            pltpu.SemaphoreType.DMA,
        ],
        compiler_params=pltpu.CompilerParams(vmem_limit_bytes=48 << 20),
    )(places, product, mine, other)


WHOLE = (0, 8)
STAGES = (
    ((4, ((0, 4, WHOLE),)), (1, ((0, 1, WHOLE),)), (2, ((0, 2, WHOLE),))),
    ((5, ((4, 1, WHOLE),)), (6, ((4, 2, WHOLE),)), (8, ((0, 8, WHOLE),)), (3, ((2, 1, WHOLE),))),
    ((7, ((5, 2, WHOLE),)),),
    ((12, ((8, 4, WHOLE),)), (9, ((8, 1, WHOLE),)), (10, ((8, 2, WHOLE),))),
    ((14, ((12, 2, WHOLE),)), (13, ((9, 4, WHOLE),)), (11, ((10, 1, WHOLE),))),
    ((15, ((14, 1, (0, 4)), (13, 2, (4, 8)))),),
)
TURNS = (
    ((0,), ()),
    ((4, 1, 2), (0,)),
    ((5, 6), (4, 1, 2)),
    ((8, 3, 7), (5, 6)),
    ((12, 9, 10), (8, 3, 7)),
    ((14, 13, 11), (12, 9, 10)),
    ((15,), (14, 13, 11)),
    ((), (15,)),
)


def shards_pairs(hamiltonian, vectors):
    chips = lax.axis_size("rows")
    here = lax.axis_index("rows")
    core = lax.axis_index("chip")
    width = vectors.shape[0]

    def from_chip(a, m):
        return lax.ppermute(a, "rows", [(s, s ^ m) for s in range(chips)])

    def from_core(a):
        return lax.ppermute(a, "chip", [(0, 1), (1, 0)])

    def spread(a, steps):
        return lax.ppermute(a, AXES, [(2 * s + c, 2 * (s ^ steps[c]) + c) for s in range(chips) for c in range(2)])

    basis = vectors.astype(BF16)
    order = [2 * m + far for turn in TURNS for far in range(2) for m in turn[far]]
    places = jnp.concatenate(
        [(2 * here + core) ^ jnp.array(order, jnp.int32), jnp.stack([here % 4, core]).astype(jnp.int32)]
    )
    mine = {0: (basis,)}
    acc = None
    other = {}
    offset = 0
    for t, (near, far) in enumerate(TURNS):
        if 0 < t <= len(STAGES):
            for m, parts in STAGES[t - 1]:
                got = []
                for source, step, (lo, hi) in parts:
                    a = mine[source][0]
                    if (lo, hi) != WHOLE:
                        a = a[lo * width // 8:hi * width // 8]
                    got.append(from_chip(a, step))
                mine[m] = tuple(got)
        for m in near:
            other[m] = tuple(from_core(a) for a in mine[m])
        units = [mine[m] for m in near] + [other[m] for m in far]
        end = basis if t == len(TURNS) - 1 else None
        acc, *pieces = stage_call(hamiltonian, units, places, offset, acc, end)
        offset += len(units)
    keep, send = pieces
    a = keep + from_core(send)
    a = a[:2] + spread(a[2:], (1, 2))
    a = a[:1] + spread(a[1:], (2, 1))
    a = a + spread(a, (4, 8))
    a = a + spread(a, (8, 4))
    a = jnp.concatenate([a, spread(a, (2, 1))])
    a = jnp.concatenate([a, spread(a, (1, 2))])
    b = from_core(a)
    return finish_call(acc, a, b, places, float(hamiltonian.shape[1]) ** 0.5)


def solution(mesh):
    in_specs = (P(AXES, None), P(AXES, None))
    out_specs = (P(AXES, None), P())
    pairs = mesh.shape["rows"] == 16 and mesh.shape["chip"] == 2
    body = shards_pairs if pairs else shards_plain
    return jax.shard_map(body, mesh=mesh, in_specs=in_specs, out_specs=out_specs, check_vma=False)
```

time: 224 us -> 220 us (0.982)
  Pallas kernels: 139 us -> 127 us
  waiting for transfers between devices: 42.5 us -> 49.2 us
  starting transfers between devices: 39 us -> 34.6 us
  local copies, waits for them, and re-layouts: 1.04 us -> 5.34 us
    pallas_call x10 -> x8, Pallas kernels: 97.1 us -> 45.3 us  [stage_call(): pl.pallas_call(body, name='stage_product', out_shape=tuple(out_shape), in...]
    pallas_call x1, Pallas kernels: 41.6 us -> 81.8 us  [finish_call(): pl.pallas_call(body, name='finish', out_shape=(jax.ShapeDtypeStruct((rows...]
    ppermute x0 -> x6, waiting for transfers between devices: none -> 23.4 us  [spread(): lax.ppermute(a, AXES, [(2 * s + c, 2 * (s ^ steps[c]) + c) for s in range...]
    ppermute x25 -> x16, waiting for transfers between devices: 41.3 us -> 22.9 us  [from_chip(): return lax.ppermute(a, 'rows', [(s, s ^ m) for s in range(chips)])]
    ppermute x25 -> x16, starting transfers between devices: 35.7 us -> 24.2 us  [from_chip(): return lax.ppermute(a, 'rows', [(s, s ^ m) for s in range(chips)])]
    ppermute x0 -> x6, starting transfers between devices: none -> 6.6 us  [spread(): lax.ppermute(a, AXES, [(2 * s + c, 2 * (s ^ steps[c]) + c) for s in range...]
    unnamed x16 -> x28, local copies, waits for them, and re-layouts: 1 us -> 5.3 us
  transfers between devices with their start and end apart: 44 -> 41, of which waited for: 17 -> 13; matrix products, arithmetic and copies ran while one was open for 0% -> 0% of each run, Pallas kernels for 42% -> 18%
where the time goes in v1:
time: 220 us; the launch traced here: 219 us
  Pallas kernels  127 us (58%)
  waiting for transfers between devices  49.2 us (22%)
  starting transfers between devices  34.6 us (16%)
  local copies, waits for them, and re-layouts  5.34 us (2%)
    pallas_call x1, Pallas kernels, finish_call(): pl.pallas_call(body, name='finish', out_shape=(jax.ShapeDtypeStruct((rows...  81.8 us
    pallas_call x8, Pallas kernels, stage_call(): pl.pallas_call(body, name='stage_product', out_shape=tuple(out_shape), in...  45.3 us
    ppermute x16, starting transfers between devices, from_chip(): return lax.ppermute(a, 'rows', [(s, s ^ m) for s in range(chips)])  24.2 us
    ppermute x6, waiting for transfers between devices, spread(): lax.ppermute(a, AXES, [(2 * s + c, 2 * (s ^ steps[c]) + c) for s in range...  23.4 us
    ppermute x16, waiting for transfers between devices, from_chip(): return lax.ppermute(a, 'rows', [(s, s ^ m) for s in range(chips)])  22.9 us
    ppermute x6, starting transfers between devices, spread(): lax.ppermute(a, AXES, [(2 * s + c, 2 * (s ^ steps[c]) + c) for s in range...  6.6 us
    unnamed x28, local copies, waits for them, and re-layouts  5.3 us
  transfers between devices with their start and end apart: 41, of which 13 were waited for; matrix products, arithmetic and copies ran while one was open for 0% of the time, Pallas kernels for 18%

profile of v1, /device:TPU:0, one launch (start us, length us, event | category | flops | bytes accessed | tf_op | source)
XLA Modules:
  0.0 219.5 jit_solution(10357011580667239214)
XLA Ops:
  1.8 3.1 %collective-permute-start.21 = (bf16[768,256]{1,0:T(8,128)(2,1)S(1)}, bf16[768,256]{1,0:T(8,128)(2,1)S(1)}, u32[]{:S(2)}, u32[]{:S(2)}) collective-permute-start(bf16[768,256]{1,0:T(8,128)(2,1)S(1)} %convert_element_type.3.rest_0_.rest_3_), channel_id=1, source_target_pairs={{0,8},{2,10},{4,12},{6,14},{8,0},{10,2},{12,4},{14,6},{16,24},{18,... | collective-permute-start | bytes 1179656 | tf_op jit(solution)/shard_map/ppermute | solution.py:305
  7.9 2.6 %collective-permute-start = (bf16[768,256]{1,0:T(8,128)(2,1)S(1)}, bf16[768,256]{1,0:T(8,128)(2,1)S(1)}, u32[]{:S(2)}, u32[]{:S(2)}) collective-permute-start(bf16[768,256]{1,0:T(8,128)(2,1)S(1)} %convert_element_type.3.rest_0_.rest_3_), channel_id=1, source_target_pairs={{0,16},{2,18},{4,20},{6,22},{8,24},{10,26},{12,28},{14,30},{16,0},... | collective-permute-start | bytes 1179656 | tf_op jit(solution)/shard_map/ppermute | solution.py:305
  10.5 7.9 %collective-permute-done.21.rest_0_ = bf16[768,256]{1,0:T(8,128)(2,1)S(1)} collective-permute-done((bf16[768,256]{1,0:T(8,128)(2,1)S(1)}, bf16[768,256]{1,0:T(8,128)(2,1)S(1)}, u32[]{:S(2)}, u32[]{:S(2)}) %collective-permute-start.21) | collective-permute-done | bytes 393248 | tf_op jit(solution)/shard_map/ppermute | solution.py:305
  18.4 2.6 %collective-permute-start.22 = (bf16[768,256]{1,0:T(8,128)(2,1)S(1)}, bf16[768,256]{1,0:T(8,128)(2,1)S(1)}, u32[]{:S(2)}, u32[]{:S(2)}) collective-permute-start(bf16[768,256]{1,0:T(8,128)(2,1)S(1)} %collective-permute-done.21.rest_0_), channel_id=1, source_target_pairs={{0,2},{2,0},{4,6},{6,4},{8,10},{10,8},{12,14},{14,12},{16,18},{18,... | collective-permute-start | bytes 1179656 | tf_op jit(solution)/shard_map/ppermute | solution.py:305
  25.6 3.3 %collective-permute-done.rest_0_ = bf16[768,256]{1,0:T(8,128)(2,1)S(1)} collective-permute-done((bf16[768,256]{1,0:T(8,128)(2,1)S(1)}, bf16[768,256]{1,0:T(8,128)(2,1)S(1)}, u32[]{:S(2)}, u32[]{:S(2)}) %collective-permute-start) | collective-permute-done | bytes 393248 | tf_op jit(solution)/shard_map/ppermute | solution.py:305
  31.8 2.6 %collective-permute-start.11 = (bf16[768,256]{1,0:T(8,128)(2,1)S(1)}, bf16[768,256]{1,0:T(8,128)(2,1)S(1)}, u32[]{:S(2)}, u32[]{:S(2)}) collective-permute-start(bf16[768,256]{1,0:T(8,128)(2,1)S(1)} %collective-permute-done.rest_0_), channel_id=1, source_target_pairs={{0,4},{2,6},{4,0},{6,2},{8,12},{10,14},{12,8},{14,10},{16,20},{18,... | collective-permute-start | bytes 1179656 | tf_op jit(solution)/shard_map/ppermute | solution.py:305
  36.2 5.4 %collective-permute-done.19.rest_1_ = bf16[768,256]{1,0:T(8,128)(2,1)S(1)} collective-permute-done((bf16[768,256]{1,0:T(8,128)(2,1)S(1)}, bf16[768,256]{1,0:T(8,128)(2,1)S(1)}, u32[]{:S(2)}, u32[]{:S(2)}) %collective-permute-start.19) | collective-permute-done | bytes 393248 | tf_op jit(solution)/shard_map/ppermute | solution.py:305
  45.8 3.7 %collective-permute-done.5.rest_1_ = bf16[768,256]{1,0:T(8,128)(2,1)S(1)} collective-permute-done((bf16[768,256]{1,0:T(8,128)(2,1)S(1)}, bf16[768,256]{1,0:T(8,128)(2,1)S(1)}, u32[]{:S(2)}, u32[]{:S(2)}) %collective-permute-start.5) | collective-permute-done | bytes 393248 | tf_op jit(solution)/shard_map/ppermute | solution.py:305
  50.1 2.6 %collective-permute-done.23.rest_2_ = bf16[768,256]{1,0:T(8,128)(2,1)} collective-permute-done((bf16[768,256]{1,0:T(8,128)(2,1)S(1)}, bf16[768,256]{1,0:T(8,128)(2,1)}, u32[]{:S(2)}, u32[]{:S(2)}) %collective-permute-start.23) | collective-permute-done | bytes 393248 | tf_op jit(solution)/shard_map/ppermute | solution.py:305
  52.7 3.0 %stage_product.8.rest_4_ = f32[768,256]{1,0:T(8,128)S(1)} custom-call(s32[34]{0:T(128)S(1)} %pad_add_fusion.places_ref, f32[768,24576]{1,0:T(8,128)} %h_ref.15, bf16[768,256]{1,0:T(8,128)(2,1)S(1)} %convert_element_type.3.rest_0_.rest_3_), custom_call_target="tpu_custom_call" | custom-call | flops 603979776 | bytes 2359296 | tf_op jit(solution)/shard_map/stage_product/pallas_call | solution.py:158
  55.8 5.4 %stage_product.9.rest_5_ = f32[768,256]{1,0:T(8,128)S(1)} custom-call(s32[34]{0:T(128)S(1)} %pad_add_fusion.places_ref, f32[768,24576]{1,0:T(8,128)} %h_ref.15, bf16[768,256]{1,0:T(8,128)(2,1)S(1)} %copy-done.1, bf16[768,256]{1,0:T(8,128)(2,1)S(1)} %copy-done.7, bf16[768,256]{1,0:T(8,128)(2,1)S(1)} %copy-done.5, ...), custom_call_target="tpu_custom_call", output_to_operand_aliasing={{}: (6, {})} | custom-call | flops 2415919104 | bytes 9437184 | tf_op jit(solution)/shard_map/stage_product/pallas_call | solution.py:158
  64.5 6.2 %stage_product.10.rest_5_ = f32[768,256]{1,0:T(8,128)S(1)} custom-call(s32[34]{0:T(128)S(1)} %pad_add_fusion.places_ref, f32[768,24576]{1,0:T(8,128)} %h_ref.15, bf16[768,256]{1,0:T(8,128)(2,1)S(1)} %collective-permute-done.22.rest_0_, bf16[768,256]{1,0:T(8,128)(2,1)S(1)} %collective-permute-done.26.rest_1_, ...), custom_call_target="tpu_custom_call", output_to_operand_aliasing={{}: (7, {})} | custom-call | flops 3019898880 | bytes 11796480 | tf_op jit(solution)/shard_map/stage_product/pallas_call | solution.py:158
  70.8 6.3 %stage_product.11.rest_6_ = f32[768,256]{1,0:T(8,128)S(1)} custom-call(s32[34]{0:T(128)S(1)} %pad_add_fusion.places_ref, f32[768,24576]{1,0:T(8,128)} %h_ref.15, bf16[768,256]{1,0:T(8,128)(2,1)S(1)} %collective-permute-done.rest_0_, bf16[768,256]{1,0:T(8,128)(2,1)S(1)} %copy-done.11, ...), custom_call_target="tpu_custom_call", output_to_operand_aliasing={{}: (7, {})} | custom-call | flops 3019898880 | bytes 11796480 | tf_op jit(solution)/shard_map/stage_product/pallas_call | solution.py:158
  78.9 7.0 %stage_product.12.rest_6_ = f32[768,256]{1,0:T(8,128)S(1)} custom-call(s32[34]{0:T(128)S(1)} %pad_add_fusion.places_ref, f32[768,24576]{1,0:T(8,128)} %h_ref.15, bf16[768,256]{1,0:T(8,128)(2,1)S(1)} %collective-permute-done.1.rest_0_, bf16[768,256]{1,0:T(8,128)(2,1)S(1)} %collective-permute-done.5.rest_1_, ...), custom_call_target="tpu_custom_call", output_to_operand_aliasing={{}: (8, {})} | custom-call | flops 3623878656 | bytes 14155776 | tf_op jit(solution)/shard_map/stage_product/pallas_call | solution.py:158
  86.5 7.0 %stage_product.13.rest_5_ = f32[768,256]{1,0:T(8,128)S(1)} custom-call(s32[34]{0:T(128)S(1)} %pad_add_fusion.places_ref, f32[768,24576]{1,0:T(8,128)} %h_ref.15, bf16[768,256]{1,0:T(8,128)(2,1)S(1)} %collective-permute-done.2.rest_0_, bf16[768,256]{1,0:T(8,128)(2,1)S(1)} %collective-permute-done.6.rest_1_, ...), custom_call_target="tpu_custom_call", output_to_operand_aliasing={{}: (8, {})} | custom-call | flops 3623878656 | bytes 14155776 | tf_op jit(solution)/shard_map/stage_product/pallas_call | solution.py:158
  93.6 5.5 %stage_product.14.rest_2_ = f32[768,256]{1,0:T(8,128)S(1)} custom-call(s32[34]{0:T(128)S(1)} %pad_add_fusion.places_ref, f32[768,24576]{1,0:T(8,128)} %h_ref.15, bf16[384,256]{1,0:T(8,128)(2,1)S(1)} %collective-permute-done.3.rest_0_, bf16[384,256]{1,0:T(8,128)(2,1)S(1)} %collective-permute-done.7.rest_1_, ...), custom_call_target="tpu_custom_call", output_to_operand_aliasing={{}: (7, {})} | custom-call | flops 2415919104 | bytes 9437184 | tf_op jit(solution)/shard_map/stage_product/pallas_call | solution.py:158
  99.1 4.9 %stage_product.15 = (f32[768,256]{1,0:T(8,128)S(1)}, f32[4,144,128]{2,1,0:T(8,128)S(1)}, f32[4,144,128]{2,1,0:T(8,128)S(1)}) custom-call(s32[34]{0:T(128)S(1)} %pad_add_fusion.places_ref, f32[768,24576]{1,0:T(8,128)} %h_ref.15, bf16[384,256]{1,0:T(8,128)(2,1)S(1)} %collective-permute-done.4.rest_0_, ...), custom_call_target="tpu_custom_call", output_to_operand_aliasing={{0}: (4, {})} | custom-call | flops 603979776 | bytes 2359296 | tf_op jit(solution)/shard_map/stage_product/pallas_call | solution.py:158
  106.9 4.1 %collective-permute-done.34 = f32[2,144,128]{2,1,0:T(8,128)S(1)} collective-permute-done((f32[2,144,128]{2,1,0:T(8,128)S(1)}, f32[2,144,128]{2,1,0:T(8,128)S(1)}, u32[]{:S(2)}, u32[]{:S(2)}) %collective-permute-start.34) | collective-permute-done | bytes 147488 | tf_op jit(solution)/shard_map/ppermute | solution.py:311
  112.1 3.3 %collective-permute-done.35 = f32[1,144,128]{2,1,0:T(8,128)S(1)} collective-permute-done((f32[1,144,128]{2,1,0:T(8,128)S(1)}, f32[1,144,128]{2,1,0:T(8,128)S(1)}, u32[]{:S(2)}, u32[]{:S(2)}) %collective-permute-start.35) | collective-permute-done | bytes 73760 | tf_op jit(solution)/shard_map/ppermute | solution.py:311
  116.5 3.3 %collective-permute-done.36 = f32[1,144,128]{2,1,0:T(8,128)S(1)} collective-permute-done((f32[1,144,128]{2,1,0:T(8,128)S(1)}, f32[1,144,128]{2,1,0:T(8,128)S(1)}, u32[]{:S(2)}, u32[]{:S(2)}) %collective-permute-start.36) | collective-permute-done | bytes 73760 | tf_op jit(solution)/shard_map/ppermute | solution.py:311
  122.0 4.0 %collective-permute-done.37 = f32[1,144,128]{2,1,0:T(8,128)S(1)} collective-permute-done((f32[1,144,128]{2,1,0:T(8,128)S(1)}, f32[1,144,128]{2,1,0:T(8,128)S(1)}, u32[]{:S(2)}, u32[]{:S(2)}) %collective-permute-start.37) | collective-permute-done | bytes 73760 | tf_op jit(solution)/shard_map/ppermute | solution.py:311
  126.3 4.4 %collective-permute-done.38 = f32[1,144,128]{2,1,0:T(8,128)S(1)} collective-permute-done((f32[1,144,128]{2,1,0:T(8,128)S(1)}, f32[1,144,128]{2,1,0:T(8,128)S(1)}, u32[]{:S(2)}, u32[]{:S(2)}) %collective-permute-start.38) | collective-permute-done | bytes 73760 | tf_op jit(solution)/shard_map/ppermute | solution.py:311
  131.5 4.4 %collective-permute-done.39 = f32[2,144,128]{2,1,0:T(8,128)S(1)} collective-permute-done((f32[2,144,128]{2,1,0:T(8,128)S(1)}, f32[2,144,128]{2,1,0:T(8,128)S(1)}, u32[]{:S(2)}, u32[]{:S(2)}) %collective-permute-start.39) | collective-permute-done | bytes 147488 | tf_op jit(solution)/shard_map/ppermute | solution.py:311
  137.6 81.8 %finish.1 = (f32[768,256]{1,0:T(8,128)}, f32[256,256]{1,0:T(8,128)}) custom-call(s32[34]{0:T(128)S(1)} %pad_add_fusion.places_ref, f32[768,256]{1,0:T(8,128)S(1)} %get-tuple-element.5.p_ref, f32[4,144,128]{2,1,0:T(8,128)S(1)} %pad_maximum_fusion.mine_ref, f32[4,144,128]{2,1,0:T(8,128)S(1)} %collective-permute-done.40.other_ref), custom_call_target="tpu_custom_call" | custom-call | tf_op jit(solution)/shard_map/finish/pallas_call | solution.py:258
  (109 shorter events, 34.0 us)
Async XLA Ops:
  1.8 16.6 %collective-permute-start.21 = (bf16[768,256]{1,0:T(8,128)(2,1)S(1)}, bf16[768,256]{1,0:T(8,128)(2,1)S(1)}, u32[]{:S(2)}, u32[]{:S(2)}) collective-permute-start(bf16[768,256]{1,0:T(8,128)(2,1)S(1)} %convert_element_type.3.rest_0_.rest_3_), channel_id=1, source_target_pairs={{0,8},{2,10},{4,12},{6,14},{8,0},{10,2},{12,4},{14,6},{16,24},{18,... | collective-permute-start | bytes 1179656 | tf_op jit(solution)/shard_map/ppermute | solution.py:305
  4.9 16.1 %collective-permute-start.18 = (bf16[768,256]{1,0:T(8,128)(2,1)S(1)}, bf16[768,256]{1,0:T(8,128)(2,1)S(1)}, u32[]{:S(2)}, u32[]{:S(2)}) collective-permute-start(bf16[768,256]{1,0:T(8,128)(2,1)S(1)} %convert_element_type.3.rest_0_.rest_3_), channel_id=1, source_target_pairs={{0,4},{2,6},{4,0},{6,2},{8,12},{10,14},{12,8},{14,10},{16,20},{18,... | collective-permute-start | bytes 1179656 | tf_op jit(solution)/shard_map/ppermute | solution.py:305
  6.4 17.1 %collective-permute-start.29 = (bf16[768,256]{1,0:T(8,128)(2,1)S(1)}, bf16[768,256]{1,0:T(8,128)(2,1)S(1)}, u32[]{:S(2)}, u32[]{:S(2)}) collective-permute-start(bf16[768,256]{1,0:T(8,128)(2,1)S(1)} %convert_element_type.3.rest_0_.rest_3_), channel_id=1, source_target_pairs={{0,2},{2,0},{4,6},{6,4},{8,10},{10,8},{12,14},{14,12},{16,18},{18,... | collective-permute-start | bytes 1179656 | tf_op jit(solution)/shard_map/ppermute | solution.py:305
  7.9 16.4 %collective-permute-start.32 = (bf16[768,256]{1,0:T(8,128)(2,1)S(1)}, bf16[768,256]{1,0:T(8,128)(2,1)S(1)}, u32[]{:S(2)}, u32[]{:S(2)}) collective-permute-start(bf16[768,256]{1,0:T(8,128)(2,1)S(1)} %convert_element_type.3.rest_0_.rest_3_), channel_id=1, source_target_pairs={{0,1},{1,0},{2,3},{3,2},{4,5},{5,4},{6,7},{7,6},{8,9},{9,8},{10,11... | collective-permute-start | bytes 1179656 | tf_op jit(solution)/shard_map/ppermute | solution.py:308
  7.9 20.9 %collective-permute-start = (bf16[768,256]{1,0:T(8,128)(2,1)S(1)}, bf16[768,256]{1,0:T(8,128)(2,1)S(1)}, u32[]{:S(2)}, u32[]{:S(2)}) collective-permute-start(bf16[768,256]{1,0:T(8,128)(2,1)S(1)} %convert_element_type.3.rest_0_.rest_3_), channel_id=1, source_target_pairs={{0,16},{2,18},{4,20},{6,22},{8,24},{10,26},{12,28},{14,30},{16,0},... | collective-permute-start | bytes 1179656 | tf_op jit(solution)/shard_map/ppermute | solution.py:305
  29.6 12.0 %collective-permute-start.19 = (bf16[768,256]{1,0:T(8,128)(2,1)S(1)}, bf16[768,256]{1,0:T(8,128)(2,1)S(1)}, u32[]{:S(2)}, u32[]{:S(2)}) collective-permute-start(bf16[768,256]{1,0:T(8,128)(2,1)S(1)} %collective-permute-done.18.rest_2_), channel_id=1, source_target_pairs={{0,2},{2,0},{4,6},{6,4},{8,10},{10,8},{12,14},{14,12},{16,18},{18,... | collective-permute-start | bytes 1179656 | tf_op jit(solution)/shard_map/ppermute | solution.py:305
  31.7 13.6 %collective-permute-start.1 = (bf16[768,256]{1,0:T(8,128)(2,1)S(1)}, bf16[768,256]{1,0:T(8,128)(2,1)S(1)}, u32[]{:S(2)}, u32[]{:S(2)}) collective-permute-start(bf16[768,256]{1,0:T(8,128)(2,1)S(1)} %collective-permute-done.rest_0_), channel_id=1, source_target_pairs={{0,8},{2,10},{4,12},{6,14},{8,0},{10,2},{12,4},{14,6},{16,24},{18,... | collective-permute-start | bytes 1179656 | tf_op jit(solution)/shard_map/ppermute | solution.py:305
  31.8 13.6 %collective-permute-start.11 = (bf16[768,256]{1,0:T(8,128)(2,1)S(1)}, bf16[768,256]{1,0:T(8,128)(2,1)S(1)}, u32[]{:S(2)}, u32[]{:S(2)}) collective-permute-start(bf16[768,256]{1,0:T(8,128)(2,1)S(1)} %collective-permute-done.rest_0_), channel_id=1, source_target_pairs={{0,4},{2,6},{4,0},{6,2},{8,12},{10,14},{12,8},{14,10},{16,20},{18,... | collective-permute-start | bytes 1179656 | tf_op jit(solution)/shard_map/ppermute | solution.py:305
  35.1 14.4 %collective-permute-start.5 = (bf16[768,256]{1,0:T(8,128)(2,1)S(1)}, bf16[768,256]{1,0:T(8,128)(2,1)S(1)}, u32[]{:S(2)}, u32[]{:S(2)}) collective-permute-start(bf16[768,256]{1,0:T(8,128)(2,1)S(1)} %collective-permute-done.rest_0_), channel_id=1, source_target_pairs={{0,2},{2,0},{4,6},{6,4},{8,10},{10,8},{12,14},{14,12},{16,18},{18,... | collective-permute-start | bytes 1179656 | tf_op jit(solution)/shard_map/ppermute | solution.py:305
  36.2 13.4 %collective-permute-start.17 = (bf16[768,256]{1,0:T(8,128)(2,1)S(1)}, bf16[768,256]{1,0:T(8,128)(2,1)S(1)}, u32[]{:S(2)}, u32[]{:S(2)}) collective-permute-start(bf16[768,256]{1,0:T(8,128)(2,1)S(1)} %collective-permute-done.rest_0_), channel_id=1, source_target_pairs={{0,1},{1,0},{2,3},{3,2},{4,5},{5,4},{6,7},{7,6},{8,9},{9,8},{10,11... | collective-permute-start | bytes 1179656 | tf_op jit(solution)/shard_map/ppermute | solution.py:308
  45.3 15.9 %collective-permute-start.25 = (bf16[768,256]{1,0:T(8,128)(2,1)S(1)}, bf16[768,256]{1,0:T(8,128)(2,1)S(1)}, u32[]{:S(2)}, u32[]{:S(2)}) collective-permute-start(bf16[768,256]{1,0:T(8,128)(2,1)S(1)} %collective-permute-done.22.rest_0_), channel_id=1, source_target_pairs={{0,1},{1,0},{2,3},{3,2},{4,5},{5,4},{6,7},{7,6},{8,9},{9,8},{10,11... | collective-permute-start | bytes 1179656 | tf_op jit(solution)/shard_map/ppermute | solution.py:308
  45.3 16.0 %collective-permute-start.27 = (bf16[768,256]{1,0:T(8,128)(2,1)S(1)}, bf16[768,256]{1,0:T(8,128)(2,1)S(1)}, u32[]{:S(2)}, u32[]{:S(2)}) collective-permute-start(bf16[768,256]{1,0:T(8,128)(2,1)S(1)} %collective-permute-done.26.rest_1_), channel_id=1, source_target_pairs={{0,1},{1,0},{2,3},{3,2},{4,5},{5,4},{6,7},{7,6},{8,9},{9,8},{10,11... | collective-permute-start | bytes 1179656 | tf_op jit(solution)/shard_map/ppermute | solution.py:308
  49.6 12.3 %collective-permute-start.20 = (bf16[768,256]{1,0:T(8,128)(2,1)}, bf16[768,256]{1,0:T(8,128)(2,1)S(1)}, u32[]{:S(2)}, u32[]{:S(2)}) collective-permute-start(bf16[768,256]{1,0:T(8,128)(2,1)} %copy-done.10), channel_id=1, source_target_pairs={{0,1},{1,0},{2,3},{3,2},{4,5},{5,4},{6,7},{7,6},{8,9},{9,8},{10,11... | collective-permute-start | bytes 1179656 | tf_op jit(solution)/shard_map/ppermute | solution.py:308
  49.6 14.5 %collective-permute-start.2 = (bf16[768,256]{1,0:T(8,128)(2,1)S(1)}, bf16[768,256]{1,0:T(8,128)(2,1)S(1)}, u32[]{:S(2)}, u32[]{:S(2)}) collective-permute-start(bf16[768,256]{1,0:T(8,128)(2,1)S(1)} %collective-permute-done.1.rest_0_), channel_id=1, source_target_pairs={{0,4},{2,6},{4,0},{6,2},{8,12},{10,14},{12,8},{14,10},{16,20},{18,... | collective-permute-start | bytes 1179656 | tf_op jit(solution)/shard_map/ppermute | solution.py:305
  61.2 16.1 %collective-permute-start.14 = (bf16[768,256]{1,0:T(8,128)(2,1)S(1)}, bf16[768,256]{1,0:T(8,128)(2,1)S(1)}, u32[]{:S(2)}, u32[]{:S(2)}) collective-permute-start(bf16[768,256]{1,0:T(8,128)(2,1)S(1)} %collective-permute-done.1.rest_0_), channel_id=1, source_target_pairs={{0,1},{1,0},{2,3},{3,2},{4,5},{5,4},{6,7},{7,6},{8,9},{9,8},{10,11... | collective-permute-start | bytes 1179656 | tf_op jit(solution)/shard_map/ppermute | solution.py:308
  61.3 17.0 %collective-permute-start.15 = (bf16[768,256]{1,0:T(8,128)(2,1)S(1)}, bf16[768,256]{1,0:T(8,128)(2,1)S(1)}, u32[]{:S(2)}, u32[]{:S(2)}) collective-permute-start(bf16[768,256]{1,0:T(8,128)(2,1)S(1)} %collective-permute-done.5.rest_1_), channel_id=1, source_target_pairs={{0,1},{1,0},{2,3},{3,2},{4,5},{5,4},{6,7},{7,6},{8,9},{9,8},{10,11... | collective-permute-start | bytes 1179656 | tf_op jit(solution)/shard_map/ppermute | solution.py:308
  61.8 15.3 %collective-permute-start.12 = (bf16[768,256]{1,0:T(8,128)(2,1)S(1)}, bf16[768,256]{1,0:T(8,128)(2,1)S(1)}, u32[]{:S(2)}, u32[]{:S(2)}) collective-permute-start(bf16[768,256]{1,0:T(8,128)(2,1)S(1)} %collective-permute-done.11.rest_2_), channel_id=1, source_target_pairs={{0,2},{2,0},{4,6},{6,4},{8,10},{10,8},{12,14},{14,12},{16,18},{18,... | collective-permute-start | bytes 1179656 | tf_op jit(solution)/shard_map/ppermute | solution.py:305
  64.0 14.3 %collective-permute-start.16 = (bf16[768,256]{1,0:T(8,128)(2,1)S(1)}, bf16[768,256]{1,0:T(8,128)(2,1)S(1)}, u32[]{:S(2)}, u32[]{:S(2)}) collective-permute-start(bf16[768,256]{1,0:T(8,128)(2,1)S(1)} %collective-permute-done.11.rest_2_), channel_id=1, source_target_pairs={{0,1},{1,0},{2,3},{3,2},{4,5},{5,4},{6,7},{7,6},{8,9},{9,8},{10,11... | collective-permute-start | bytes 1179656 | tf_op jit(solution)/shard_map/ppermute | solution.py:308
  64.0 14.8 %collective-permute-start.24 = (bf16[768,256]{1,0:T(8,128)(2,1)}, bf16[768,256]{1,0:T(8,128)(2,1)S(1)}, u32[]{:S(2)}, u32[]{:S(2)}) collective-permute-start(bf16[768,256]{1,0:T(8,128)(2,1)} %collective-permute-done.23.rest_2_), channel_id=1, source_target_pairs={{0,1},{1,0},{2,3},{3,2},{4,5},{5,4},{6,7},{7,6},{8,9},{9,8},{10,11... | collective-permute-start | bytes 1179656 | tf_op jit(solution)/shard_map/ppermute | solution.py:308
  78.3 15.3 %collective-permute-start.10 = (bf16[768,256]{1,0:T(8,128)(2,1)S(1)}, bf16[768,256]{1,0:T(8,128)(2,1)S(1)}, u32[]{:S(2)}, u32[]{:S(2)}) collective-permute-start(bf16[768,256]{1,0:T(8,128)(2,1)S(1)} %collective-permute-done.6.rest_1_), channel_id=1, source_target_pairs={{0,1},{1,0},{2,3},{3,2},{4,5},{5,4},{6,7},{7,6},{8,9},{9,8},{10,11... | collective-permute-start | bytes 1179656 | tf_op jit(solution)/shard_map/ppermute | solution.py:308
  78.3 15.3 %collective-permute-start.9 = (bf16[768,256]{1,0:T(8,128)(2,1)S(1)}, bf16[768,256]{1,0:T(8,128)(2,1)S(1)}, u32[]{:S(2)}, u32[]{:S(2)}) collective-permute-start(bf16[768,256]{1,0:T(8,128)(2,1)S(1)} %collective-permute-done.2.rest_0_), channel_id=1, source_target_pairs={{0,1},{1,0},{2,3},{3,2},{4,5},{5,4},{6,7},{7,6},{8,9},{9,8},{10,11... | collective-permute-start | bytes 1179656 | tf_op jit(solution)/shard_map/ppermute | solution.py:308
  78.8 14.8 %collective-permute-start.13 = (bf16[768,256]{1,0:T(8,128)(2,1)S(1)}, bf16[768,256]{1,0:T(8,128)(2,1)S(1)}, u32[]{:S(2)}, u32[]{:S(2)}) collective-permute-start(bf16[768,256]{1,0:T(8,128)(2,1)S(1)} %collective-permute-done.12.rest_2_), channel_id=1, source_target_pairs={{0,1},{1,0},{2,3},{3,2},{4,5},{5,4},{6,7},{7,6},{8,9},{9,8},{10,11... | collective-permute-start | bytes 1179656 | tf_op jit(solution)/shard_map/ppermute | solution.py:308
  86.0 13.1 %collective-permute-start.4 = (bf16[384,256]{1,0:T(8,128)(2,1)S(1)}, bf16[384,256]{1,0:T(8,128)(2,1)S(1)}, u32[]{:S(2)}, u32[]{:S(2)}) collective-permute-start(bf16[384,256]{1,0:T(8,128)(2,1)S(1)} %collective-permute-done.3.rest_0_), channel_id=1, source_target_pairs={{0,1},{1,0},{2,3},{3,2},{4,5},{5,4},{6,7},{7,6},{8,9},{9,8},{10,11... | collective-permute-start | bytes 589832 | tf_op jit(solution)/shard_map/ppermute | solution.py:308
  86.5 12.6 %collective-permute-start.8 = (bf16[384,256]{1,0:T(8,128)(2,1)S(1)}, bf16[384,256]{1,0:T(8,128)(2,1)S(1)}, u32[]{:S(2)}, u32[]{:S(2)}) collective-permute-start(bf16[384,256]{1,0:T(8,128)(2,1)S(1)} %collective-permute-done.7.rest_1_), channel_id=1, source_target_pairs={{0,1},{1,0},{2,3},{3,2},{4,5},{5,4},{6,7},{7,6},{8,9},{9,8},{10,11... | collective-permute-start | bytes 589832 | tf_op jit(solution)/shard_map/ppermute | solution.py:308
  (31 other events, 208.0 us)

commit v2 on v1

--- a/solution.py
+++ b/solution.py
@@ -47,12 +47,7 @@
     return dot1(ah, bh, dims) + (dot1(ah, bl, dims) + dot1(al, bh, dims))
 
 
-def piece_at(quarter, core, slot):
-    step = (0, 2 - core, 1 + core, 3)[slot]
-    return 4 * core + (quarter ^ step)
-
-
-def cut_pieces(p, b, quarter, core, buf, keep_ref, send_ref):
+def cut_pieces(p, b, own, buf, keep_ref, send_ref):
     half = p.shape[1] // 2
     piece = buf.shape[0] // 8
     pt_high, pt_low = split(p.T)
@@ -62,20 +57,17 @@
     gram = dot1(pt_high, p_high) + (cross + dot1(pt_low, p_high))
     coupling = dot1(bt, p_high) + dot1(bt, p_low)
     coupling = 0.5 * (coupling + coupling.T)
-    correlation = dot1(bt, b)
     at = 0
-    for a in (gram, coupling, correlation):
+    for a in (gram, coupling):
         for i, j in ((0, 0), (1, 0), (1, 1)):
             buf[at * half:(at + 1) * half, :] = a[i * half:(i + 1) * half, j * half:(j + 1) * half]
             at += 1
-    for slot in range(4):
-        at = pl.multiple_of(piece_at(quarter, core, slot) * piece, 8)
-        keep_ref[slot] = buf[pl.ds(at, piece), :]
-        at = pl.multiple_of(piece_at(quarter, 1 - core, slot) * piece, 8)
-        send_ref[slot] = buf[pl.ds(at, piece), :]
-
-
-def stage_call(hamiltonian, units, places, offset, acc, basis=None):
+    for m in range(4):
+        keep_ref[m] = buf[pl.ds(pl.multiple_of((own ^ m) * piece, 8), piece), :]
+        send_ref[m] = buf[pl.ds(pl.multiple_of((own ^ (m + 4)) * piece, 8), piece), :]
+
+
+def stage_call(hamiltonian, units, near, places, offset, acc, basis=None):
     n = len(units)
     rows, _ = hamiltonian.shape
     width = sum(a.shape[0] for a in units[0])
@@ -91,16 +83,16 @@
             pieces.append((i, at, a))
             at += a.shape[0]
     count = len(pieces)
-    tail = places.shape[0] - 2
+    tail = places.shape[0] - 1
 
     def body(places_ref, h_ref, *rest):
         piece_refs, rest = rest[:count], rest[count:]
-        if not first:
-            acc_ref, rest = rest[0], rest[1:]
         if last:
-            b_ref, out_ref, keep_ref, send_ref, hbuf, ubuf, hsem, usem, buf = rest
+            acc_ref, b_ref, out_ref, keep_ref, send_ref, hbuf, ubuf, hsem, usem, buf = rest
+        elif first:
+            out_ref, corr_ref, hbuf, ubuf, hsem, usem = rest
         else:
-            out_ref, hbuf, ubuf, hsem, usem = rest
+            acc_ref, acc_corr_ref, out_ref, corr_ref, hbuf, ubuf, hsem, usem = rest
 
         def hcopy(i, slot):
             at = pl.multiple_of(places_ref[offset + i] * width, 128)
@@ -113,12 +105,21 @@
                     pltpu.make_async_copy(ref, ubuf.at[k, pl.ds(at, a.shape[0]), :], usem.at[k]).start()
         if first:
             out_ref[...] = jnp.zeros_like(out_ref)
+            corr_ref[...] = jnp.zeros_like(corr_ref)
         else:
             out_ref[...] = acc_ref[...]
+            if not last:
+                corr_ref[...] = acc_corr_ref[...]
 
         def step(i, _):
             slot = lax.rem(i, nbuf)
             pltpu.make_async_copy(ubuf.at[i], ubuf.at[i], usem.at[i]).wait()
+            if near:
+                @pl.when(i < near)
+                def _():
+                    u = ubuf[i]
+                    corr_ref[...] += lax.dot_general(u, u, (((0,), (0,)), ((), ())), preferred_element_type=F32)
+
             hcopy(i, slot).wait()
             high, low = split(hbuf[slot])
             u = ubuf[i]
@@ -132,7 +133,7 @@
 
         lax.fori_loop(0, n, step, 0)
         if last:
-            cut_pieces(out_ref[...], b_ref[...], places_ref[tail], places_ref[tail + 1], buf, keep_ref, send_ref)
+            cut_pieces(out_ref[...], b_ref[...], places_ref[tail], buf, keep_ref, send_ref)
 
     any_spec = pl.BlockSpec(memory_space=pl.ANY)
     vmem = pl.BlockSpec(memory_space=pltpu.VMEM)
@@ -141,9 +142,15 @@
     aliases = {}
     if not first:
         aliases = {len(operands): 0}
-        operands.append(acc)
+        operands.append(acc[0])
         in_specs.append(vmem)
+        if not last:
+            aliases[len(operands)] = 1
+            operands.append(acc[1])
+            in_specs.append(vmem)
     out_shape = [jax.ShapeDtypeStruct((rows, nvec), F32)]
+    if not last:
+        out_shape.append(jax.ShapeDtypeStruct((nvec, nvec), F32))
     scratch = [
         pltpu.VMEM((nbuf, rows, width), F32),
         pltpu.VMEM((n, width, nvec), BF16),
@@ -153,8 +160,8 @@
     if last:
         operands.append(basis)
         in_specs.append(vmem)
-        out_shape += [jax.ShapeDtypeStruct((4, 9 * half // 8, half), F32)] * 2
-        scratch.append(pltpu.VMEM((9 * half, half), F32))
+        out_shape += [jax.ShapeDtypeStruct((4, 6 * half // 8, half), F32)] * 2
+        scratch.append(pltpu.VMEM((6 * half, half), F32))
     return pl.pallas_call(
         body,
         name="stage_product",
@@ -166,7 +173,7 @@
         cost_estimate=pl.CostEstimate(
             flops=4 * n * rows * width * nvec, transcendentals=0, bytes_accessed=4 * n * rows * width
         ),
-        compiler_params=pltpu.CompilerParams(vmem_limit_bytes=48 << 20),
+        compiler_params=pltpu.CompilerParams(vmem_limit_bytes=24 << 20),
     )(*operands)
 
 
@@ -189,10 +196,10 @@
     def residual(m):
         return dot3(dot3(m, k), m, NT) - eye
 
-    m = m - dot3(residual(m) * weight, m)
+    m = m - dot1((residual(m) * weight).astype(BF16), m.astype(BF16))
     e = residual(m)
     norm = jnp.max(jnp.sum(jnp.abs(e), axis=1))
-    m = m - dot3(e * weight, m)
+    m = m - dot1((e * weight).astype(BF16), m.astype(BF16))
     return m * scale_row, norm
 
 
@@ -221,37 +228,59 @@
     out_ref[...] = work_w[...] * lax.rsqrt(pivots)
 
 
-def finish_call(product, mine, other, places, scale):
+def inverse_factor(a_ref, out_ref, work_a, work_w):
+    out_ref[...], norm = refine(a_ref[...])
+
+    @pl.when(jnp.logical_not(norm < 3e-3))
+    def _():
+        eliminate(a_ref[...], out_ref, work_a, work_w)
+
+
+def inverse_call(near, far):
+    vmem = pl.BlockSpec(memory_space=pltpu.VMEM)
+    square = pltpu.VMEM(near.shape, F32)
+
+    def body(near_ref, far_ref, out_ref, whole, work_a, work_w):
+        whole[...] = near_ref[...] + far_ref[...]
+        inverse_factor(whole, out_ref, work_a, work_w)
+
+    return pl.pallas_call(
+        body,
+        name="inverse_factor",
+        out_shape=jax.ShapeDtypeStruct(near.shape, F32),
+        in_specs=[vmem, vmem],
+        out_specs=vmem,
+        scratch_shapes=[square, square, square],
+        cost_estimate=pl.CostEstimate(flops=60 * near.shape[0] ** 3, transcendentals=0, bytes_accessed=0),
+        compiler_params=pltpu.CompilerParams(vmem_limit_bytes=12 << 20),
+    )(near, far)
+
+
+def finish_call(product, mine, other, low, places, scale):
     rows, nvec = product.shape
     half = nvec // 2
     _, piece, _ = mine.shape
-    tail = places.shape[0] - 2
-
-    def body(places_ref, p_ref, mine_ref, other_ref, ritz_ref, projected_ref, pbuf, buf, whole, inv, work_a, work_w, sem):
+    tail = places.shape[0] - 1
+
+    def body(places_ref, p_ref, mine_ref, other_ref, low_ref, ritz_ref, projected_ref, pbuf, buf, whole, inv, work_a, work_w, sem):
         copy = pltpu.make_async_copy(p_ref, pbuf, sem)
         copy.start()
-        quarter = places_ref[tail]
-        core = places_ref[tail + 1]
-        for slot in range(4):
-            buf[pl.ds(pl.multiple_of(piece_at(quarter, core, slot) * piece, 8), piece), :] = mine_ref[slot]
-            buf[pl.ds(pl.multiple_of(piece_at(quarter, 1 - core, slot) * piece, 8), piece), :] = other_ref[slot]
-        for q in range(3):
+        own = places_ref[tail]
+        for m in range(4):
+            buf[pl.ds(pl.multiple_of((own ^ m) * piece, 8), piece), :] = mine_ref[m]
+            buf[pl.ds(pl.multiple_of((own ^ (m + 4)) * piece, 8), piece), :] = other_ref[m]
+        for q in range(2):
             at = 3 * q * half
             corner = buf[at + half:at + 2 * half, :]
             whole[q, :half, :half] = buf[at:at + half, :]
             whole[q, half:, :half] = corner
             whole[q, :half, half:] = corner.T
             whole[q, half:, half:] = buf[at + 2 * half:at + 3 * half, :]
-        inv[0], gram_norm = refine(whole[0])
-        inv[1], correlation_norm = refine(whole[2])
-        for at, source, norm in ((0, 0, gram_norm), (1, 2, correlation_norm)):
-            @pl.when(jnp.logical_not(norm < 3e-3))
-            def _():
-                eliminate(whole[source], inv.at[at], work_a, work_w)
+        low = low_ref[...]
+        projected_ref[...] = dot3(dot3(low, whole[1]), low, NT)
+        inverse_factor(whole.at[0], inv, work_a, work_w)
         copy.wait()
-        ritz_ref[...] = dot3(pbuf[...], inv[0] * scale, NT)
-        low = inv[1]
-        projected_ref[...] = dot3(dot3(low, whole[1]), low, NT)
+        ritz_ref[...] = dot3(pbuf[...], inv[...] * scale, NT)
 
     vmem = pl.BlockSpec(memory_space=pltpu.VMEM)
     square = pltpu.VMEM((nvec, nvec), F32)
@@ -259,19 +288,19 @@
         body,
         name="finish",
         out_shape=(jax.ShapeDtypeStruct((rows, nvec), F32), jax.ShapeDtypeStruct((nvec, nvec), F32)),
-        in_specs=[pl.BlockSpec(memory_space=pltpu.SMEM), pl.BlockSpec(memory_space=pl.ANY), vmem, vmem],
+        in_specs=[pl.BlockSpec(memory_space=pltpu.SMEM), pl.BlockSpec(memory_space=pl.ANY), vmem, vmem, vmem],
         out_specs=(vmem, vmem),
         scratch_shapes=[
             pltpu.VMEM((rows, nvec), F32),
-            pltpu.VMEM((9 * half, half), F32),
-            pltpu.VMEM((3, nvec, nvec), F32),
+            pltpu.VMEM((6 * half, half), F32),
             pltpu.VMEM((2, nvec, nvec), F32),
+            square,
             square,
             square,
             pltpu.SemaphoreType.DMA,
         ],
-        compiler_params=pltpu.CompilerParams(vmem_limit_bytes=48 << 20),
-    )(places, product, mine, other)
+        compiler_params=pltpu.CompilerParams(vmem_limit_bytes=16 << 20),
+    )(places, product, mine, other, low)
 
 
 WHOLE = (0, 8)
@@ -307,13 +336,10 @@
     def from_core(a):
         return lax.ppermute(a, "chip", [(0, 1), (1, 0)])
 
-    def spread(a, steps):
-        return lax.ppermute(a, AXES, [(2 * s + c, 2 * (s ^ steps[c]) + c) for s in range(chips) for c in range(2)])
-
     basis = vectors.astype(BF16)
     order = [2 * m + far for turn in TURNS for far in range(2) for m in turn[far]]
     places = jnp.concatenate(
-        [(2 * here + core) ^ jnp.array(order, jnp.int32), jnp.stack([here % 4, core]).astype(jnp.int32)]
+        [(2 * here + core) ^ jnp.array(order, jnp.int32), (4 * core + here % 4).astype(jnp.int32).reshape(1)]
     )
     mine = {0: (basis,)}
     acc = None
@@ -333,18 +359,19 @@
             other[m] = tuple(from_core(a) for a in mine[m])
         units = [mine[m] for m in near] + [other[m] for m in far]
         end = basis if t == len(TURNS) - 1 else None
-        acc, *pieces = stage_call(hamiltonian, units, places, offset, acc, end)
+        acc = stage_call(hamiltonian, units, len(near), places, offset, acc, end)
         offset += len(units)
-    keep, send = pieces
+        if t == len(TURNS) - 2:
+            correlation = acc[1]
+            correlation_far = from_core(correlation)
+    product, keep, send = acc
     a = keep + from_core(send)
-    a = a[:2] + spread(a[2:], (1, 2))
-    a = a[:1] + spread(a[1:], (2, 1))
-    a = a + spread(a, (4, 8))
-    a = a + spread(a, (8, 4))
-    a = jnp.concatenate([a, spread(a, (2, 1))])
-    a = jnp.concatenate([a, spread(a, (1, 2))])
-    b = from_core(a)
-    return finish_call(acc, a, b, places, float(hamiltonian.shape[1]) ** 0.5)
+    b = a[0] + from_chip(a[1], 1) + from_chip(a[2], 2) + from_chip(a[3], 3)
+    b = b + from_chip(b, 4) + from_chip(b, 8) + from_chip(b, 12)
+    mine4 = jnp.stack([b, from_chip(b, 1), from_chip(b, 2), from_chip(b, 3)])
+    other4 = from_core(mine4)
+    low = inverse_call(correlation, correlation_far)
+    return finish_call(product, mine4, other4, low, places, float(hamiltonian.shape[1]) ** 0.5)
 
 
 def solution(mesh):

time: 220 us -> 214 us (0.973)
  waiting for transfers between devices: 49.2 us -> 36.2 us
  starting transfers between devices: 34.6 us -> 40.2 us
    pallas_call x1, Pallas kernels: 81.8 us -> 41.7 us  [finish_call(): pl.pallas_call(body, name='finish', out_shape=(jax.ShapeDtypeStruct((rows...]
    pallas_call x0 -> x1, Pallas kernels: none -> 39.4 us  [inverse_call(): pl.pallas_call(body, name='inverse_factor', out_shape=jax.ShapeDtypeStruc...]
    ppermute x6 -> x0, waiting for transfers between devices: 23.4 us -> none  [spread(): lax.ppermute(a, AXES, [(2 * s + c, 2 * (s ^ steps[c]) + c) for s in range...]
    ppermute x16 -> x25, waiting for transfers between devices: 22.9 us -> 35.1 us  [from_chip(): return lax.ppermute(a, 'rows', [(s, s ^ m) for s in range(chips)])]
    ppermute x16 -> x25, starting transfers between devices: 24.2 us -> 36.4 us  [from_chip(): return lax.ppermute(a, 'rows', [(s, s ^ m) for s in range(chips)])]
    ppermute x6 -> x0, starting transfers between devices: 6.6 us -> none  [spread(): lax.ppermute(a, AXES, [(2 * s + c, 2 * (s ^ steps[c]) + c) for s in range...]
    pallas_call x8, Pallas kernels: 45.3 us -> 48 us  [stage_call(): pl.pallas_call(body, name='stage_product', out_shape=tuple(out_shape), in...]
    unnamed x28 -> x24, local copies, waits for them, and re-layouts: 5.3 us -> 4.54 us
  transfers between devices with their start and end apart: 41 -> 45, of which waited for: 13 -> 14; matrix products, arithmetic and copies ran while one was open for 0% -> 0% of each run, Pallas kernels for 18% -> 39%
where the time goes in v2:
time: 214 us; the launch traced here: 213 us
  Pallas kernels  129 us (60%)
  starting transfers between devices  40.2 us (19%)
  waiting for transfers between devices  36.2 us (17%)
  local copies, waits for them, and re-layouts  4.58 us (2%)
    pallas_call x8, Pallas kernels, stage_call(): pl.pallas_call(body, name='stage_product', out_shape=tuple(out_shape), in...  48 us
    pallas_call x1, Pallas kernels, finish_call(): pl.pallas_call(body, name='finish', out_shape=(jax.ShapeDtypeStruct((rows...  41.7 us
    pallas_call x1, Pallas kernels, inverse_call(): pl.pallas_call(body, name='inverse_factor', out_shape=jax.ShapeDtypeStruc...  39.4 us
    ppermute x25, starting transfers between devices, from_chip(): return lax.ppermute(a, 'rows', [(s, s ^ m) for s in range(chips)])  36.4 us
    ppermute x25, waiting for transfers between devices, from_chip(): return lax.ppermute(a, 'rows', [(s, s ^ m) for s in range(chips)])  35.1 us
    unnamed x24, local copies, waits for them, and re-layouts  4.54 us
  transfers between devices with their start and end apart: 45, of which 14 were waited for; matrix products, arithmetic and copies ran while one was open for 0% of the time, Pallas kernels for 39%

profile of v2, /device:TPU:0, one launch (start us, length us, event | category | flops | bytes accessed | tf_op | source)
XLA Modules:
  0.0 213.3 jit_solution(8658005414113169862)
XLA Ops:
  1.8 3.1 %collective-permute-start.21 = (bf16[768,256]{1,0:T(8,128)(2,1)S(1)}, bf16[768,256]{1,0:T(8,128)(2,1)S(1)}, u32[]{:S(2)}, u32[]{:S(2)}) collective-permute-start(bf16[768,256]{1,0:T(8,128)(2,1)S(1)} %convert_element_type.3.rest_0_.rest_3_), channel_id=1, source_target_pairs={{0,8},{2,10},{4,12},{6,14},{8,0},{10,2},{12,4},{14,6},{16,24},{18,... | collective-permute-start | bytes 1179656 | tf_op jit(solution)/shard_map/ppermute | solution.py:334
  7.9 2.6 %collective-permute-start = (bf16[768,256]{1,0:T(8,128)(2,1)S(1)}, bf16[768,256]{1,0:T(8,128)(2,1)S(1)}, u32[]{:S(2)}, u32[]{:S(2)}) collective-permute-start(bf16[768,256]{1,0:T(8,128)(2,1)S(1)} %convert_element_type.3.rest_0_.rest_3_), channel_id=1, source_target_pairs={{0,16},{2,18},{4,20},{6,22},{8,24},{10,26},{12,28},{14,30},{16,0},... | collective-permute-start | bytes 1179656 | tf_op jit(solution)/shard_map/ppermute | solution.py:334
  10.5 7.9 %collective-permute-done.21.rest_0_ = bf16[768,256]{1,0:T(8,128)(2,1)S(1)} collective-permute-done((bf16[768,256]{1,0:T(8,128)(2,1)S(1)}, bf16[768,256]{1,0:T(8,128)(2,1)S(1)}, u32[]{:S(2)}, u32[]{:S(2)}) %collective-permute-start.21) | collective-permute-done | bytes 393248 | tf_op jit(solution)/shard_map/ppermute | solution.py:334
  18.4 2.6 %collective-permute-start.22 = (bf16[768,256]{1,0:T(8,128)(2,1)S(1)}, bf16[768,256]{1,0:T(8,128)(2,1)S(1)}, u32[]{:S(2)}, u32[]{:S(2)}) collective-permute-start(bf16[768,256]{1,0:T(8,128)(2,1)S(1)} %collective-permute-done.21.rest_0_), channel_id=1, source_target_pairs={{0,2},{2,0},{4,6},{6,4},{8,10},{10,8},{12,14},{14,12},{16,18},{18,... | collective-permute-start | bytes 1179656 | tf_op jit(solution)/shard_map/ppermute | solution.py:334
  21.0 2.5 %collective-permute-start.26 = (bf16[768,256]{1,0:T(8,128)(2,1)S(1)}, bf16[768,256]{1,0:T(8,128)(2,1)S(1)}, u32[]{:S(2)}, u32[]{:S(2)}) collective-permute-start(bf16[768,256]{1,0:T(8,128)(2,1)S(1)} %collective-permute-done.21.rest_0_), channel_id=1, source_target_pairs={{0,4},{2,6},{4,0},{6,2},{8,12},{10,14},{12,8},{14,10},{16,20},{18,... | collective-permute-start | bytes 1179656 | tf_op jit(solution)/shard_map/ppermute | solution.py:334
  25.6 3.3 %collective-permute-done.rest_0_ = bf16[768,256]{1,0:T(8,128)(2,1)S(1)} collective-permute-done((bf16[768,256]{1,0:T(8,128)(2,1)S(1)}, bf16[768,256]{1,0:T(8,128)(2,1)S(1)}, u32[]{:S(2)}, u32[]{:S(2)}) %collective-permute-start) | collective-permute-done | bytes 393248 | tf_op jit(solution)/shard_map/ppermute | solution.py:334
  31.8 2.6 %collective-permute-start.11 = (bf16[768,256]{1,0:T(8,128)(2,1)S(1)}, bf16[768,256]{1,0:T(8,128)(2,1)S(1)}, u32[]{:S(2)}, u32[]{:S(2)}) collective-permute-start(bf16[768,256]{1,0:T(8,128)(2,1)S(1)} %collective-permute-done.rest_0_), channel_id=1, source_target_pairs={{0,4},{2,6},{4,0},{6,2},{8,12},{10,14},{12,8},{14,10},{16,20},{18,... | collective-permute-start | bytes 1179656 | tf_op jit(solution)/shard_map/ppermute | solution.py:334
  36.2 5.5 %collective-permute-done.19.rest_1_ = bf16[768,256]{1,0:T(8,128)(2,1)} collective-permute-done((bf16[768,256]{1,0:T(8,128)(2,1)S(1)}, bf16[768,256]{1,0:T(8,128)(2,1)}, u32[]{:S(2)}, u32[]{:S(2)}) %collective-permute-start.19) | collective-permute-done | bytes 393248 | tf_op jit(solution)/shard_map/ppermute | solution.py:334
  41.7 2.2 %collective-permute-start.23 = (bf16[768,256]{1,0:T(8,128)(2,1)S(1)}, bf16[768,256]{1,0:T(8,128)(2,1)}, u32[]{:S(2)}, u32[]{:S(2)}) collective-permute-start(bf16[768,256]{1,0:T(8,128)(2,1)S(1)} %collective-permute-done.22.rest_0_), channel_id=1, source_target_pairs={{0,4},{2,6},{4,0},{6,2},{8,12},{10,14},{12,8},{14,10},{16,20},{18,... | collective-permute-start | bytes 1179656 | tf_op jit(solution)/shard_map/ppermute | solution.py:334
  45.2 4.4 %collective-permute-done.5.rest_1_ = bf16[768,256]{1,0:T(8,128)(2,1)S(1)} collective-permute-done((bf16[768,256]{1,0:T(8,128)(2,1)S(1)}, bf16[768,256]{1,0:T(8,128)(2,1)S(1)}, u32[]{:S(2)}, u32[]{:S(2)}) %collective-permute-start.5) | collective-permute-done | bytes 393248 | tf_op jit(solution)/shard_map/ppermute | solution.py:334
  52.5 3.1 %stage_product.8 = (f32[768,256]{1,0:T(8,128)S(1)}, f32[256,256]{1,0:T(8,128)S(1)}) custom-call(s32[33]{0:T(128)S(1)} %pad_add_fusion.places_ref, f32[768,24576]{1,0:T(8,128)} %h_ref.15, bf16[768,256]{1,0:T(8,128)(2,1)S(1)} %convert_element_type.3.rest_0_.rest_3_), custom_call_target="tpu_custom_call" | custom-call | flops 603979776 | bytes 2359296 | tf_op jit(solution)/shard_map/stage_product/pallas_call | solution.py:165
  55.7 6.0 %stage_product.9 = (f32[768,256]{1,0:T(8,128)S(1)}, f32[256,256]{1,0:T(8,128)S(1)}) custom-call(s32[33]{0:T(128)S(1)} %pad_add_fusion.places_ref, f32[768,24576]{1,0:T(8,128)} %h_ref.15, bf16[768,256]{1,0:T(8,128)(2,1)S(1)} %copy-done.3, bf16[768,256]{1,0:T(8,128)(2,1)S(1)} %copy-done.9, ...), custom_call_target="tpu_custom_call", output_to_operand_aliasing={{0}: (6, {}), {1}: (7, {})} | custom-call | flops 2415919104 | bytes 9437184 | tf_op jit(solution)/shard_map/stage_product/pallas_call | solution.py:165
  62.3 2.4 %collective-permute-start.12 = (bf16[768,256]{1,0:T(8,128)(2,1)S(1)}, bf16[768,256]{1,0:T(8,128)(2,1)S(1)}, u32[]{:S(2)}, u32[]{:S(2)}) collective-permute-start(bf16[768,256]{1,0:T(8,128)(2,1)S(1)} %collective-permute-done.11.rest_2_), channel_id=1, source_target_pairs={{0,2},{2,0},{4,6},{6,4},{8,10},{10,8},{12,14},{14,12},{16,18},{18,... | collective-permute-start | bytes 1179656 | tf_op jit(solution)/shard_map/ppermute | solution.py:334
  65.3 6.6 %stage_product.10 = (f32[768,256]{1,0:T(8,128)S(1)}, f32[256,256]{1,0:T(8,128)S(1)}) custom-call(s32[33]{0:T(128)S(1)} %pad_add_fusion.places_ref, f32[768,24576]{1,0:T(8,128)} %h_ref.15, bf16[768,256]{1,0:T(8,128)(2,1)S(1)} %collective-permute-done.22.rest_0_, ...), custom_call_target="tpu_custom_call", output_to_operand_aliasing={{0}: (7, {}), {1}: (8, {})} | custom-call | flops 3019898880 | bytes 11796480 | tf_op jit(solution)/shard_map/stage_product/pallas_call | solution.py:165
  71.9 6.9 %stage_product.11 = (f32[768,256]{1,0:T(8,128)S(1)}, f32[256,256]{1,0:T(8,128)S(1)}) custom-call(s32[33]{0:T(128)S(1)} %pad_add_fusion.places_ref, f32[768,24576]{1,0:T(8,128)} %h_ref.15, bf16[768,256]{1,0:T(8,128)(2,1)S(1)} %collective-permute-done.rest_0_, ...), custom_call_target="tpu_custom_call", output_to_operand_aliasing={{0}: (7, {}), {1}: (8, {})} | custom-call | flops 3019898880 | bytes 11796480 | tf_op jit(solution)/shard_map/stage_product/pallas_call | solution.py:165
  80.5 7.7 %stage_product.12 = (f32[768,256]{1,0:T(8,128)S(1)}, f32[256,256]{1,0:T(8,128)S(1)}) custom-call(s32[33]{0:T(128)S(1)} %pad_add_fusion.places_ref, f32[768,24576]{1,0:T(8,128)} %h_ref.15, bf16[768,256]{1,0:T(8,128)(2,1)S(1)} %collective-permute-done.1.rest_0_, ...), custom_call_target="tpu_custom_call", output_to_operand_aliasing={{0}: (8, {}), {1}: (9, {})} | custom-call | flops 3623878656 | bytes 14155776 | tf_op jit(solution)/shard_map/stage_product/pallas_call | solution.py:165
  88.8 7.7 %stage_product.13 = (f32[768,256]{1,0:T(8,128)S(1)}, f32[256,256]{1,0:T(8,128)S(1)}) custom-call(s32[33]{0:T(128)S(1)} %pad_add_fusion.places_ref, f32[768,24576]{1,0:T(8,128)} %h_ref.15, bf16[768,256]{1,0:T(8,128)(2,1)S(1)} %collective-permute-done.2.rest_0_, ...), custom_call_target="tpu_custom_call", output_to_operand_aliasing={{0}: (8, {}), {1}: (9, {})} | custom-call | flops 3623878656 | bytes 14155776 | tf_op jit(solution)/shard_map/stage_product/pallas_call | solution.py:165
  96.5 5.5 %stage_product.14 = (f32[768,256]{1,0:T(8,128)S(1)}, f32[256,256]{1,0:T(8,128)S(1)}) custom-call(s32[33]{0:T(128)S(1)} %pad_add_fusion.places_ref, f32[768,24576]{1,0:T(8,128)} %h_ref.15, bf16[384,256]{1,0:T(8,128)(2,1)S(1)} %collective-permute-done.3.rest_0_, ...), custom_call_target="tpu_custom_call", output_to_operand_aliasing={{0}: (7, {}), {1}: (8, {})} | custom-call | flops 2415919104 | bytes 9437184 | tf_op jit(solution)/shard_map/stage_product/pallas_call | solution.py:165
  102.0 4.6 %stage_product.15 = (f32[768,256]{1,0:T(8,128)S(1)}, f32[4,96,128]{2,1,0:T(8,128)S(1)}, f32[4,96,128]{2,1,0:T(8,128)S(1)}) custom-call(s32[33]{0:T(128)S(1)} %pad_add_fusion.places_ref, f32[768,24576]{1,0:T(8,128)} %h_ref.15, bf16[384,256]{1,0:T(8,128)(2,1)S(1)} %collective-permute-done.4.rest_0_, ...), custom_call_target="tpu_custom_call", output_to_operand_aliasing={{0}: (4, {})} | custom-call | flops 603979776 | bytes 2359296 | tf_op jit(solution)/shard_map/stage_product/pallas_call | solution.py:165
  113.5 2.8 %collective-permute-done.36 = f32[96,128]{1,0:T(8,128)S(1)} collective-permute-done((f32[96,128]{1,0:T(8,128)S(1)}, f32[96,128]{1,0:T(8,128)S(1)}, u32[]{:S(2)}, u32[]{:S(2)}) %collective-permute-start.36) | collective-permute-done | bytes 49184 | tf_op jit(solution)/shard_map/ppermute | solution.py:334
  116.4 3.3 %collective-permute-start.38 = (f32[96,128]{1,0:T(8,128)S(1)}, f32[96,128]{1,0:T(8,128)S(1)}, u32[]{:S(2)}, u32[]{:S(2)}) collective-permute-start(f32[96,128]{1,0:T(8,128)S(1)} %fusion.2), channel_id=1, source_target_pairs={{0,16},{2,18},{4,20},{6,22},{8,24},{10,26},{12,28},{14,30},{16,0},... | collective-permute-start | bytes 147464 | tf_op jit(solution)/shard_map/ppermute | solution.py:334
  121.7 3.8 %collective-permute-done.39 = f32[96,128]{1,0:T(8,128)S(1)} collective-permute-done((f32[96,128]{1,0:T(8,128)S(1)}, f32[96,128]{1,0:T(8,128)S(1)}, u32[]{:S(2)}, u32[]{:S(2)}) %collective-permute-start.39) | collective-permute-done | bytes 49184 | tf_op jit(solution)/shard_map/ppermute | solution.py:334
  132.1 39.4 %inverse_factor.1.low_ref = f32[256,256]{1,0:T(8,128)S(1)} custom-call(f32[256,256]{1,0:T(8,128)S(1)} %get-tuple-element.35.near_ref, f32[256,256]{1,0:T(8,128)S(1)} %collective-permute-done.44.far_ref), custom_call_target="tpu_custom_call" | custom-call | flops 1006632960 | tf_op jit(solution)/shard_map/inverse_factor/pallas_call | solution.py:247
  171.5 41.7 %finish.1 = (f32[768,256]{1,0:T(8,128)}, f32[256,256]{1,0:T(8,128)}) custom-call(s32[33]{0:T(128)S(1)} %pad_add_fusion.places_ref, f32[768,256]{1,0:T(8,128)S(1)} %get-tuple-element.32.p_ref, f32[4,96,128]{2,1,0:T(8,128)S(1)} %pad_maximum_fusion.mine_ref, f32[4,96,128]{2,1,0:T(8,128)S(1)} %collective-permute-done.43.other_ref, ...), custom_call_target="tpu_custom_call" | custom-call | tf_op jit(solution)/shard_map/finish/pallas_call | solution.py:287
  (110 shorter events, 34.1 us)
Async XLA Ops:
  1.8 16.6 %collective-permute-start.21 = (bf16[768,256]{1,0:T(8,128)(2,1)S(1)}, bf16[768,256]{1,0:T(8,128)(2,1)S(1)}, u32[]{:S(2)}, u32[]{:S(2)}) collective-permute-start(bf16[768,256]{1,0:T(8,128)(2,1)S(1)} %convert_element_type.3.rest_0_.rest_3_), channel_id=1, source_target_pairs={{0,8},{2,10},{4,12},{6,14},{8,0},{10,2},{12,4},{14,6},{16,24},{18,... | collective-permute-start | bytes 1179656 | tf_op jit(solution)/shard_map/ppermute | solution.py:334
  4.9 16.1 %collective-permute-start.18 = (bf16[768,256]{1,0:T(8,128)(2,1)S(1)}, bf16[768,256]{1,0:T(8,128)(2,1)S(1)}, u32[]{:S(2)}, u32[]{:S(2)}) collective-permute-start(bf16[768,256]{1,0:T(8,128)(2,1)S(1)} %convert_element_type.3.rest_0_.rest_3_), channel_id=1, source_target_pairs={{0,4},{2,6},{4,0},{6,2},{8,12},{10,14},{12,8},{14,10},{16,20},{18,... | collective-permute-start | bytes 1179656 | tf_op jit(solution)/shard_map/ppermute | solution.py:334
  6.4 17.1 %collective-permute-start.29 = (bf16[768,256]{1,0:T(8,128)(2,1)S(1)}, bf16[768,256]{1,0:T(8,128)(2,1)S(1)}, u32[]{:S(2)}, u32[]{:S(2)}) collective-permute-start(bf16[768,256]{1,0:T(8,128)(2,1)S(1)} %convert_element_type.3.rest_0_.rest_3_), channel_id=1, source_target_pairs={{0,2},{2,0},{4,6},{6,4},{8,10},{10,8},{12,14},{14,12},{16,18},{18,... | collective-permute-start | bytes 1179656 | tf_op jit(solution)/shard_map/ppermute | solution.py:334
  7.9 16.4 %collective-permute-start.32 = (bf16[768,256]{1,0:T(8,128)(2,1)S(1)}, bf16[768,256]{1,0:T(8,128)(2,1)S(1)}, u32[]{:S(2)}, u32[]{:S(2)}) collective-permute-start(bf16[768,256]{1,0:T(8,128)(2,1)S(1)} %convert_element_type.3.rest_0_.rest_3_), channel_id=1, source_target_pairs={{0,1},{1,0},{2,3},{3,2},{4,5},{5,4},{6,7},{7,6},{8,9},{9,8},{10,11... | collective-permute-start | bytes 1179656 | tf_op jit(solution)/shard_map/ppermute | solution.py:337
  7.9 20.9 %collective-permute-start = (bf16[768,256]{1,0:T(8,128)(2,1)S(1)}, bf16[768,256]{1,0:T(8,128)(2,1)S(1)}, u32[]{:S(2)}, u32[]{:S(2)}) collective-permute-start(bf16[768,256]{1,0:T(8,128)(2,1)S(1)} %convert_element_type.3.rest_0_.rest_3_), channel_id=1, source_target_pairs={{0,16},{2,18},{4,20},{6,22},{8,24},{10,26},{12,28},{14,30},{16,0},... | collective-permute-start | bytes 1179656 | tf_op jit(solution)/shard_map/ppermute | solution.py:334
  31.8 12.9 %collective-permute-start.1 = (bf16[768,256]{1,0:T(8,128)(2,1)S(1)}, bf16[768,256]{1,0:T(8,128)(2,1)S(1)}, u32[]{:S(2)}, u32[]{:S(2)}) collective-permute-start(bf16[768,256]{1,0:T(8,128)(2,1)S(1)} %collective-permute-done.rest_0_), channel_id=1, source_target_pairs={{0,8},{2,10},{4,12},{6,14},{8,0},{10,2},{12,4},{14,6},{16,24},{18,... | collective-permute-start | bytes 1179656 | tf_op jit(solution)/shard_map/ppermute | solution.py:334
  31.8 12.9 %collective-permute-start.11 = (bf16[768,256]{1,0:T(8,128)(2,1)S(1)}, bf16[768,256]{1,0:T(8,128)(2,1)S(1)}, u32[]{:S(2)}, u32[]{:S(2)}) collective-permute-start(bf16[768,256]{1,0:T(8,128)(2,1)S(1)} %collective-permute-done.rest_0_), channel_id=1, source_target_pairs={{0,4},{2,6},{4,0},{6,2},{8,12},{10,14},{12,8},{14,10},{16,20},{18,... | collective-permute-start | bytes 1179656 | tf_op jit(solution)/shard_map/ppermute | solution.py:334
  35.1 14.4 %collective-permute-start.5 = (bf16[768,256]{1,0:T(8,128)(2,1)S(1)}, bf16[768,256]{1,0:T(8,128)(2,1)S(1)}, u32[]{:S(2)}, u32[]{:S(2)}) collective-permute-start(bf16[768,256]{1,0:T(8,128)(2,1)S(1)} %collective-permute-done.rest_0_), channel_id=1, source_target_pairs={{0,2},{2,0},{4,6},{6,4},{8,10},{10,8},{12,14},{14,12},{16,18},{18,... | collective-permute-start | bytes 1179656 | tf_op jit(solution)/shard_map/ppermute | solution.py:334
  36.2 13.4 %collective-permute-start.17 = (bf16[768,256]{1,0:T(8,128)(2,1)S(1)}, bf16[768,256]{1,0:T(8,128)(2,1)S(1)}, u32[]{:S(2)}, u32[]{:S(2)}) collective-permute-start(bf16[768,256]{1,0:T(8,128)(2,1)S(1)} %collective-permute-done.rest_0_), channel_id=1, source_target_pairs={{0,1},{1,0},{2,3},{3,2},{4,5},{5,4},{6,7},{7,6},{8,9},{9,8},{10,11... | collective-permute-start | bytes 1179656 | tf_op jit(solution)/shard_map/ppermute | solution.py:337
  44.7 17.0 %collective-permute-start.25 = (bf16[768,256]{1,0:T(8,128)(2,1)S(1)}, bf16[768,256]{1,0:T(8,128)(2,1)S(1)}, u32[]{:S(2)}, u32[]{:S(2)}) collective-permute-start(bf16[768,256]{1,0:T(8,128)(2,1)S(1)} %collective-permute-done.22.rest_0_), channel_id=1, source_target_pairs={{0,1},{1,0},{2,3},{3,2},{4,5},{5,4},{6,7},{7,6},{8,9},{9,8},{10,11... | collective-permute-start | bytes 1179656 | tf_op jit(solution)/shard_map/ppermute | solution.py:337
  44.7 17.1 %collective-permute-start.27 = (bf16[768,256]{1,0:T(8,128)(2,1)S(1)}, bf16[768,256]{1,0:T(8,128)(2,1)S(1)}, u32[]{:S(2)}, u32[]{:S(2)}) collective-permute-start(bf16[768,256]{1,0:T(8,128)(2,1)S(1)} %collective-permute-done.26.rest_1_), channel_id=1, source_target_pairs={{0,1},{1,0},{2,3},{3,2},{4,5},{5,4},{6,7},{7,6},{8,9},{9,8},{10,11... | collective-permute-start | bytes 1179656 | tf_op jit(solution)/shard_map/ppermute | solution.py:337
  49.6 15.2 %collective-permute-start.2 = (bf16[768,256]{1,0:T(8,128)(2,1)S(1)}, bf16[768,256]{1,0:T(8,128)(2,1)S(1)}, u32[]{:S(2)}, u32[]{:S(2)}) collective-permute-start(bf16[768,256]{1,0:T(8,128)(2,1)S(1)} %collective-permute-done.1.rest_0_), channel_id=1, source_target_pairs={{0,4},{2,6},{4,0},{6,2},{8,12},{10,14},{12,8},{14,10},{16,20},{18,... | collective-permute-start | bytes 1179656 | tf_op jit(solution)/shard_map/ppermute | solution.py:334
  52.0 12.8 %collective-permute-start.6 = (bf16[768,256]{1,0:T(8,128)(2,1)S(1)}, bf16[768,256]{1,0:T(8,128)(2,1)S(1)}, u32[]{:S(2)}, u32[]{:S(2)}) collective-permute-start(bf16[768,256]{1,0:T(8,128)(2,1)S(1)} %collective-permute-done.5.rest_1_), channel_id=1, source_target_pairs={{0,8},{2,10},{4,12},{6,14},{8,0},{10,2},{12,4},{14,6},{16,24},{18,... | collective-permute-start | bytes 1179656 | tf_op jit(solution)/shard_map/ppermute | solution.py:334
  61.7 17.2 %collective-permute-start.14 = (bf16[768,256]{1,0:T(8,128)(2,1)S(1)}, bf16[768,256]{1,0:T(8,128)(2,1)S(1)}, u32[]{:S(2)}, u32[]{:S(2)}) collective-permute-start(bf16[768,256]{1,0:T(8,128)(2,1)S(1)} %collective-permute-done.1.rest_0_), channel_id=1, source_target_pairs={{0,1},{1,0},{2,3},{3,2},{4,5},{5,4},{6,7},{7,6},{8,9},{9,8},{10,11... | collective-permute-start | bytes 1179656 | tf_op jit(solution)/shard_map/ppermute | solution.py:337
  61.8 18.1 %collective-permute-start.15 = (bf16[768,256]{1,0:T(8,128)(2,1)S(1)}, bf16[768,256]{1,0:T(8,128)(2,1)S(1)}, u32[]{:S(2)}, u32[]{:S(2)}) collective-permute-start(bf16[768,256]{1,0:T(8,128)(2,1)S(1)} %collective-permute-done.5.rest_1_), channel_id=1, source_target_pairs={{0,1},{1,0},{2,3},{3,2},{4,5},{5,4},{6,7},{7,6},{8,9},{9,8},{10,11... | collective-permute-start | bytes 1179656 | tf_op jit(solution)/shard_map/ppermute | solution.py:337
  62.3 16.5 %collective-permute-start.12 = (bf16[768,256]{1,0:T(8,128)(2,1)S(1)}, bf16[768,256]{1,0:T(8,128)(2,1)S(1)}, u32[]{:S(2)}, u32[]{:S(2)}) collective-permute-start(bf16[768,256]{1,0:T(8,128)(2,1)S(1)} %collective-permute-done.11.rest_2_), channel_id=1, source_target_pairs={{0,2},{2,0},{4,6},{6,4},{8,10},{10,8},{12,14},{14,12},{16,18},{18,... | collective-permute-start | bytes 1179656 | tf_op jit(solution)/shard_map/ppermute | solution.py:334
  64.8 15.2 %collective-permute-start.16 = (bf16[768,256]{1,0:T(8,128)(2,1)S(1)}, bf16[768,256]{1,0:T(8,128)(2,1)S(1)}, u32[]{:S(2)}, u32[]{:S(2)}) collective-permute-start(bf16[768,256]{1,0:T(8,128)(2,1)S(1)} %collective-permute-done.11.rest_2_), channel_id=1, source_target_pairs={{0,1},{1,0},{2,3},{3,2},{4,5},{5,4},{6,7},{7,6},{8,9},{9,8},{10,11... | collective-permute-start | bytes 1179656 | tf_op jit(solution)/shard_map/ppermute | solution.py:337
  64.8 15.7 %collective-permute-start.24 = (bf16[768,256]{1,0:T(8,128)(2,1)}, bf16[768,256]{1,0:T(8,128)(2,1)S(1)}, u32[]{:S(2)}, u32[]{:S(2)}) collective-permute-start(bf16[768,256]{1,0:T(8,128)(2,1)} %collective-permute-done.23.rest_2_), channel_id=1, source_target_pairs={{0,1},{1,0},{2,3},{3,2},{4,5},{5,4},{6,7},{7,6},{8,9},{9,8},{10,11... | collective-permute-start | bytes 1179656 | tf_op jit(solution)/shard_map/ppermute | solution.py:337
  79.9 16.5 %collective-permute-start.10 = (bf16[768,256]{1,0:T(8,128)(2,1)S(1)}, bf16[768,256]{1,0:T(8,128)(2,1)S(1)}, u32[]{:S(2)}, u32[]{:S(2)}) collective-permute-start(bf16[768,256]{1,0:T(8,128)(2,1)S(1)} %collective-permute-done.6.rest_1_), channel_id=1, source_target_pairs={{0,1},{1,0},{2,3},{3,2},{4,5},{5,4},{6,7},{7,6},{8,9},{9,8},{10,11... | collective-permute-start | bytes 1179656 | tf_op jit(solution)/shard_map/ppermute | solution.py:337
  79.9 16.5 %collective-permute-start.9 = (bf16[768,256]{1,0:T(8,128)(2,1)S(1)}, bf16[768,256]{1,0:T(8,128)(2,1)S(1)}, u32[]{:S(2)}, u32[]{:S(2)}) collective-permute-start(bf16[768,256]{1,0:T(8,128)(2,1)S(1)} %collective-permute-done.2.rest_0_), channel_id=1, source_target_pairs={{0,1},{1,0},{2,3},{3,2},{4,5},{5,4},{6,7},{7,6},{8,9},{9,8},{10,11... | collective-permute-start | bytes 1179656 | tf_op jit(solution)/shard_map/ppermute | solution.py:337
  80.5 16.0 %collective-permute-start.13 = (bf16[768,256]{1,0:T(8,128)(2,1)S(1)}, bf16[768,256]{1,0:T(8,128)(2,1)S(1)}, u32[]{:S(2)}, u32[]{:S(2)}) collective-permute-start(bf16[768,256]{1,0:T(8,128)(2,1)S(1)} %collective-permute-done.12.rest_2_), channel_id=1, source_target_pairs={{0,1},{1,0},{2,3},{3,2},{4,5},{5,4},{6,7},{7,6},{8,9},{9,8},{10,11... | collective-permute-start | bytes 1179656 | tf_op jit(solution)/shard_map/ppermute | solution.py:337
  88.2 13.8 %collective-permute-start.4 = (bf16[384,256]{1,0:T(8,128)(2,1)S(1)}, bf16[384,256]{1,0:T(8,128)(2,1)S(1)}, u32[]{:S(2)}, u32[]{:S(2)}) collective-permute-start(bf16[384,256]{1,0:T(8,128)(2,1)S(1)} %collective-permute-done.3.rest_0_), channel_id=1, source_target_pairs={{0,1},{1,0},{2,3},{3,2},{4,5},{5,4},{6,7},{7,6},{8,9},{9,8},{10,11... | collective-permute-start | bytes 589832 | tf_op jit(solution)/shard_map/ppermute | solution.py:337
  88.7 13.3 %collective-permute-start.8 = (bf16[384,256]{1,0:T(8,128)(2,1)S(1)}, bf16[384,256]{1,0:T(8,128)(2,1)S(1)}, u32[]{:S(2)}, u32[]{:S(2)}) collective-permute-start(bf16[384,256]{1,0:T(8,128)(2,1)S(1)} %collective-permute-done.7.rest_1_), channel_id=1, source_target_pairs={{0,1},{1,0},{2,3},{3,2},{4,5},{5,4},{6,7},{7,6},{8,9},{9,8},{10,11... | collective-permute-start | bytes 589832 | tf_op jit(solution)/shard_map/ppermute | solution.py:337
  132.0 39.5 %collective-permute-start.43 = (f32[4,96,128]{2,1,0:T(8,128)S(1)}, f32[4,96,128]{2,1,0:T(8,128)S(1)}, u32[]{:S(2)}, u32[]{:S(2)}) collective-permute-start(f32[4,96,128]{2,1,0:T(8,128)S(1)} %pad_maximum_fusion.mine_ref), channel_id=1, source_target_pairs={{0,1},{1,0},{2,3},{3,2},{4,5},{5,4},{6,7},{7,6},{8,9},{9,8},{10,11... | collective-permute-start | bytes 589832 | tf_op jit(solution)/shard_map/ppermute | solution.py:337
  (33 other events, 224.3 us)

commit v3 on v2

--- a/solution.py
+++ b/solution.py
@@ -47,133 +47,131 @@
     return dot1(ah, bh, dims) + (dot1(ah, bl, dims) + dot1(al, bh, dims))
 
 
-def cut_pieces(p, b, own, buf, keep_ref, send_ref):
-    half = p.shape[1] // 2
-    piece = buf.shape[0] // 8
-    pt_high, pt_low = split(p.T)
-    bt = b.astype(F32).T.astype(BF16)
-    p_high, p_low = split(p)
-    cross = dot1(pt_high, p_low)
-    gram = dot1(pt_high, p_high) + (cross + dot1(pt_low, p_high))
-    coupling = dot1(bt, p_high) + dot1(bt, p_low)
-    coupling = 0.5 * (coupling + coupling.T)
-    at = 0
-    for a in (gram, coupling):
-        for i, j in ((0, 0), (1, 0), (1, 1)):
-            buf[at * half:(at + 1) * half, :] = a[i * half:(i + 1) * half, j * half:(j + 1) * half]
-            at += 1
-    for m in range(4):
-        keep_ref[m] = buf[pl.ds(pl.multiple_of((own ^ m) * piece, 8), piece), :]
-        send_ref[m] = buf[pl.ds(pl.multiple_of((own ^ (m + 4)) * piece, 8), piece), :]
-
-
-def stage_call(hamiltonian, units, near, places, offset, acc, basis=None):
+def cut_call(product, basis, places):
+    _, nvec = product.shape
+    half = nvec // 2
+    piece = 6 * half // 8
+    tail = places.shape[0] - 1
+
+    def body(places_ref, p_ref, b_ref, keep_ref, send_ref, buf):
+        p = p_ref[...]
+        own = places_ref[tail]
+        pt_high, pt_low = split(p.T)
+        bt = b_ref[...].astype(F32).T.astype(BF16)
+        p_high, p_low = split(p)
+        cross = dot1(pt_high, p_low)
+        gram = dot1(pt_high, p_high) + (cross + dot1(pt_low, p_high))
+        coupling = dot1(bt, p_high) + dot1(bt, p_low)
+        coupling = 0.5 * (coupling + coupling.T)
+        at = 0
+        for a in (gram, coupling):
+            for i, j in ((0, 0), (1, 0), (1, 1)):
+                buf[at * half:(at + 1) * half, :] = a[i * half:(i + 1) * half, j * half:(j + 1) * half]
+                at += 1
+        for m in range(4):
+            keep_ref[m] = buf[pl.ds(pl.multiple_of((own ^ m) * piece, 8), piece), :]
+            send_ref[m] = buf[pl.ds(pl.multiple_of((own ^ (m + 4)) * piece, 8), piece), :]
+
+    vmem = pl.BlockSpec(memory_space=pltpu.VMEM)
+    shape = jax.ShapeDtypeStruct((4, piece, half), F32)
+    return pl.pallas_call(
+        body,
+        name="cut_pieces",
+        out_shape=(shape, shape),
+        in_specs=[pl.BlockSpec(memory_space=pltpu.SMEM), vmem, vmem],
+        out_specs=(vmem, vmem),
+        scratch_shapes=[pltpu.VMEM((6 * half, half), F32)],
+        compiler_params=pltpu.CompilerParams(vmem_limit_bytes=16 << 20),
+    )(places, product, basis)
+
+
+BUFFERS = 5
+
+
+def stage_call(hamiltonian, units, near, places, offset, ready, ahead, acc):
     n = len(units)
     rows, _ = hamiltonian.shape
-    width = sum(a.shape[0] for a in units[0])
-    nvec = units[0][0].shape[1]
-    half = nvec // 2
+    width, nvec = units[0].shape
     first = acc is None
-    last = basis is not None
-    nbuf = min(5, n)
-    pieces = []
-    for i, unit in enumerate(units):
-        at = 0
-        for a in unit:
-            pieces.append((i, at, a))
-            at += a.shape[0]
-    count = len(pieces)
-    tail = places.shape[0] - 1
+    count = 3 if near else 2
 
     def body(places_ref, h_ref, *rest):
-        piece_refs, rest = rest[:count], rest[count:]
-        if last:
-            acc_ref, b_ref, out_ref, keep_ref, send_ref, hbuf, ubuf, hsem, usem, buf = rest
-        elif first:
-            out_ref, corr_ref, hbuf, ubuf, hsem, usem = rest
-        else:
-            acc_ref, acc_corr_ref, out_ref, corr_ref, hbuf, ubuf, hsem, usem = rest
-
-        def hcopy(i, slot):
+        unit_refs, rest = rest[:n], rest[n:]
+        if not first:
+            sums, rest = rest[:count], rest[count:]
+        totals, rest = rest[:count], rest[count:]
+        ring, out_ref = totals[:2]
+        ubuf, hsem, usem = rest
+
+        def fetch(i):
             at = pl.multiple_of(places_ref[offset + i] * width, 128)
-            return pltpu.make_async_copy(h_ref.at[:, pl.ds(at, width)], hbuf.at[slot], hsem.at[slot])
-
-        for i in range(nbuf):
-            hcopy(i, i).start()
-            for (k, at, a), ref in zip(pieces, piece_refs):
-                if k == i or (k > i and i == nbuf - 1):
-                    pltpu.make_async_copy(ref, ubuf.at[k, pl.ds(at, a.shape[0]), :], usem.at[k]).start()
-        if first:
-            out_ref[...] = jnp.zeros_like(out_ref)
-            corr_ref[...] = jnp.zeros_like(corr_ref)
-        else:
-            out_ref[...] = acc_ref[...]
-            if not last:
-                corr_ref[...] = acc_corr_ref[...]
+            slot = lax.rem(offset + i, BUFFERS)
+            return pltpu.make_async_copy(h_ref.at[:, pl.ds(at, width)], ring.at[slot], hsem.at[slot])
+
+        for i in range(n):
+            if ready <= i < min(BUFFERS, n + ahead):
+                fetch(i).start()
+            pltpu.make_async_copy(unit_refs[i], ubuf.at[i], usem.at[i]).start()
+        for i in range(n, min(BUFFERS, n + ahead)):
+            fetch(i).start()
+        for k in range(1, count):
+            totals[k][...] = jnp.zeros_like(totals[k]) if first else sums[k][...]
 
         def step(i, _):
-            slot = lax.rem(i, nbuf)
             pltpu.make_async_copy(ubuf.at[i], ubuf.at[i], usem.at[i]).wait()
             if near:
                 @pl.when(i < near)
                 def _():
                     u = ubuf[i]
-                    corr_ref[...] += lax.dot_general(u, u, (((0,), (0,)), ((), ())), preferred_element_type=F32)
-
-            hcopy(i, slot).wait()
-            high, low = split(hbuf[slot])
+                    totals[2][...] += lax.dot_general(u, u, (((0,), (0,)), ((), ())), preferred_element_type=F32)
+
+            @pl.when(i >= ready)
+            def _():
+                fetch(i).wait()
+
+            high, low = split(ring[lax.rem(offset + i, BUFFERS)])
             u = ubuf[i]
             out_ref[...] += dot1(high, u) + dot1(low, u)
 
-            @pl.when(i + nbuf < n)
+            @pl.when(i + BUFFERS < n + ahead)
             def _():
-                hcopy(i + nbuf, slot).start()
+                fetch(i + BUFFERS).start()
 
             return 0
 
         lax.fori_loop(0, n, step, 0)
-        if last:
-            cut_pieces(out_ref[...], b_ref[...], places_ref[tail], buf, keep_ref, send_ref)
+        for i in range(n, n + ahead):
+            fetch(i).wait()
 
     any_spec = pl.BlockSpec(memory_space=pl.ANY)
     vmem = pl.BlockSpec(memory_space=pltpu.VMEM)
-    operands = [places, hamiltonian, *(a for _, _, a in pieces)]
-    in_specs = [pl.BlockSpec(memory_space=pltpu.SMEM), any_spec] + [any_spec] * count
+    operands = [places, hamiltonian, *units]
+    in_specs = [pl.BlockSpec(memory_space=pltpu.SMEM), any_spec] + [any_spec] * n
     aliases = {}
     if not first:
-        aliases = {len(operands): 0}
-        operands.append(acc[0])
-        in_specs.append(vmem)
-        if not last:
-            aliases[len(operands)] = 1
-            operands.append(acc[1])
-            in_specs.append(vmem)
-    out_shape = [jax.ShapeDtypeStruct((rows, nvec), F32)]
-    if not last:
-        out_shape.append(jax.ShapeDtypeStruct((nvec, nvec), F32))
-    scratch = [
-        pltpu.VMEM((nbuf, rows, width), F32),
-        pltpu.VMEM((n, width, nvec), BF16),
-        pltpu.SemaphoreType.DMA((nbuf,)),
-        pltpu.SemaphoreType.DMA((n,)),
-    ]
-    if last:
-        operands.append(basis)
-        in_specs.append(vmem)
-        out_shape += [jax.ShapeDtypeStruct((4, 6 * half // 8, half), F32)] * 2
-        scratch.append(pltpu.VMEM((6 * half, half), F32))
+        aliases = {len(operands) + k: k for k in range(count)}
+        operands += list(acc[:count])
+        in_specs += [vmem] * count
     return pl.pallas_call(
         body,
         name="stage_product",
-        out_shape=tuple(out_shape),
+        out_shape=(
+            jax.ShapeDtypeStruct((BUFFERS, rows, width), F32),
+            jax.ShapeDtypeStruct((rows, nvec), F32),
+            jax.ShapeDtypeStruct((nvec, nvec), F32),
+        )[:count],
         in_specs=in_specs,
-        out_specs=(vmem,) * len(out_shape),
-        scratch_shapes=scratch,
+        out_specs=(vmem,) * count,
+        scratch_shapes=[
+            pltpu.VMEM((n, width, nvec), BF16),
+            pltpu.SemaphoreType.DMA((BUFFERS,)),
+            pltpu.SemaphoreType.DMA((n,)),
+        ],
         input_output_aliases=aliases,
         cost_estimate=pl.CostEstimate(
             flops=4 * n * rows * width * nvec, transcendentals=0, bytes_accessed=4 * n * rows * width
         ),
-        compiler_params=pltpu.CompilerParams(vmem_limit_bytes=24 << 20),
+        compiler_params=pltpu.CompilerParams(vmem_limit_bytes=8 << 20),
     )(*operands)
 
 
@@ -303,24 +301,23 @@
     )(places, product, mine, other, low)
 
 
-WHOLE = (0, 8)
 STAGES = (
-    ((4, ((0, 4, WHOLE),)), (1, ((0, 1, WHOLE),)), (2, ((0, 2, WHOLE),))),
-    ((5, ((4, 1, WHOLE),)), (6, ((4, 2, WHOLE),)), (8, ((0, 8, WHOLE),)), (3, ((2, 1, WHOLE),))),
-    ((7, ((5, 2, WHOLE),)),),
-    ((12, ((8, 4, WHOLE),)), (9, ((8, 1, WHOLE),)), (10, ((8, 2, WHOLE),))),
-    ((14, ((12, 2, WHOLE),)), (13, ((9, 4, WHOLE),)), (11, ((10, 1, WHOLE),))),
-    ((15, ((14, 1, (0, 4)), (13, 2, (4, 8)))),),
+    ((4, 0, 4), (1, 0, 1), (2, 0, 2)),
+    ((5, 4, 1), (6, 4, 2), (8, 0, 8), (3, 2, 1)),
+    ((7, 5, 2),),
+    ((12, 8, 4), (9, 8, 1), (10, 8, 2)),
+    ((14, 12, 2), (13, 9, 4), (11, 10, 1)),
+    ((15, 14, 1),),
 )
 TURNS = (
-    ((0,), ()),
-    ((4, 1, 2), (0,)),
-    ((5, 6), (4, 1, 2)),
-    ((8, 3, 7), (5, 6)),
-    ((12, 9, 10), (8, 3, 7)),
-    ((14, 13, 11), (12, 9, 10)),
-    ((15,), (14, 13, 11)),
-    ((), (15,)),
+    ((0,), (0,), 3),
+    ((4, 1, 2), (), 1),
+    ((5, 6), (4, 1, 2), 1),
+    ((8, 3, 7), (5, 6), 1),
+    ((12, 9, 10), (8, 3, 7), 1),
+    ((14, 13, 11), (12, 9, 10), 1),
+    ((15,), (14, 13, 11), 1),
+    ((), (15,), 0),
 )
 
 
@@ -328,7 +325,6 @@
     chips = lax.axis_size("rows")
     here = lax.axis_index("rows")
     core = lax.axis_index("chip")
-    width = vectors.shape[0]
 
     def from_chip(a, m):
         return lax.ppermute(a, "rows", [(s, s ^ m) for s in range(chips)])
@@ -341,30 +337,25 @@
     places = jnp.concatenate(
         [(2 * here + core) ^ jnp.array(order, jnp.int32), (4 * core + here % 4).astype(jnp.int32).reshape(1)]
     )
-    mine = {0: (basis,)}
+    mine = {0: basis}
     acc = None
     other = {}
-    offset = 0
-    for t, (near, far) in enumerate(TURNS):
+    offset = ready = 0
+    for t, (near, far, ahead) in enumerate(TURNS):
         if 0 < t <= len(STAGES):
-            for m, parts in STAGES[t - 1]:
-                got = []
-                for source, step, (lo, hi) in parts:
-                    a = mine[source][0]
-                    if (lo, hi) != WHOLE:
-                        a = a[lo * width // 8:hi * width // 8]
-                    got.append(from_chip(a, step))
-                mine[m] = tuple(got)
+            for m, source, step in STAGES[t - 1]:
+                mine[m] = from_chip(mine[source], step)
         for m in near:
-            other[m] = tuple(from_core(a) for a in mine[m])
+            other[m] = from_core(mine[m])
         units = [mine[m] for m in near] + [other[m] for m in far]
-        end = basis if t == len(TURNS) - 1 else None
-        acc = stage_call(hamiltonian, units, len(near), places, offset, acc, end)
+        acc = stage_call(hamiltonian, units, len(near), places, offset, ready, ahead, acc)
         offset += len(units)
+        ready = ahead
         if t == len(TURNS) - 2:
-            correlation = acc[1]
+            correlation = acc[2]
             correlation_far = from_core(correlation)
-    product, keep, send = acc
+    product = acc[1]
+    keep, send = cut_call(product, basis, places)
     a = keep + from_core(send)
     b = a[0] + from_chip(a[1], 1) + from_chip(a[2], 2) + from_chip(a[3], 3)
     b = b + from_chip(b, 4) + from_chip(b, 8) + from_chip(b, 12)

time: 214 us -> 209 us (0.977)
    pallas_call x8 -> x9, Pallas kernels: 48 us -> 46 us  [the longest x8 44.6 us: stage_call(): pl.pallas_call(body, name='stage_product', out_shape=(jax.ShapeDtypeStruc...]
    ppermute x25 -> x24, waiting for transfers between devices: 35.1 us -> 33.2 us  [from_chip(): return lax.ppermute(a, 'rows', [(s, s ^ m) for s in range(chips)])]
    ppermute x25 -> x24, starting transfers between devices: 36.4 us -> 35.1 us  [from_chip(): return lax.ppermute(a, 'rows', [(s, s ^ m) for s in range(chips)])]
  transfers between devices with their start and end apart: 45 -> 43, of which waited for: 14 -> 16; matrix products, arithmetic and copies ran while one was open for 0% -> 0% of each run, Pallas kernels for 39% -> 39%
where the time goes in v3:
time: 209 us
  Pallas kernels  127 us (61%)
  starting transfers between devices  38.6 us (18%)
  waiting for transfers between devices  34.6 us (17%)
  local copies, waits for them, and re-layouts  5.56 us (3%)
    pallas_call x8, Pallas kernels, stage_call(): pl.pallas_call(body, name='stage_product', out_shape=(jax.ShapeDtypeStruc...  44.6 us
    pallas_call x1, Pallas kernels, finish_call(): pl.pallas_call(body, name='finish', out_shape=(jax.ShapeDtypeStruct((rows...  41.7 us
    pallas_call x1, Pallas kernels, inverse_call(): pl.pallas_call(body, name='inverse_factor', out_shape=jax.ShapeDtypeStruc...  39.4 us
    ppermute x24, starting transfers between devices, from_chip(): return lax.ppermute(a, 'rows', [(s, s ^ m) for s in range(chips)])  35.1 us
    ppermute x24, waiting for transfers between devices, from_chip(): return lax.ppermute(a, 'rows', [(s, s ^ m) for s in range(chips)])  33.2 us
    unnamed x24, local copies, waits for them, and re-layouts  5.55 us
  transfers between devices with their start and end apart: 43, of which 16 were waited for; matrix products, arithmetic and copies ran while one was open for 0% of the time, Pallas kernels for 39%

profile of v3, /device:TPU:0, one launch (start us, length us, event | category | flops | bytes accessed | tf_op | source)
XLA Modules:
  0.0 208.9 jit_solution(1353741681050217392)
XLA Ops:
  1.8 3.1 %collective-permute-start.19 = (bf16[768,256]{1,0:T(8,128)(2,1)S(1)}, bf16[768,256]{1,0:T(8,128)(2,1)S(1)}, u32[]{:S(2)}, u32[]{:S(2)}) collective-permute-start(bf16[768,256]{1,0:T(8,128)(2,1)S(1)} %convert_element_type.3.rest_0_.b_ref), channel_id=1, source_target_pairs={{0,8},{2,10},{4,12},{6,14},{8,0},{10,2},{12,4},{14,6},{16,24},{18,... | collective-permute-start | bytes 1179656 | tf_op jit(solution)/shard_map/ppermute | solution.py:330
  7.9 2.6 %collective-permute-start = (bf16[768,256]{1,0:T(8,128)(2,1)S(1)}, bf16[768,256]{1,0:T(8,128)(2,1)S(1)}, u32[]{:S(2)}, u32[]{:S(2)}) collective-permute-start(bf16[768,256]{1,0:T(8,128)(2,1)S(1)} %convert_element_type.3.rest_0_.b_ref), channel_id=1, source_target_pairs={{0,16},{2,18},{4,20},{6,22},{8,24},{10,26},{12,28},{14,30},{16,0},... | collective-permute-start | bytes 1179656 | tf_op jit(solution)/shard_map/ppermute | solution.py:330
  10.5 8.4 %collective-permute-done.19.rest_0_ = bf16[768,256]{1,0:T(8,128)(2,1)S(1)} collective-permute-done((bf16[768,256]{1,0:T(8,128)(2,1)S(1)}, bf16[768,256]{1,0:T(8,128)(2,1)S(1)}, u32[]{:S(2)}, u32[]{:S(2)}) %collective-permute-start.19) | collective-permute-done | bytes 393248 | tf_op jit(solution)/shard_map/ppermute | solution.py:330
  18.9 2.6 %collective-permute-start.20 = (bf16[768,256]{1,0:T(8,128)(2,1)S(1)}, bf16[768,256]{1,0:T(8,128)(2,1)S(1)}, u32[]{:S(2)}, u32[]{:S(2)}) collective-permute-start(bf16[768,256]{1,0:T(8,128)(2,1)S(1)} %collective-permute-done.19.rest_0_), channel_id=1, source_target_pairs={{0,2},{2,0},{4,6},{6,4},{8,10},{10,8},{12,14},{14,12},{16,18},{18,... | collective-permute-start | bytes 1179656 | tf_op jit(solution)/shard_map/ppermute | solution.py:330
  22.3 2.5 %collective-permute-start.24 = (bf16[768,256]{1,0:T(8,128)(2,1)S(1)}, bf16[768,256]{1,0:T(8,128)(2,1)S(1)}, u32[]{:S(2)}, u32[]{:S(2)}) collective-permute-start(bf16[768,256]{1,0:T(8,128)(2,1)S(1)} %collective-permute-done.19.rest_0_), channel_id=1, source_target_pairs={{0,4},{2,6},{4,0},{6,2},{8,12},{10,14},{12,8},{14,10},{16,20},{18,... | collective-permute-start | bytes 1179656 | tf_op jit(solution)/shard_map/ppermute | solution.py:330
  26.1 2.1 %collective-permute-done.rest_0_ = bf16[768,256]{1,0:T(8,128)(2,1)S(1)} collective-permute-done((bf16[768,256]{1,0:T(8,128)(2,1)S(1)}, bf16[768,256]{1,0:T(8,128)(2,1)S(1)}, u32[]{:S(2)}, u32[]{:S(2)}) %collective-permute-start) | collective-permute-done | bytes 393248 | tf_op jit(solution)/shard_map/ppermute | solution.py:330
  37.1 4.9 %collective-permute-done.17.rest_1_ = bf16[768,256]{1,0:T(8,128)(2,1)S(1)} collective-permute-done((bf16[768,256]{1,0:T(8,128)(2,1)}, bf16[768,256]{1,0:T(8,128)(2,1)S(1)}, u32[]{:S(2)}, u32[]{:S(2)}) %collective-permute-start.17) | collective-permute-done | bytes 393248 | tf_op jit(solution)/shard_map/ppermute | solution.py:330
  42.0 2.5 %collective-permute-start.21 = (bf16[768,256]{1,0:T(8,128)(2,1)S(1)}, bf16[768,256]{1,0:T(8,128)(2,1)S(1)}, u32[]{:S(2)}, u32[]{:S(2)}) collective-permute-start(bf16[768,256]{1,0:T(8,128)(2,1)S(1)} %collective-permute-done.20.rest_0_), channel_id=1, source_target_pairs={{0,4},{2,6},{4,0},{6,2},{8,12},{10,14},{12,8},{14,10},{16,20},{18,... | collective-permute-start | bytes 1179656 | tf_op jit(solution)/shard_map/ppermute | solution.py:330
  45.2 4.0 %collective-permute-done.6.rest_1_ = bf16[768,256]{1,0:T(8,128)(2,1)S(1)} collective-permute-done((bf16[768,256]{1,0:T(8,128)(2,1)S(1)}, bf16[768,256]{1,0:T(8,128)(2,1)S(1)}, u32[]{:S(2)}, u32[]{:S(2)}) %collective-permute-start.6) | collective-permute-done | bytes 393248 | tf_op jit(solution)/shard_map/ppermute | solution.py:330
  52.0 5.2 %stage_product.8 = (f32[5,768,768]{2,1,0:T(8,128)S(1)}, f32[768,256]{1,0:T(8,128)S(1)}, f32[256,256]{1,0:T(8,128)S(1)}) custom-call(s32[33]{0:T(128)S(1)} %pad_add_fusion.places_ref, f32[768,24576]{1,0:T(8,128)} %h_ref.15, bf16[768,256]{1,0:T(8,128)(2,1)S(1)} %convert_element_type.3.rest_0_.b_ref, bf16[768,256]{1,0:T(8,128)(2,1)S(1)} %copy-done.11), custom_call_target="tpu_custom_call" | custom-call | flops 1207959552 | bytes 4718592 | tf_op jit(solution)/shard_map/stage_product/pallas_call | solution.py:155
  58.8 4.4 %stage_product.9 = (f32[5,768,768]{2,1,0:T(8,128)S(1)}, f32[768,256]{1,0:T(8,128)S(1)}, f32[256,256]{1,0:T(8,128)S(1)}) custom-call(s32[33]{0:T(128)S(1)} %pad_add_fusion.places_ref, f32[768,24576]{1,0:T(8,128)} %h_ref.15, bf16[768,256]{1,0:T(8,128)(2,1)S(1)} %copy-done.1, ...), custom_call_target="tpu_custom_call", output_to_operand_aliasing={{0}: (5, {}), {1}: (6, {}), {2}: (7, {})} | custom-call | flops 1811939328 | bytes 7077888 | tf_op jit(solution)/shard_map/stage_product/pallas_call | solution.py:155
  63.9 6.3 %stage_product.10 = (f32[5,768,768]{2,1,0:T(8,128)S(1)}, f32[768,256]{1,0:T(8,128)S(1)}, f32[256,256]{1,0:T(8,128)S(1)}) custom-call(s32[33]{0:T(128)S(1)} %pad_add_fusion.places_ref, f32[768,24576]{1,0:T(8,128)} %h_ref.15, bf16[768,256]{1,0:T(8,128)(2,1)S(1)} %collective-permute-done.20.rest_0_, ...), custom_call_target="tpu_custom_call", output_to_operand_aliasing={{0}: (7, {}), {1}: (8, {}), {2}: (9, {})} | custom-call | flops 3019898880 | bytes 11796480 | tf_op jit(solution)/shard_map/stage_product/pallas_call | solution.py:155
  71.3 6.6 %stage_product.11 = (f32[5,768,768]{2,1,0:T(8,128)S(1)}, f32[768,256]{1,0:T(8,128)S(1)}, f32[256,256]{1,0:T(8,128)S(1)}) custom-call(s32[33]{0:T(128)S(1)} %pad_add_fusion.places_ref, f32[768,24576]{1,0:T(8,128)} %h_ref.15, bf16[768,256]{1,0:T(8,128)(2,1)S(1)} %collective-permute-done.rest_0_, ...), custom_call_target="tpu_custom_call", output_to_operand_aliasing={{0}: (7, {}), {1}: (8, {}), {2}: (9, {})} | custom-call | flops 3019898880 | bytes 11796480 | tf_op jit(solution)/shard_map/stage_product/pallas_call | solution.py:155
  78.6 7.6 %stage_product.12 = (f32[5,768,768]{2,1,0:T(8,128)S(1)}, f32[768,256]{1,0:T(8,128)S(1)}, f32[256,256]{1,0:T(8,128)S(1)}) custom-call(s32[33]{0:T(128)S(1)} %pad_add_fusion.places_ref, f32[768,24576]{1,0:T(8,128)} %h_ref.15, bf16[768,256]{1,0:T(8,128)(2,1)S(1)} %collective-permute-done.1.rest_0_, ...), custom_call_target="tpu_custom_call", output_to_operand_aliasing={{0}: (8, {}), {1}: (9, {}), {2}: (10, {})} | custom-call | flops 3623878656 | bytes 14155776 | tf_op jit(solution)/shard_map/stage_product/pallas_call | solution.py:155
  86.7 7.6 %stage_product.13 = (f32[5,768,768]{2,1,0:T(8,128)S(1)}, f32[768,256]{1,0:T(8,128)S(1)}, f32[256,256]{1,0:T(8,128)S(1)}) custom-call(s32[33]{0:T(128)S(1)} %pad_add_fusion.places_ref, f32[768,24576]{1,0:T(8,128)} %h_ref.15, bf16[768,256]{1,0:T(8,128)(2,1)S(1)} %collective-permute-done.2.rest_0_, ...), custom_call_target="tpu_custom_call", output_to_operand_aliasing={{0}: (8, {}), {1}: (9, {}), {2}: (10, {})} | custom-call | flops 3623878656 | bytes 14155776 | tf_op jit(solution)/shard_map/stage_product/pallas_call | solution.py:155
  94.3 5.0 %stage_product.14 = (f32[5,768,768]{2,1,0:T(8,128)S(1)}, f32[768,256]{1,0:T(8,128)S(1)}, f32[256,256]{1,0:T(8,128)S(1)}) custom-call(s32[33]{0:T(128)S(1)} %pad_add_fusion.places_ref, f32[768,24576]{1,0:T(8,128)} %h_ref.15, bf16[768,256]{1,0:T(8,128)(2,1)S(1)} %collective-permute-done.3.rest_0_, ...), custom_call_target="tpu_custom_call", output_to_operand_aliasing={{0}: (6, {}), {1}: (7, {}), {2}: (8, {})} | custom-call | flops 2415919104 | bytes 9437184 | tf_op jit(solution)/shard_map/stage_product/pallas_call | solution.py:155
  99.3 1.9 stage_product.15
  105.7 2.0 collective-permute-start.34
  108.3 1.8 collective-permute-done.33
  110.7 2.1 collective-permute-start.35
  115.4 3.2 %collective-permute-done.36 = f32[96,128]{1,0:T(8,128)S(1)} collective-permute-done((f32[96,128]{1,0:T(8,128)S(1)}, f32[96,128]{1,0:T(8,128)S(1)}, u32[]{:S(2)}, u32[]{:S(2)}) %collective-permute-start.36) | collective-permute-done | bytes 49184 | tf_op jit(solution)/shard_map/ppermute | solution.py:330
  125.4 2.1 %collective-permute-done.40 = f32[96,128]{1,0:T(8,128)S(1)} collective-permute-done((f32[96,128]{1,0:T(8,128)S(1)}, f32[96,128]{1,0:T(8,128)S(1)}, u32[]{:S(2)}, u32[]{:S(2)}) %collective-permute-start.40) | collective-permute-done | bytes 49184 | tf_op jit(solution)/shard_map/ppermute | solution.py:330
  127.7 39.4 %inverse_factor.1.low_ref = f32[256,256]{1,0:T(8,128)S(1)} custom-call(f32[256,256]{1,0:T(8,128)S(1)} %get-tuple-element.49.near_ref, f32[256,256]{1,0:T(8,128)S(1)} %collective-permute-done.42.far_ref), custom_call_target="tpu_custom_call" | custom-call | flops 1006632960 | tf_op jit(solution)/shard_map/inverse_factor/pallas_call | solution.py:245
  167.0 41.7 %finish.1 = (f32[768,256]{1,0:T(8,128)}, f32[256,256]{1,0:T(8,128)}) custom-call(s32[33]{0:T(128)S(1)} %pad_add_fusion.places_ref, f32[768,256]{1,0:T(8,128)S(1)} %get-tuple-element.46.p_ref, f32[4,96,128]{2,1,0:T(8,128)S(1)} %pad_maximum_fusion.mine_ref, f32[4,96,128]{2,1,0:T(8,128)S(1)} %collective-permute-done.41.other_ref, ...), custom_call_target="tpu_custom_call" | custom-call | tf_op jit(solution)/shard_map/finish/pallas_call | solution.py:285
  (105 shorter events, 38.2 us)
Async XLA Ops:
  1.8 17.1 %collective-permute-start.19 = (bf16[768,256]{1,0:T(8,128)(2,1)S(1)}, bf16[768,256]{1,0:T(8,128)(2,1)S(1)}, u32[]{:S(2)}, u32[]{:S(2)}) collective-permute-start(bf16[768,256]{1,0:T(8,128)(2,1)S(1)} %convert_element_type.3.rest_0_.b_ref), channel_id=1, source_target_pairs={{0,8},{2,10},{4,12},{6,14},{8,0},{10,2},{12,4},{14,6},{16,24},{18,... | collective-permute-start | bytes 1179656 | tf_op jit(solution)/shard_map/ppermute | solution.py:330
  4.9 16.6 %collective-permute-start.30 = (bf16[768,256]{1,0:T(8,128)(2,1)S(1)}, bf16[768,256]{1,0:T(8,128)(2,1)S(1)}, u32[]{:S(2)}, u32[]{:S(2)}) collective-permute-start(bf16[768,256]{1,0:T(8,128)(2,1)S(1)} %convert_element_type.3.rest_0_.b_ref), channel_id=1, source_target_pairs={{0,1},{1,0},{2,3},{3,2},{4,5},{5,4},{6,7},{7,6},{8,9},{9,8},{10,11... | collective-permute-start | bytes 1179656 | tf_op jit(solution)/shard_map/ppermute | solution.py:333
  4.9 19.9 %collective-permute-start.16 = (bf16[768,256]{1,0:T(8,128)(2,1)S(1)}, bf16[768,256]{1,0:T(8,128)(2,1)}, u32[]{:S(2)}, u32[]{:S(2)}) collective-permute-start(bf16[768,256]{1,0:T(8,128)(2,1)S(1)} %convert_element_type.3.rest_0_.b_ref), channel_id=1, source_target_pairs={{0,4},{2,6},{4,0},{6,2},{8,12},{10,14},{12,8},{14,10},{16,20},{18,... | collective-permute-start | bytes 1179656 | tf_op jit(solution)/shard_map/ppermute | solution.py:330
  6.4 19.2 %collective-permute-start.27 = (bf16[768,256]{1,0:T(8,128)(2,1)S(1)}, bf16[768,256]{1,0:T(8,128)(2,1)S(1)}, u32[]{:S(2)}, u32[]{:S(2)}) collective-permute-start(bf16[768,256]{1,0:T(8,128)(2,1)S(1)} %convert_element_type.3.rest_0_.b_ref), channel_id=1, source_target_pairs={{0,2},{2,0},{4,6},{6,4},{8,10},{10,8},{12,14},{14,12},{16,18},{18,... | collective-permute-start | bytes 1179656 | tf_op jit(solution)/shard_map/ppermute | solution.py:330
  7.9 20.3 %collective-permute-start = (bf16[768,256]{1,0:T(8,128)(2,1)S(1)}, bf16[768,256]{1,0:T(8,128)(2,1)S(1)}, u32[]{:S(2)}, u32[]{:S(2)}) collective-permute-start(bf16[768,256]{1,0:T(8,128)(2,1)S(1)} %convert_element_type.3.rest_0_.b_ref), channel_id=1, source_target_pairs={{0,16},{2,18},{4,20},{6,22},{8,24},{10,26},{12,28},{14,30},{16,0},... | collective-permute-start | bytes 1179656 | tf_op jit(solution)/shard_map/ppermute | solution.py:330
  33.6 15.6 %collective-permute-start.6 = (bf16[768,256]{1,0:T(8,128)(2,1)S(1)}, bf16[768,256]{1,0:T(8,128)(2,1)S(1)}, u32[]{:S(2)}, u32[]{:S(2)}) collective-permute-start(bf16[768,256]{1,0:T(8,128)(2,1)S(1)} %collective-permute-done.rest_0_), channel_id=1, source_target_pairs={{0,2},{2,0},{4,6},{6,4},{8,10},{10,8},{12,14},{14,12},{16,18},{18,... | collective-permute-start | bytes 1179656 | tf_op jit(solution)/shard_map/ppermute | solution.py:330
  34.6 14.6 %collective-permute-start.9 = (bf16[768,256]{1,0:T(8,128)(2,1)S(1)}, bf16[768,256]{1,0:T(8,128)(2,1)S(1)}, u32[]{:S(2)}, u32[]{:S(2)}) collective-permute-start(bf16[768,256]{1,0:T(8,128)(2,1)S(1)} %collective-permute-done.rest_0_), channel_id=1, source_target_pairs={{0,4},{2,6},{4,0},{6,2},{8,12},{10,14},{12,8},{14,10},{16,20},{18,... | collective-permute-start | bytes 1179656 | tf_op jit(solution)/shard_map/ppermute | solution.py:330
  37.1 12.6 %collective-permute-start.15 = (bf16[768,256]{1,0:T(8,128)(2,1)S(1)}, bf16[768,256]{1,0:T(8,128)(2,1)S(1)}, u32[]{:S(2)}, u32[]{:S(2)}) collective-permute-start(bf16[768,256]{1,0:T(8,128)(2,1)S(1)} %collective-permute-done.rest_0_), channel_id=1, source_target_pairs={{0,1},{1,0},{2,3},{3,2},{4,5},{5,4},{6,7},{7,6},{8,9},{9,8},{10,11... | collective-permute-start | bytes 1179656 | tf_op jit(solution)/shard_map/ppermute | solution.py:333
  42.0 15.2 %collective-permute-start.21 = (bf16[768,256]{1,0:T(8,128)(2,1)S(1)}, bf16[768,256]{1,0:T(8,128)(2,1)S(1)}, u32[]{:S(2)}, u32[]{:S(2)}) collective-permute-start(bf16[768,256]{1,0:T(8,128)(2,1)S(1)} %collective-permute-done.20.rest_0_), channel_id=1, source_target_pairs={{0,4},{2,6},{4,0},{6,2},{8,12},{10,14},{12,8},{14,10},{16,20},{18,... | collective-permute-start | bytes 1179656 | tf_op jit(solution)/shard_map/ppermute | solution.py:330
  44.5 14.2 %collective-permute-start.23 = (bf16[768,256]{1,0:T(8,128)(2,1)S(1)}, bf16[768,256]{1,0:T(8,128)(2,1)S(1)}, u32[]{:S(2)}, u32[]{:S(2)}) collective-permute-start(bf16[768,256]{1,0:T(8,128)(2,1)S(1)} %collective-permute-done.20.rest_0_), channel_id=1, source_target_pairs={{0,1},{1,0},{2,3},{3,2},{4,5},{5,4},{6,7},{7,6},{8,9},{9,8},{10,11... | collective-permute-start | bytes 1179656 | tf_op jit(solution)/shard_map/ppermute | solution.py:333
  49.2 14.0 %collective-permute-start.25 = (bf16[768,256]{1,0:T(8,128)(2,1)S(1)}, bf16[768,256]{1,0:T(8,128)(2,1)S(1)}, u32[]{:S(2)}, u32[]{:S(2)}) collective-permute-start(bf16[768,256]{1,0:T(8,128)(2,1)S(1)} %collective-permute-done.24.rest_1_), channel_id=1, source_target_pairs={{0,1},{1,0},{2,3},{3,2},{4,5},{5,4},{6,7},{7,6},{8,9},{9,8},{10,11... | collective-permute-start | bytes 1179656 | tf_op jit(solution)/shard_map/ppermute | solution.py:333
  49.2 14.1 %collective-permute-start.18 = (bf16[768,256]{1,0:T(8,128)(2,1)S(1)}, bf16[768,256]{1,0:T(8,128)(2,1)S(1)}, u32[]{:S(2)}, u32[]{:S(2)}) collective-permute-start(bf16[768,256]{1,0:T(8,128)(2,1)S(1)} %collective-permute-done.17.rest_1_), channel_id=1, source_target_pairs={{0,1},{1,0},{2,3},{3,2},{4,5},{5,4},{6,7},{7,6},{8,9},{9,8},{10,11... | collective-permute-start | bytes 1179656 | tf_op jit(solution)/shard_map/ppermute | solution.py:333
  49.7 14.1 %collective-permute-start.2 = (bf16[768,256]{1,0:T(8,128)(2,1)S(1)}, bf16[768,256]{1,0:T(8,128)(2,1)S(1)}, u32[]{:S(2)}, u32[]{:S(2)}) collective-permute-start(bf16[768,256]{1,0:T(8,128)(2,1)S(1)} %collective-permute-done.1.rest_0_), channel_id=1, source_target_pairs={{0,4},{2,6},{4,0},{6,2},{8,12},{10,14},{12,8},{14,10},{16,20},{18,... | collective-permute-start | bytes 1179656 | tf_op jit(solution)/shard_map/ppermute | solution.py:330
  57.2 13.0 %collective-permute-start.10 = (bf16[768,256]{1,0:T(8,128)(2,1)S(1)}, bf16[768,256]{1,0:T(8,128)(2,1)S(1)}, u32[]{:S(2)}, u32[]{:S(2)}) collective-permute-start(bf16[768,256]{1,0:T(8,128)(2,1)S(1)} %collective-permute-done.9.rest_2_), channel_id=1, source_target_pairs={{0,2},{2,0},{4,6},{6,4},{8,10},{10,8},{12,14},{14,12},{16,18},{18,... | collective-permute-start | bytes 1179656 | tf_op jit(solution)/shard_map/ppermute | solution.py:330
  63.2 14.7 %collective-permute-start.12 = (bf16[768,256]{1,0:T(8,128)(2,1)S(1)}, bf16[768,256]{1,0:T(8,128)(2,1)S(1)}, u32[]{:S(2)}, u32[]{:S(2)}) collective-permute-start(bf16[768,256]{1,0:T(8,128)(2,1)S(1)} %collective-permute-done.1.rest_0_), channel_id=1, source_target_pairs={{0,1},{1,0},{2,3},{3,2},{4,5},{5,4},{6,7},{7,6},{8,9},{9,8},{10,11... | collective-permute-start | bytes 1179656 | tf_op jit(solution)/shard_map/ppermute | solution.py:333
  63.3 14.7 %collective-permute-start.13 = (bf16[768,256]{1,0:T(8,128)(2,1)S(1)}, bf16[768,256]{1,0:T(8,128)(2,1)S(1)}, u32[]{:S(2)}, u32[]{:S(2)}) collective-permute-start(bf16[768,256]{1,0:T(8,128)(2,1)S(1)} %collective-permute-done.6.rest_1_), channel_id=1, source_target_pairs={{0,1},{1,0},{2,3},{3,2},{4,5},{5,4},{6,7},{7,6},{8,9},{9,8},{10,11... | collective-permute-start | bytes 1179656 | tf_op jit(solution)/shard_map/ppermute | solution.py:333
  63.8 14.7 %collective-permute-start.22 = (bf16[768,256]{1,0:T(8,128)(2,1)S(1)}, bf16[768,256]{1,0:T(8,128)(2,1)S(1)}, u32[]{:S(2)}, u32[]{:S(2)}) collective-permute-start(bf16[768,256]{1,0:T(8,128)(2,1)S(1)} %collective-permute-done.21.rest_2_), channel_id=1, source_target_pairs={{0,1},{1,0},{2,3},{3,2},{4,5},{5,4},{6,7},{7,6},{8,9},{9,8},{10,11... | collective-permute-start | bytes 1179656 | tf_op jit(solution)/shard_map/ppermute | solution.py:333
  70.2 16.5 %collective-permute-start.14 = (bf16[768,256]{1,0:T(8,128)(2,1)S(1)}, bf16[768,256]{1,0:T(8,128)(2,1)S(1)}, u32[]{:S(2)}, u32[]{:S(2)}) collective-permute-start(bf16[768,256]{1,0:T(8,128)(2,1)S(1)} %collective-permute-done.9.rest_2_), channel_id=1, source_target_pairs={{0,1},{1,0},{2,3},{3,2},{4,5},{5,4},{6,7},{7,6},{8,9},{9,8},{10,11... | collective-permute-start | bytes 1179656 | tf_op jit(solution)/shard_map/ppermute | solution.py:333
  70.7 15.5 %collective-permute-start.3 = (bf16[768,256]{1,0:T(8,128)(2,1)S(1)}, bf16[768,256]{1,0:T(8,128)(2,1)S(1)}, u32[]{:S(2)}, u32[]{:S(2)}) collective-permute-start(bf16[768,256]{1,0:T(8,128)(2,1)S(1)} %collective-permute-done.2.rest_0_), channel_id=1, source_target_pairs={{0,2},{2,0},{4,6},{6,4},{8,10},{10,8},{12,14},{14,12},{16,18},{18,... | collective-permute-start | bytes 1179656 | tf_op jit(solution)/shard_map/ppermute | solution.py:330
  77.9 16.4 %collective-permute-start.5 = (bf16[768,256]{1,0:T(8,128)(2,1)S(1)}, bf16[768,256]{1,0:T(8,128)(2,1)S(1)}, u32[]{:S(2)}, u32[]{:S(2)}) collective-permute-start(bf16[768,256]{1,0:T(8,128)(2,1)S(1)} %collective-permute-done.2.rest_0_), channel_id=1, source_target_pairs={{0,1},{1,0},{2,3},{3,2},{4,5},{5,4},{6,7},{7,6},{8,9},{9,8},{10,11... | collective-permute-start | bytes 1179656 | tf_op jit(solution)/shard_map/ppermute | solution.py:333
  78.0 16.3 %collective-permute-start.11 = (bf16[768,256]{1,0:T(8,128)(2,1)S(1)}, bf16[768,256]{1,0:T(8,128)(2,1)S(1)}, u32[]{:S(2)}, u32[]{:S(2)}) collective-permute-start(bf16[768,256]{1,0:T(8,128)(2,1)S(1)} %collective-permute-done.10.rest_2_), channel_id=1, source_target_pairs={{0,1},{1,0},{2,3},{3,2},{4,5},{5,4},{6,7},{7,6},{8,9},{9,8},{10,11... | collective-permute-start | bytes 1179656 | tf_op jit(solution)/shard_map/ppermute | solution.py:333
  78.5 15.8 %collective-permute-start.8 = (bf16[768,256]{1,0:T(8,128)(2,1)S(1)}, bf16[768,256]{1,0:T(8,128)(2,1)S(1)}, u32[]{:S(2)}, u32[]{:S(2)}) collective-permute-start(bf16[768,256]{1,0:T(8,128)(2,1)S(1)} %collective-permute-done.7.rest_1_), channel_id=1, source_target_pairs={{0,1},{1,0},{2,3},{3,2},{4,5},{5,4},{6,7},{7,6},{8,9},{9,8},{10,11... | collective-permute-start | bytes 1179656 | tf_op jit(solution)/shard_map/ppermute | solution.py:333
  86.2 13.1 %collective-permute-start.4 = (bf16[768,256]{1,0:T(8,128)(2,1)S(1)}, bf16[768,256]{1,0:T(8,128)(2,1)S(1)}, u32[]{:S(2)}, u32[]{:S(2)}) collective-permute-start(bf16[768,256]{1,0:T(8,128)(2,1)S(1)} %collective-permute-done.3.rest_0_), channel_id=1, source_target_pairs={{0,1},{1,0},{2,3},{3,2},{4,5},{5,4},{6,7},{7,6},{8,9},{9,8},{10,11... | collective-permute-start | bytes 1179656 | tf_op jit(solution)/shard_map/ppermute | solution.py:333
  127.6 39.5 %collective-permute-start.41 = (f32[4,96,128]{2,1,0:T(8,128)S(1)}, f32[4,96,128]{2,1,0:T(8,128)S(1)}, u32[]{:S(2)}, u32[]{:S(2)}) collective-permute-start(f32[4,96,128]{2,1,0:T(8,128)S(1)} %pad_maximum_fusion.mine_ref), channel_id=1, source_target_pairs={{0,1},{1,0},{2,3},{3,2},{4,5},{5,4},{6,7},{7,6},{8,9},{9,8},{10,11... | collective-permute-start | bytes 589832 | tf_op jit(solution)/shard_map/ppermute | solution.py:333
  (31 other events, 164.8 us)

commit v4 on v3

--- a/solution.py
+++ b/solution.py
@@ -117,13 +117,8 @@
         for k in range(1, count):
             totals[k][...] = jnp.zeros_like(totals[k]) if first else sums[k][...]
 
-        def step(i, _):
+        def step(i, correlate):
             pltpu.make_async_copy(ubuf.at[i], ubuf.at[i], usem.at[i]).wait()
-            if near:
-                @pl.when(i < near)
-                def _():
-                    u = ubuf[i]
-                    totals[2][...] += lax.dot_general(u, u, (((0,), (0,)), ((), ())), preferred_element_type=F32)
 
             @pl.when(i >= ready)
             def _():
@@ -131,15 +126,26 @@
 
             high, low = split(ring[lax.rem(offset + i, BUFFERS)])
             u = ubuf[i]
+            if correlate:
+                totals[2][...] += lax.dot_general(u, u, (((0,), (0,)), ((), ())), preferred_element_type=F32)
             out_ref[...] += dot1(high, u) + dot1(low, u)
 
             @pl.when(i + BUFFERS < n + ahead)
             def _():
                 fetch(i + BUFFERS).start()
 
+        def near_step(i, _):
+            step(i, True)
             return 0
 
-        lax.fori_loop(0, n, step, 0)
+        def far_step(i, _):
+            step(i, False)
+            return 0
+
+        if near:
+            lax.fori_loop(0, near, near_step, 0)
+        if near < n:
+            lax.fori_loop(near, n, far_step, 0)
         for i in range(n, n + ahead):
             fetch(i).wait()
 
@@ -310,14 +316,17 @@
     ((15, 14, 1),),
 )
 TURNS = (
-    ((0,), (0,), 3),
-    ((4, 1, 2), (), 1),
-    ((5, 6), (4, 1, 2), 1),
-    ((8, 3, 7), (5, 6), 1),
-    ((12, 9, 10), (8, 3, 7), 1),
-    ((14, 13, 11), (12, 9, 10), 1),
-    ((15,), (14, 13, 11), 1),
-    ((), (15,), 0),
+    ((0,), (0,), 3, (4, 1, 2)),
+    ((4, 1, 2), (), 1, (5, 6, 8, 3)),
+    ((), (4, 1, 2), 2, (5, 6, 8, 3)),
+    ((5, 6), (), 1, (7, 8, 3)),
+    ((), (5, 6), 3, (7, 8, 3)),
+    ((8, 3, 7), (), 2, (12, 9, 10)),
+    ((12, 9, 10), (8, 3, 7), 1, (14, 13, 11)),
+    ((14, 13, 11), (12, 9, 10), 1, (15,)),
+    ((), (14, 13, 11), 1, (15,)),
+    ((15,), (), 1, ()),
+    ((), (15,), 0, ()),
 )
 
 
@@ -341,18 +350,20 @@
     acc = None
     other = {}
     offset = ready = 0
-    for t, (near, far, ahead) in enumerate(TURNS):
-        if 0 < t <= len(STAGES):
-            for m, source, step in STAGES[t - 1]:
-                mine[m] = from_chip(mine[source], step)
+    for stage in STAGES:
+        for m, source, step in stage:
+            mine[m] = from_chip(mine[source], step)
+    for t, (near, far, ahead, _) in enumerate(TURNS):
         for m in near:
             other[m] = from_core(mine[m])
         units = [mine[m] for m in near] + [other[m] for m in far]
-        acc = stage_call(hamiltonian, units, len(near), places, offset, ready, ahead, acc)
+        sums = stage_call(hamiltonian, units, len(near), places, offset, ready, ahead, acc)
+        acc = sums if near else (*sums, acc[2])
         offset += len(units)
         ready = ahead
+        if near:
+            correlation = acc[2]
         if t == len(TURNS) - 2:
-            correlation = acc[2]
             correlation_far = from_core(correlation)
     product = acc[1]
     keep, send = cut_call(product, basis, places)

time: 209 us -> 215 us (1.029)
  waiting for transfers between devices: 34.6 us -> 39.2 us
  Pallas kernels: 127 us -> 130 us
  starting transfers between devices: 38.6 us -> 36.4 us
    ppermute x24, waiting for transfers between devices: 33.2 us -> 37.8 us  [from_chip(): return lax.ppermute(a, 'rows', [(s, s ^ m) for s in range(chips)])]
    pallas_call x8 -> x11, Pallas kernels: 44.6 us -> 47.9 us  [stage_call(): pl.pallas_call(body, name='stage_product', out_shape=(jax.ShapeDtypeStruc...]
    ppermute x24, starting transfers between devices: 35.1 us -> 32.8 us  [from_chip(): return lax.ppermute(a, 'rows', [(s, s ^ m) for s in range(chips)])]
  transfers between devices with their start and end apart: 43 -> 43, of which waited for: 16 -> 15; matrix products, arithmetic and copies ran while one was open for 0% -> 0% of each run, Pallas kernels for 39% -> 40%
where the time goes in v4:
time: 215 us
  Pallas kernels  130 us (60%)
  waiting for transfers between devices  39.2 us (18%)
  starting transfers between devices  36.4 us (17%)
  local copies, waits for them, and re-layouts  5.53 us (3%)
    pallas_call x11, Pallas kernels, stage_call(): pl.pallas_call(body, name='stage_product', out_shape=(jax.ShapeDtypeStruc...  47.9 us
    pallas_call x1, Pallas kernels, finish_call(): pl.pallas_call(body, name='finish', out_shape=(jax.ShapeDtypeStruct((rows...  41.7 us
    pallas_call x1, Pallas kernels, inverse_call(): pl.pallas_call(body, name='inverse_factor', out_shape=jax.ShapeDtypeStruc...  39.4 us
    ppermute x24, waiting for transfers between devices, from_chip(): return lax.ppermute(a, 'rows', [(s, s ^ m) for s in range(chips)])  37.8 us
    ppermute x24, starting transfers between devices, from_chip(): return lax.ppermute(a, 'rows', [(s, s ^ m) for s in range(chips)])  32.8 us
    unnamed x24, local copies, waits for them, and re-layouts  5.52 us
  transfers between devices with their start and end apart: 43, of which 15 were waited for; matrix products, arithmetic and copies ran while one was open for 0% of the time, Pallas kernels for 40%

profile of v4, /device:TPU:0, one launch (start us, length us, event | category | flops | bytes accessed | tf_op | source)
XLA Modules:
  0.0 214.7 jit_solution(11288788892772783744)
XLA Ops:
  1.8 3.1 %collective-permute-start.19 = (bf16[768,256]{1,0:T(8,128)(2,1)S(1)}, bf16[768,256]{1,0:T(8,128)(2,1)S(1)}, u32[]{:S(2)}, u32[]{:S(2)}) collective-permute-start(bf16[768,256]{1,0:T(8,128)(2,1)S(1)} %convert_element_type.3.rest_0_.b_ref), channel_id=1, source_target_pairs={{0,8},{2,10},{4,12},{6,14},{8,0},{10,2},{12,4},{14,6},{16,24},{18,... | collective-permute-start | bytes 1179656 | tf_op jit(solution)/shard_map/ppermute | solution.py:339
  7.9 2.6 %collective-permute-start = (bf16[768,256]{1,0:T(8,128)(2,1)S(1)}, bf16[768,256]{1,0:T(8,128)(2,1)S(1)}, u32[]{:S(2)}, u32[]{:S(2)}) collective-permute-start(bf16[768,256]{1,0:T(8,128)(2,1)S(1)} %convert_element_type.3.rest_0_.b_ref), channel_id=1, source_target_pairs={{0,16},{2,18},{4,20},{6,22},{8,24},{10,26},{12,28},{14,30},{16,0},... | collective-permute-start | bytes 1179656 | tf_op jit(solution)/shard_map/ppermute | solution.py:339
  10.5 7.9 %collective-permute-done.19.rest_0_ = bf16[768,256]{1,0:T(8,128)(2,1)S(1)} collective-permute-done((bf16[768,256]{1,0:T(8,128)(2,1)S(1)}, bf16[768,256]{1,0:T(8,128)(2,1)S(1)}, u32[]{:S(2)}, u32[]{:S(2)}) %collective-permute-start.19) | collective-permute-done | bytes 393248 | tf_op jit(solution)/shard_map/ppermute | solution.py:339
  20.5 2.6 %collective-permute-start.20 = (bf16[768,256]{1,0:T(8,128)(2,1)S(1)}, bf16[768,256]{1,0:T(8,128)(2,1)S(1)}, u32[]{:S(2)}, u32[]{:S(2)}) collective-permute-start(bf16[768,256]{1,0:T(8,128)(2,1)S(1)} %collective-permute-done.19.rest_0_), channel_id=1, source_target_pairs={{0,2},{2,0},{4,6},{6,4},{8,10},{10,8},{12,14},{14,12},{16,18},{18,... | collective-permute-start | bytes 1179656 | tf_op jit(solution)/shard_map/ppermute | solution.py:339
  23.1 5.8 %collective-permute-done.rest_0_ = bf16[768,256]{1,0:T(8,128)(2,1)S(1)} collective-permute-done((bf16[768,256]{1,0:T(8,128)(2,1)S(1)}, bf16[768,256]{1,0:T(8,128)(2,1)S(1)}, u32[]{:S(2)}, u32[]{:S(2)}) %collective-permute-start) | collective-permute-done | bytes 393248 | tf_op jit(solution)/shard_map/ppermute | solution.py:339
  35.9 4.9 %collective-permute-done.24.rest_1_ = bf16[768,256]{1,0:T(8,128)(2,1)S(1)} collective-permute-done((bf16[768,256]{1,0:T(8,128)(2,1)S(1)}, bf16[768,256]{1,0:T(8,128)(2,1)S(1)}, u32[]{:S(2)}, u32[]{:S(2)}) %collective-permute-start.24) | collective-permute-done | bytes 393248 | tf_op jit(solution)/shard_map/ppermute | solution.py:339
  43.6 6.2 %collective-permute-done.6.rest_1_ = bf16[768,256]{1,0:T(8,128)(2,1)S(1)} collective-permute-done((bf16[768,256]{1,0:T(8,128)(2,1)S(1)}, bf16[768,256]{1,0:T(8,128)(2,1)S(1)}, u32[]{:S(2)}, u32[]{:S(2)}) %collective-permute-start.6) | collective-permute-done | bytes 393248 | tf_op jit(solution)/shard_map/ppermute | solution.py:339
  49.9 2.3 %collective-permute-start.21 = (bf16[768,256]{1,0:T(8,128)(2,1)S(1)}, bf16[768,256]{1,0:T(8,128)(2,1)S(1)}, u32[]{:S(2)}, u32[]{:S(2)}) collective-permute-start(bf16[768,256]{1,0:T(8,128)(2,1)S(1)} %collective-permute-done.20.rest_0_), channel_id=1, source_target_pairs={{0,4},{2,6},{4,0},{6,2},{8,12},{10,14},{12,8},{14,10},{16,20},{18,... | collective-permute-start | bytes 1179656 | tf_op jit(solution)/shard_map/ppermute | solution.py:339
  53.3 5.2 %stage_product.11 = (f32[5,768,768]{2,1,0:T(8,128)S(1)}, f32[768,256]{1,0:T(8,128)S(1)}, f32[256,256]{1,0:T(8,128)S(1)}) custom-call(s32[33]{0:T(128)S(1)} %pad_add_fusion.places_ref, f32[768,24576]{1,0:T(8,128)} %h_ref.21, bf16[768,256]{1,0:T(8,128)(2,1)S(1)} %convert_element_type.3.rest_0_.b_ref, bf16[768,256]{1,0:T(8,128)(2,1)S(1)} %copy-done.11), custom_call_target="tpu_custom_call" | custom-call | flops 1207959552 | bytes 4718592 | tf_op jit(solution)/shard_map/stage_product/pallas_call | solution.py:161
  58.5 3.9 %stage_product.12 = (f32[5,768,768]{2,1,0:T(8,128)S(1)}, f32[768,256]{1,0:T(8,128)S(1)}, f32[256,256]{1,0:T(8,128)S(1)}) custom-call(s32[33]{0:T(128)S(1)} %pad_add_fusion.places_ref, f32[768,24576]{1,0:T(8,128)} %h_ref.21, bf16[768,256]{1,0:T(8,128)(2,1)S(1)} %copy-done.1, ...), custom_call_target="tpu_custom_call", output_to_operand_aliasing={{0}: (5, {}), {1}: (6, {}), {2}: (7, {})} | custom-call | flops 1811939328 | bytes 7077888 | tf_op jit(solution)/shard_map/stage_product/pallas_call | solution.py:161
  64.3 4.7 %stage_product.13 = (f32[5,768,768]{2,1,0:T(8,128)S(1)}, f32[768,256]{1,0:T(8,128)S(1)}) custom-call(s32[33]{0:T(128)S(1)} %pad_add_fusion.places_ref, f32[768,24576]{1,0:T(8,128)} %h_ref.21, bf16[768,256]{1,0:T(8,128)(2,1)S(1)} %copy-done.3, bf16[768,256]{1,0:T(8,128)(2,1)S(1)} %copy-done.9, ...), custom_call_target="tpu_custom_call", output_to_operand_aliasing={{0}: (5, {}), {1}: (6, {})} | custom-call | flops 1811939328 | bytes 7077888 | tf_op jit(solution)/shard_map/stage_product/pallas_call | solution.py:161
  69.8 3.0 %stage_product.14 = (f32[5,768,768]{2,1,0:T(8,128)S(1)}, f32[768,256]{1,0:T(8,128)S(1)}, f32[256,256]{1,0:T(8,128)S(1)}) custom-call(s32[33]{0:T(128)S(1)} %pad_add_fusion.places_ref, f32[768,24576]{1,0:T(8,128)} %h_ref.21, bf16[768,256]{1,0:T(8,128)(2,1)S(1)} %collective-permute-done.20.rest_0_, ...), custom_call_target="tpu_custom_call", output_to_operand_aliasing={{0}: (4, {}), {1}: (5, {}), {2}: (6, {})} | custom-call | flops 1207959552 | bytes 4718592 | tf_op jit(solution)/shard_map/stage_product/pallas_call | solution.py:161
  72.8 4.6 %stage_product.15 = (f32[5,768,768]{2,1,0:T(8,128)S(1)}, f32[768,256]{1,0:T(8,128)S(1)}) custom-call(s32[33]{0:T(128)S(1)} %pad_add_fusion.places_ref, f32[768,24576]{1,0:T(8,128)} %h_ref.21, bf16[768,256]{1,0:T(8,128)(2,1)S(1)} %collective-permute-done.23.rest_0_, ...), custom_call_target="tpu_custom_call", output_to_operand_aliasing={{0}: (4, {}), {1}: (5, {})} | custom-call | flops 1207959552 | bytes 4718592 | tf_op jit(solution)/shard_map/stage_product/pallas_call | solution.py:161
  79.4 4.1 %stage_product.16 = (f32[5,768,768]{2,1,0:T(8,128)S(1)}, f32[768,256]{1,0:T(8,128)S(1)}, f32[256,256]{1,0:T(8,128)S(1)}) custom-call(s32[33]{0:T(128)S(1)} %pad_add_fusion.places_ref, f32[768,24576]{1,0:T(8,128)} %h_ref.21, bf16[768,256]{1,0:T(8,128)(2,1)S(1)} %collective-permute-done.rest_0_, ...), custom_call_target="tpu_custom_call", output_to_operand_aliasing={{0}: (5, {}), {1}: (6, {}), {2}: (7, {})} | custom-call | flops 1811939328 | bytes 7077888 | tf_op jit(solution)/shard_map/stage_product/pallas_call | solution.py:161
  84.3 7.1 %stage_product.17 = (f32[5,768,768]{2,1,0:T(8,128)S(1)}, f32[768,256]{1,0:T(8,128)S(1)}, f32[256,256]{1,0:T(8,128)S(1)}) custom-call(s32[33]{0:T(128)S(1)} %pad_add_fusion.places_ref, f32[768,24576]{1,0:T(8,128)} %h_ref.21, bf16[768,256]{1,0:T(8,128)(2,1)S(1)} %collective-permute-done.1.rest_0_, ...), custom_call_target="tpu_custom_call", output_to_operand_aliasing={{0}: (8, {}), {1}: (9, {}), {2}: (10, {})} | custom-call | flops 3623878656 | bytes 14155776 | tf_op jit(solution)/shard_map/stage_product/pallas_call | solution.py:161
  91.9 7.1 %stage_product.18 = (f32[5,768,768]{2,1,0:T(8,128)S(1)}, f32[768,256]{1,0:T(8,128)S(1)}, f32[256,256]{1,0:T(8,128)S(1)}) custom-call(s32[33]{0:T(128)S(1)} %pad_add_fusion.places_ref, f32[768,24576]{1,0:T(8,128)} %h_ref.21, bf16[768,256]{1,0:T(8,128)(2,1)S(1)} %collective-permute-done.2.rest_0_, ...), custom_call_target="tpu_custom_call", output_to_operand_aliasing={{0}: (8, {}), {1}: (9, {}), {2}: (10, {})} | custom-call | flops 3623878656 | bytes 14155776 | tf_op jit(solution)/shard_map/stage_product/pallas_call | solution.py:161
  99.0 4.0 %stage_product.19 = (f32[5,768,768]{2,1,0:T(8,128)S(1)}, f32[768,256]{1,0:T(8,128)S(1)}) custom-call(s32[33]{0:T(128)S(1)} %pad_add_fusion.places_ref, f32[768,24576]{1,0:T(8,128)} %h_ref.21, bf16[768,256]{1,0:T(8,128)(2,1)S(1)} %collective-permute-done.5.rest_0_, ...), custom_call_target="tpu_custom_call", output_to_operand_aliasing={{0}: (5, {}), {1}: (6, {})} | custom-call | flops 1811939328 | bytes 7077888 | tf_op jit(solution)/shard_map/stage_product/pallas_call | solution.py:161
  103.1 2.5 %stage_product.20 = (f32[5,768,768]{2,1,0:T(8,128)S(1)}, f32[768,256]{1,0:T(8,128)S(1)}, f32[256,256]{1,0:T(8,128)S(1)}) custom-call(s32[33]{0:T(128)S(1)} %pad_add_fusion.places_ref, f32[768,24576]{1,0:T(8,128)} %h_ref.21, bf16[768,256]{1,0:T(8,128)(2,1)S(1)} %collective-permute-done.3.rest_0_, ...), custom_call_target="tpu_custom_call", output_to_operand_aliasing={{0}: (3, {}), {1}: (4, {}), {2}: (5, {})} | custom-call | flops 603979776 | bytes 2359296 | tf_op jit(solution)/shard_map/stage_product/pallas_call | solution.py:161
  110.7 2.0 collective-permute-start.33
  114.8 2.9 %collective-permute-done.34 = f32[96,128]{1,0:T(8,128)S(1)} collective-permute-done((f32[96,128]{1,0:T(8,128)S(1)}, f32[96,128]{1,0:T(8,128)S(1)}, u32[]{:S(2)}, u32[]{:S(2)}) %collective-permute-start.34) | collective-permute-done | bytes 49184 | tf_op jit(solution)/shard_map/ppermute | solution.py:339
  117.7 2.1 collective-permute-start.35
  122.3 3.0 %collective-permute-done.36 = f32[96,128]{1,0:T(8,128)S(1)} collective-permute-done((f32[96,128]{1,0:T(8,128)S(1)}, f32[96,128]{1,0:T(8,128)S(1)}, u32[]{:S(2)}, u32[]{:S(2)}) %collective-permute-start.36) | collective-permute-done | bytes 49184 | tf_op jit(solution)/shard_map/ppermute | solution.py:339
  133.5 39.4 %inverse_factor.1.low_ref = f32[256,256]{1,0:T(8,128)S(1)} custom-call(f32[256,256]{1,0:T(8,128)S(1)} %get-tuple-element.61.near_ref, f32[256,256]{1,0:T(8,128)S(1)} %collective-permute-done.42.far_ref), custom_call_target="tpu_custom_call" | custom-call | flops 1006632960 | tf_op jit(solution)/shard_map/inverse_factor/pallas_call | solution.py:251
  172.9 41.7 %finish.1 = (f32[768,256]{1,0:T(8,128)}, f32[256,256]{1,0:T(8,128)}) custom-call(s32[33]{0:T(128)S(1)} %pad_add_fusion.places_ref, f32[768,256]{1,0:T(8,128)S(1)} %get-tuple-element.58.p_ref, f32[4,96,128]{2,1,0:T(8,128)S(1)} %pad_maximum_fusion.mine_ref, f32[4,96,128]{2,1,0:T(8,128)S(1)} %collective-permute-done.41.other_ref, ...), custom_call_target="tpu_custom_call" | custom-call | tf_op jit(solution)/shard_map/finish/pallas_call | solution.py:291
  (108 shorter events, 41.0 us)
Async XLA Ops:
  1.8 16.6 %collective-permute-start.19 = (bf16[768,256]{1,0:T(8,128)(2,1)S(1)}, bf16[768,256]{1,0:T(8,128)(2,1)S(1)}, u32[]{:S(2)}, u32[]{:S(2)}) collective-permute-start(bf16[768,256]{1,0:T(8,128)(2,1)S(1)} %convert_element_type.3.rest_0_.b_ref), channel_id=1, source_target_pairs={{0,8},{2,10},{4,12},{6,14},{8,0},{10,2},{12,4},{14,6},{16,24},{18,... | collective-permute-start | bytes 1179656 | tf_op jit(solution)/shard_map/ppermute | solution.py:339
  4.9 13.5 %collective-permute-start.16 = (bf16[768,256]{1,0:T(8,128)(2,1)S(1)}, bf16[768,256]{1,0:T(8,128)(2,1)}, u32[]{:S(2)}, u32[]{:S(2)}) collective-permute-start(bf16[768,256]{1,0:T(8,128)(2,1)S(1)} %convert_element_type.3.rest_0_.b_ref), channel_id=1, source_target_pairs={{0,4},{2,6},{4,0},{6,2},{8,12},{10,14},{12,8},{14,10},{16,20},{18,... | collective-permute-start | bytes 1179656 | tf_op jit(solution)/shard_map/ppermute | solution.py:339
  7.9 20.9 %collective-permute-start = (bf16[768,256]{1,0:T(8,128)(2,1)S(1)}, bf16[768,256]{1,0:T(8,128)(2,1)S(1)}, u32[]{:S(2)}, u32[]{:S(2)}) collective-permute-start(bf16[768,256]{1,0:T(8,128)(2,1)S(1)} %convert_element_type.3.rest_0_.b_ref), channel_id=1, source_target_pairs={{0,16},{2,18},{4,20},{6,22},{8,24},{10,26},{12,28},{14,30},{16,0},... | collective-permute-start | bytes 1179656 | tf_op jit(solution)/shard_map/ppermute | solution.py:339
  18.9 13.3 %collective-permute-start.28 = (bf16[768,256]{1,0:T(8,128)(2,1)S(1)}, bf16[768,256]{1,0:T(8,128)(2,1)S(1)}, u32[]{:S(2)}, u32[]{:S(2)}) collective-permute-start(bf16[768,256]{1,0:T(8,128)(2,1)S(1)} %collective-permute-done.27.rest_1_), channel_id=1, source_target_pairs={{0,1},{1,0},{2,3},{3,2},{4,5},{5,4},{6,7},{7,6},{8,9},{9,8},{10,11... | collective-permute-start | bytes 1179656 | tf_op jit(solution)/shard_map/ppermute | solution.py:342
  20.5 13.9 %collective-permute-start.20 = (bf16[768,256]{1,0:T(8,128)(2,1)S(1)}, bf16[768,256]{1,0:T(8,128)(2,1)S(1)}, u32[]{:S(2)}, u32[]{:S(2)}) collective-permute-start(bf16[768,256]{1,0:T(8,128)(2,1)S(1)} %collective-permute-done.19.rest_0_), channel_id=1, source_target_pairs={{0,2},{2,0},{4,6},{6,4},{8,10},{10,8},{12,14},{14,12},{16,18},{18,... | collective-permute-start | bytes 1179656 | tf_op jit(solution)/shard_map/ppermute | solution.py:339
  32.9 17.0 %collective-permute-start.6 = (bf16[768,256]{1,0:T(8,128)(2,1)S(1)}, bf16[768,256]{1,0:T(8,128)(2,1)S(1)}, u32[]{:S(2)}, u32[]{:S(2)}) collective-permute-start(bf16[768,256]{1,0:T(8,128)(2,1)S(1)} %collective-permute-done.rest_0_), channel_id=1, source_target_pairs={{0,2},{2,0},{4,6},{6,4},{8,10},{10,8},{12,14},{14,12},{16,18},{18,... | collective-permute-start | bytes 1179656 | tf_op jit(solution)/shard_map/ppermute | solution.py:339
  34.4 17.8 %collective-permute-start.9 = (bf16[768,256]{1,0:T(8,128)(2,1)S(1)}, bf16[768,256]{1,0:T(8,128)(2,1)S(1)}, u32[]{:S(2)}, u32[]{:S(2)}) collective-permute-start(bf16[768,256]{1,0:T(8,128)(2,1)S(1)} %collective-permute-done.rest_0_), channel_id=1, source_target_pairs={{0,4},{2,6},{4,0},{6,2},{8,12},{10,14},{12,8},{14,10},{16,20},{18,... | collective-permute-start | bytes 1179656 | tf_op jit(solution)/shard_map/ppermute | solution.py:339
  43.0 19.4 %collective-permute-start.23 = (bf16[768,256]{1,0:T(8,128)(2,1)S(1)}, bf16[768,256]{1,0:T(8,128)(2,1)S(1)}, u32[]{:S(2)}, u32[]{:S(2)}) collective-permute-start(bf16[768,256]{1,0:T(8,128)(2,1)S(1)} %collective-permute-done.20.rest_0_), channel_id=1, source_target_pairs={{0,1},{1,0},{2,3},{3,2},{4,5},{5,4},{6,7},{7,6},{8,9},{9,8},{10,11... | collective-permute-start | bytes 1179656 | tf_op jit(solution)/shard_map/ppermute | solution.py:342
  43.1 21.2 %collective-permute-start.25 = (bf16[768,256]{1,0:T(8,128)(2,1)S(1)}, bf16[768,256]{1,0:T(8,128)(2,1)S(1)}, u32[]{:S(2)}, u32[]{:S(2)}) collective-permute-start(bf16[768,256]{1,0:T(8,128)(2,1)S(1)} %collective-permute-done.24.rest_1_), channel_id=1, source_target_pairs={{0,1},{1,0},{2,3},{3,2},{4,5},{5,4},{6,7},{7,6},{8,9},{9,8},{10,11... | collective-permute-start | bytes 1179656 | tf_op jit(solution)/shard_map/ppermute | solution.py:342
  49.9 19.1 %collective-permute-start.21 = (bf16[768,256]{1,0:T(8,128)(2,1)S(1)}, bf16[768,256]{1,0:T(8,128)(2,1)S(1)}, u32[]{:S(2)}, u32[]{:S(2)}) collective-permute-start(bf16[768,256]{1,0:T(8,128)(2,1)S(1)} %collective-permute-done.20.rest_0_), channel_id=1, source_target_pairs={{0,4},{2,6},{4,0},{6,2},{8,12},{10,14},{12,8},{14,10},{16,20},{18,... | collective-permute-start | bytes 1179656 | tf_op jit(solution)/shard_map/ppermute | solution.py:339
  52.2 17.1 %collective-permute-start.18 = (bf16[768,256]{1,0:T(8,128)(2,1)S(1)}, bf16[768,256]{1,0:T(8,128)(2,1)S(1)}, u32[]{:S(2)}, u32[]{:S(2)}) collective-permute-start(bf16[768,256]{1,0:T(8,128)(2,1)S(1)} %collective-permute-done.17.rest_1_), channel_id=1, source_target_pairs={{0,1},{1,0},{2,3},{3,2},{4,5},{5,4},{6,7},{7,6},{8,9},{9,8},{10,11... | collective-permute-start | bytes 1179656 | tf_op jit(solution)/shard_map/ppermute | solution.py:342
  52.2 17.4 %collective-permute-start.2 = (bf16[768,256]{1,0:T(8,128)(2,1)S(1)}, bf16[768,256]{1,0:T(8,128)(2,1)S(1)}, u32[]{:S(2)}, u32[]{:S(2)}) collective-permute-start(bf16[768,256]{1,0:T(8,128)(2,1)S(1)} %collective-permute-done.1.rest_0_), channel_id=1, source_target_pairs={{0,4},{2,6},{4,0},{6,2},{8,12},{10,14},{12,8},{14,10},{16,20},{18,... | collective-permute-start | bytes 1179656 | tf_op jit(solution)/shard_map/ppermute | solution.py:339
  62.5 14.9 %collective-permute-start.10 = (bf16[768,256]{1,0:T(8,128)(2,1)S(1)}, bf16[768,256]{1,0:T(8,128)(2,1)S(1)}, u32[]{:S(2)}, u32[]{:S(2)}) collective-permute-start(bf16[768,256]{1,0:T(8,128)(2,1)S(1)} %collective-permute-done.9.rest_2_), channel_id=1, source_target_pairs={{0,2},{2,0},{4,6},{6,4},{8,10},{10,8},{12,14},{14,12},{16,18},{18,... | collective-permute-start | bytes 1179656 | tf_op jit(solution)/shard_map/ppermute | solution.py:339
  64.3 13.5 %collective-permute-start.7 = (bf16[768,256]{1,0:T(8,128)(2,1)S(1)}, bf16[768,256]{1,0:T(8,128)(2,1)S(1)}, u32[]{:S(2)}, u32[]{:S(2)}) collective-permute-start(bf16[768,256]{1,0:T(8,128)(2,1)S(1)} %collective-permute-done.6.rest_1_), channel_id=1, source_target_pairs={{0,8},{2,10},{4,12},{6,14},{8,0},{10,2},{12,4},{14,6},{16,24},{18,... | collective-permute-start | bytes 1179656 | tf_op jit(solution)/shard_map/ppermute | solution.py:339
  69.0 14.6 %collective-permute-start.12 = (bf16[768,256]{1,0:T(8,128)(2,1)S(1)}, bf16[768,256]{1,0:T(8,128)(2,1)S(1)}, u32[]{:S(2)}, u32[]{:S(2)}) collective-permute-start(bf16[768,256]{1,0:T(8,128)(2,1)S(1)} %collective-permute-done.1.rest_0_), channel_id=1, source_target_pairs={{0,1},{1,0},{2,3},{3,2},{4,5},{5,4},{6,7},{7,6},{8,9},{9,8},{10,11... | collective-permute-start | bytes 1179656 | tf_op jit(solution)/shard_map/ppermute | solution.py:342
  69.2 14.4 %collective-permute-start.13 = (bf16[768,256]{1,0:T(8,128)(2,1)S(1)}, bf16[768,256]{1,0:T(8,128)(2,1)S(1)}, u32[]{:S(2)}, u32[]{:S(2)}) collective-permute-start(bf16[768,256]{1,0:T(8,128)(2,1)S(1)} %collective-permute-done.6.rest_1_), channel_id=1, source_target_pairs={{0,1},{1,0},{2,3},{3,2},{4,5},{5,4},{6,7},{7,6},{8,9},{9,8},{10,11... | collective-permute-start | bytes 1179656 | tf_op jit(solution)/shard_map/ppermute | solution.py:342
  69.6 14.6 %collective-permute-start.22 = (bf16[768,256]{1,0:T(8,128)(2,1)S(1)}, bf16[768,256]{1,0:T(8,128)(2,1)S(1)}, u32[]{:S(2)}, u32[]{:S(2)}) collective-permute-start(bf16[768,256]{1,0:T(8,128)(2,1)S(1)} %collective-permute-done.21.rest_2_), channel_id=1, source_target_pairs={{0,1},{1,0},{2,3},{3,2},{4,5},{5,4},{6,7},{7,6},{8,9},{9,8},{10,11... | collective-permute-start | bytes 1179656 | tf_op jit(solution)/shard_map/ppermute | solution.py:342
  77.4 14.5 %collective-permute-start.14 = (bf16[768,256]{1,0:T(8,128)(2,1)S(1)}, bf16[768,256]{1,0:T(8,128)(2,1)S(1)}, u32[]{:S(2)}, u32[]{:S(2)}) collective-permute-start(bf16[768,256]{1,0:T(8,128)(2,1)S(1)} %collective-permute-done.9.rest_2_), channel_id=1, source_target_pairs={{0,1},{1,0},{2,3},{3,2},{4,5},{5,4},{6,7},{7,6},{8,9},{9,8},{10,11... | collective-permute-start | bytes 1179656 | tf_op jit(solution)/shard_map/ppermute | solution.py:342
  77.8 13.5 %collective-permute-start.3 = (bf16[768,256]{1,0:T(8,128)(2,1)S(1)}, bf16[768,256]{1,0:T(8,128)(2,1)S(1)}, u32[]{:S(2)}, u32[]{:S(2)}) collective-permute-start(bf16[768,256]{1,0:T(8,128)(2,1)S(1)} %collective-permute-done.2.rest_0_), channel_id=1, source_target_pairs={{0,2},{2,0},{4,6},{6,4},{8,10},{10,8},{12,14},{14,12},{16,18},{18,... | collective-permute-start | bytes 1179656 | tf_op jit(solution)/shard_map/ppermute | solution.py:339
  83.6 15.4 %collective-permute-start.5 = (bf16[768,256]{1,0:T(8,128)(2,1)S(1)}, bf16[768,256]{1,0:T(8,128)(2,1)S(1)}, u32[]{:S(2)}, u32[]{:S(2)}) collective-permute-start(bf16[768,256]{1,0:T(8,128)(2,1)S(1)} %collective-permute-done.2.rest_0_), channel_id=1, source_target_pairs={{0,1},{1,0},{2,3},{3,2},{4,5},{5,4},{6,7},{7,6},{8,9},{9,8},{10,11... | collective-permute-start | bytes 1179656 | tf_op jit(solution)/shard_map/ppermute | solution.py:342
  83.7 15.3 %collective-permute-start.11 = (bf16[768,256]{1,0:T(8,128)(2,1)S(1)}, bf16[768,256]{1,0:T(8,128)(2,1)S(1)}, u32[]{:S(2)}, u32[]{:S(2)}) collective-permute-start(bf16[768,256]{1,0:T(8,128)(2,1)S(1)} %collective-permute-done.10.rest_2_), channel_id=1, source_target_pairs={{0,1},{1,0},{2,3},{3,2},{4,5},{5,4},{6,7},{7,6},{8,9},{9,8},{10,11... | collective-permute-start | bytes 1179656 | tf_op jit(solution)/shard_map/ppermute | solution.py:342
  84.2 14.8 %collective-permute-start.8 = (bf16[768,256]{1,0:T(8,128)(2,1)S(1)}, bf16[768,256]{1,0:T(8,128)(2,1)S(1)}, u32[]{:S(2)}, u32[]{:S(2)}) collective-permute-start(bf16[768,256]{1,0:T(8,128)(2,1)S(1)} %collective-permute-done.7.rest_1_), channel_id=1, source_target_pairs={{0,1},{1,0},{2,3},{3,2},{4,5},{5,4},{6,7},{7,6},{8,9},{9,8},{10,11... | collective-permute-start | bytes 1179656 | tf_op jit(solution)/shard_map/ppermute | solution.py:342
  91.4 14.2 %collective-permute-start.4 = (bf16[768,256]{1,0:T(8,128)(2,1)S(1)}, bf16[768,256]{1,0:T(8,128)(2,1)S(1)}, u32[]{:S(2)}, u32[]{:S(2)}) collective-permute-start(bf16[768,256]{1,0:T(8,128)(2,1)S(1)} %collective-permute-done.3.rest_0_), channel_id=1, source_target_pairs={{0,1},{1,0},{2,3},{3,2},{4,5},{5,4},{6,7},{7,6},{8,9},{9,8},{10,11... | collective-permute-start | bytes 1179656 | tf_op jit(solution)/shard_map/ppermute | solution.py:342
  133.4 39.5 %collective-permute-start.41 = (f32[4,96,128]{2,1,0:T(8,128)S(1)}, f32[4,96,128]{2,1,0:T(8,128)S(1)}, u32[]{:S(2)}, u32[]{:S(2)}) collective-permute-start(f32[4,96,128]{2,1,0:T(8,128)S(1)} %pad_maximum_fusion.mine_ref), channel_id=1, source_target_pairs={{0,1},{1,0},{2,3},{3,2},{4,5},{5,4},{6,7},{7,6},{8,9},{9,8},{10,11... | collective-permute-start | bytes 589832 | tf_op jit(solution)/shard_map/ppermute | solution.py:342
  (31 other events, 195.2 us)

commit v5 on v4

--- a/solution.py
+++ b/solution.py
@@ -316,16 +316,13 @@
     ((15, 14, 1),),
 )
 TURNS = (
-    ((0,), (0,), 3, (4, 1, 2)),
+    ((0,), (0,), 2, (4, 1, 2)),
     ((4, 1, 2), (), 1, (5, 6, 8, 3)),
-    ((), (4, 1, 2), 2, (5, 6, 8, 3)),
-    ((5, 6), (), 1, (7, 8, 3)),
-    ((), (5, 6), 3, (7, 8, 3)),
-    ((8, 3, 7), (), 2, (12, 9, 10)),
+    ((5, 6), (4, 1, 2), 1, (7, 8, 3)),
+    ((8, 3, 7), (5, 6), 1, (12, 9, 10)),
     ((12, 9, 10), (8, 3, 7), 1, (14, 13, 11)),
     ((14, 13, 11), (12, 9, 10), 1, (15,)),
-    ((), (14, 13, 11), 1, (15,)),
-    ((15,), (), 1, ()),
+    ((15,), (14, 13, 11), 1, ()),
     ((), (15,), 0, ()),
 )
 

time: 215 us -> 207 us (0.963)
  Pallas kernels: 130 us -> 125 us
  waiting for transfers between devices: 39.2 us -> 34.5 us
  starting transfers between devices: 36.4 us -> 38.6 us
    pallas_call x11 -> x8, Pallas kernels: 47.9 us -> 42.1 us  [stage_call(): pl.pallas_call(body, name='stage_product', out_shape=(jax.ShapeDtypeStruc...]
    ppermute x24, waiting for transfers between devices: 37.8 us -> 33.1 us  [from_chip(): return lax.ppermute(a, 'rows', [(s, s ^ m) for s in range(chips)])]
    ppermute x24, starting transfers between devices: 32.8 us -> 35.1 us  [from_chip(): return lax.ppermute(a, 'rows', [(s, s ^ m) for s in range(chips)])]
  transfers between devices with their start and end apart: 43 -> 43, of which waited for: 15 -> 16; matrix products, arithmetic and copies ran while one was open for 0% -> 0% of each run, Pallas kernels for 40% -> 39%
where the time goes in v5:
time: 207 us; the launch traced here: 206 us
  Pallas kernels  125 us (60%)
  starting transfers between devices  38.6 us (19%)
  waiting for transfers between devices  34.5 us (17%)
  local copies, waits for them, and re-layouts  5.56 us (3%)
    pallas_call x8, Pallas kernels, stage_call(): pl.pallas_call(body, name='stage_product', out_shape=(jax.ShapeDtypeStruc...  42.1 us
    pallas_call x1, Pallas kernels, finish_call(): pl.pallas_call(body, name='finish', out_shape=(jax.ShapeDtypeStruct((rows...  41.7 us
    pallas_call x1, Pallas kernels, inverse_call(): pl.pallas_call(body, name='inverse_factor', out_shape=jax.ShapeDtypeStruc...  39.4 us
    ppermute x24, starting transfers between devices, from_chip(): return lax.ppermute(a, 'rows', [(s, s ^ m) for s in range(chips)])  35.1 us
    ppermute x24, waiting for transfers between devices, from_chip(): return lax.ppermute(a, 'rows', [(s, s ^ m) for s in range(chips)])  33.1 us
    unnamed x24, local copies, waits for them, and re-layouts  5.55 us
  transfers between devices with their start and end apart: 43, of which 16 were waited for; matrix products, arithmetic and copies ran while one was open for 0% of the time, Pallas kernels for 39%

profile of v5, /device:TPU:0, one launch (start us, length us, event | category | flops | bytes accessed | tf_op | source)
XLA Modules:
  0.0 206.4 jit_solution(18007936011237800167)
XLA Ops:
  1.8 3.1 %collective-permute-start.19 = (bf16[768,256]{1,0:T(8,128)(2,1)S(1)}, bf16[768,256]{1,0:T(8,128)(2,1)S(1)}, u32[]{:S(2)}, u32[]{:S(2)}) collective-permute-start(bf16[768,256]{1,0:T(8,128)(2,1)S(1)} %convert_element_type.3.rest_0_.b_ref), channel_id=1, source_target_pairs={{0,8},{2,10},{4,12},{6,14},{8,0},{10,2},{12,4},{14,6},{16,24},{18,... | collective-permute-start | bytes 1179656 | tf_op jit(solution)/shard_map/ppermute | solution.py:336
  7.9 2.6 %collective-permute-start = (bf16[768,256]{1,0:T(8,128)(2,1)S(1)}, bf16[768,256]{1,0:T(8,128)(2,1)S(1)}, u32[]{:S(2)}, u32[]{:S(2)}) collective-permute-start(bf16[768,256]{1,0:T(8,128)(2,1)S(1)} %convert_element_type.3.rest_0_.b_ref), channel_id=1, source_target_pairs={{0,16},{2,18},{4,20},{6,22},{8,24},{10,26},{12,28},{14,30},{16,0},... | collective-permute-start | bytes 1179656 | tf_op jit(solution)/shard_map/ppermute | solution.py:336
  10.5 8.4 %collective-permute-done.19.rest_0_ = bf16[768,256]{1,0:T(8,128)(2,1)S(1)} collective-permute-done((bf16[768,256]{1,0:T(8,128)(2,1)S(1)}, bf16[768,256]{1,0:T(8,128)(2,1)S(1)}, u32[]{:S(2)}, u32[]{:S(2)}) %collective-permute-start.19) | collective-permute-done | bytes 393248 | tf_op jit(solution)/shard_map/ppermute | solution.py:336
  18.9 2.6 %collective-permute-start.20 = (bf16[768,256]{1,0:T(8,128)(2,1)S(1)}, bf16[768,256]{1,0:T(8,128)(2,1)S(1)}, u32[]{:S(2)}, u32[]{:S(2)}) collective-permute-start(bf16[768,256]{1,0:T(8,128)(2,1)S(1)} %collective-permute-done.19.rest_0_), channel_id=1, source_target_pairs={{0,2},{2,0},{4,6},{6,4},{8,10},{10,8},{12,14},{14,12},{16,18},{18,... | collective-permute-start | bytes 1179656 | tf_op jit(solution)/shard_map/ppermute | solution.py:336
  22.3 2.5 %collective-permute-start.24 = (bf16[768,256]{1,0:T(8,128)(2,1)S(1)}, bf16[768,256]{1,0:T(8,128)(2,1)S(1)}, u32[]{:S(2)}, u32[]{:S(2)}) collective-permute-start(bf16[768,256]{1,0:T(8,128)(2,1)S(1)} %collective-permute-done.19.rest_0_), channel_id=1, source_target_pairs={{0,4},{2,6},{4,0},{6,2},{8,12},{10,14},{12,8},{14,10},{16,20},{18,... | collective-permute-start | bytes 1179656 | tf_op jit(solution)/shard_map/ppermute | solution.py:336
  26.1 2.1 %collective-permute-done.rest_0_ = bf16[768,256]{1,0:T(8,128)(2,1)S(1)} collective-permute-done((bf16[768,256]{1,0:T(8,128)(2,1)S(1)}, bf16[768,256]{1,0:T(8,128)(2,1)S(1)}, u32[]{:S(2)}, u32[]{:S(2)}) %collective-permute-start) | collective-permute-done | bytes 393248 | tf_op jit(solution)/shard_map/ppermute | solution.py:336
  34.6 1.7 collective-permute-start.9
  37.1 4.9 %collective-permute-done.17.rest_1_ = bf16[768,256]{1,0:T(8,128)(2,1)S(1)} collective-permute-done((bf16[768,256]{1,0:T(8,128)(2,1)}, bf16[768,256]{1,0:T(8,128)(2,1)S(1)}, u32[]{:S(2)}, u32[]{:S(2)}) %collective-permute-start.17) | collective-permute-done | bytes 393248 | tf_op jit(solution)/shard_map/ppermute | solution.py:336
  42.0 2.5 %collective-permute-start.21 = (bf16[768,256]{1,0:T(8,128)(2,1)S(1)}, bf16[768,256]{1,0:T(8,128)(2,1)S(1)}, u32[]{:S(2)}, u32[]{:S(2)}) collective-permute-start(bf16[768,256]{1,0:T(8,128)(2,1)S(1)} %collective-permute-done.20.rest_0_), channel_id=1, source_target_pairs={{0,4},{2,6},{4,0},{6,2},{8,12},{10,14},{12,8},{14,10},{16,20},{18,... | collective-permute-start | bytes 1179656 | tf_op jit(solution)/shard_map/ppermute | solution.py:336
  45.2 4.0 %collective-permute-done.6.rest_1_ = bf16[768,256]{1,0:T(8,128)(2,1)S(1)} collective-permute-done((bf16[768,256]{1,0:T(8,128)(2,1)S(1)}, bf16[768,256]{1,0:T(8,128)(2,1)S(1)}, u32[]{:S(2)}, u32[]{:S(2)}) %collective-permute-start.6) | collective-permute-done | bytes 393248 | tf_op jit(solution)/shard_map/ppermute | solution.py:336
  52.0 5.1 %stage_product.8 = (f32[5,768,768]{2,1,0:T(8,128)S(1)}, f32[768,256]{1,0:T(8,128)S(1)}, f32[256,256]{1,0:T(8,128)S(1)}) custom-call(s32[33]{0:T(128)S(1)} %pad_add_fusion.places_ref, f32[768,24576]{1,0:T(8,128)} %h_ref.15, bf16[768,256]{1,0:T(8,128)(2,1)S(1)} %convert_element_type.3.rest_0_.b_ref, bf16[768,256]{1,0:T(8,128)(2,1)S(1)} %copy-done.11), custom_call_target="tpu_custom_call" | custom-call | flops 1207959552 | bytes 4718592 | tf_op jit(solution)/shard_map/stage_product/pallas_call | solution.py:161
  58.7 4.0 %stage_product.9 = (f32[5,768,768]{2,1,0:T(8,128)S(1)}, f32[768,256]{1,0:T(8,128)S(1)}, f32[256,256]{1,0:T(8,128)S(1)}) custom-call(s32[33]{0:T(128)S(1)} %pad_add_fusion.places_ref, f32[768,24576]{1,0:T(8,128)} %h_ref.15, bf16[768,256]{1,0:T(8,128)(2,1)S(1)} %copy-done.1, ...), custom_call_target="tpu_custom_call", output_to_operand_aliasing={{0}: (5, {}), {1}: (6, {}), {2}: (7, {})} | custom-call | flops 1811939328 | bytes 7077888 | tf_op jit(solution)/shard_map/stage_product/pallas_call | solution.py:161
  63.4 6.0 %stage_product.10 = (f32[5,768,768]{2,1,0:T(8,128)S(1)}, f32[768,256]{1,0:T(8,128)S(1)}, f32[256,256]{1,0:T(8,128)S(1)}) custom-call(s32[33]{0:T(128)S(1)} %pad_add_fusion.places_ref, f32[768,24576]{1,0:T(8,128)} %h_ref.15, bf16[768,256]{1,0:T(8,128)(2,1)S(1)} %collective-permute-done.20.rest_0_, ...), custom_call_target="tpu_custom_call", output_to_operand_aliasing={{0}: (7, {}), {1}: (8, {}), {2}: (9, {})} | custom-call | flops 3019898880 | bytes 11796480 | tf_op jit(solution)/shard_map/stage_product/pallas_call | solution.py:161
  70.5 6.1 %stage_product.11 = (f32[5,768,768]{2,1,0:T(8,128)S(1)}, f32[768,256]{1,0:T(8,128)S(1)}, f32[256,256]{1,0:T(8,128)S(1)}) custom-call(s32[33]{0:T(128)S(1)} %pad_add_fusion.places_ref, f32[768,24576]{1,0:T(8,128)} %h_ref.15, bf16[768,256]{1,0:T(8,128)(2,1)S(1)} %collective-permute-done.rest_0_, ...), custom_call_target="tpu_custom_call", output_to_operand_aliasing={{0}: (7, {}), {1}: (8, {}), {2}: (9, {})} | custom-call | flops 3019898880 | bytes 11796480 | tf_op jit(solution)/shard_map/stage_product/pallas_call | solution.py:161
  77.3 7.1 %stage_product.12 = (f32[5,768,768]{2,1,0:T(8,128)S(1)}, f32[768,256]{1,0:T(8,128)S(1)}, f32[256,256]{1,0:T(8,128)S(1)}) custom-call(s32[33]{0:T(128)S(1)} %pad_add_fusion.places_ref, f32[768,24576]{1,0:T(8,128)} %h_ref.15, bf16[768,256]{1,0:T(8,128)(2,1)S(1)} %collective-permute-done.1.rest_0_, ...), custom_call_target="tpu_custom_call", output_to_operand_aliasing={{0}: (8, {}), {1}: (9, {}), {2}: (10, {})} | custom-call | flops 3623878656 | bytes 14155776 | tf_op jit(solution)/shard_map/stage_product/pallas_call | solution.py:161
  84.9 7.1 %stage_product.13 = (f32[5,768,768]{2,1,0:T(8,128)S(1)}, f32[768,256]{1,0:T(8,128)S(1)}, f32[256,256]{1,0:T(8,128)S(1)}) custom-call(s32[33]{0:T(128)S(1)} %pad_add_fusion.places_ref, f32[768,24576]{1,0:T(8,128)} %h_ref.15, bf16[768,256]{1,0:T(8,128)(2,1)S(1)} %collective-permute-done.2.rest_0_, ...), custom_call_target="tpu_custom_call", output_to_operand_aliasing={{0}: (8, {}), {1}: (9, {}), {2}: (10, {})} | custom-call | flops 3623878656 | bytes 14155776 | tf_op jit(solution)/shard_map/stage_product/pallas_call | solution.py:161
  92.0 5.0 %stage_product.14 = (f32[5,768,768]{2,1,0:T(8,128)S(1)}, f32[768,256]{1,0:T(8,128)S(1)}, f32[256,256]{1,0:T(8,128)S(1)}) custom-call(s32[33]{0:T(128)S(1)} %pad_add_fusion.places_ref, f32[768,24576]{1,0:T(8,128)} %h_ref.15, bf16[768,256]{1,0:T(8,128)(2,1)S(1)} %collective-permute-done.3.rest_0_, ...), custom_call_target="tpu_custom_call", output_to_operand_aliasing={{0}: (6, {}), {1}: (7, {}), {2}: (8, {})} | custom-call | flops 2415919104 | bytes 9437184 | tf_op jit(solution)/shard_map/stage_product/pallas_call | solution.py:161
  103.3 2.0 collective-permute-start.34
  105.9 1.8 collective-permute-done.33
  108.3 2.1 collective-permute-start.35
  112.9 3.2 %collective-permute-done.36 = f32[96,128]{1,0:T(8,128)S(1)} collective-permute-done((f32[96,128]{1,0:T(8,128)S(1)}, f32[96,128]{1,0:T(8,128)S(1)}, u32[]{:S(2)}, u32[]{:S(2)}) %collective-permute-start.36) | collective-permute-done | bytes 49184 | tf_op jit(solution)/shard_map/ppermute | solution.py:336
  123.0 2.1 %collective-permute-done.40 = f32[96,128]{1,0:T(8,128)S(1)} collective-permute-done((f32[96,128]{1,0:T(8,128)S(1)}, f32[96,128]{1,0:T(8,128)S(1)}, u32[]{:S(2)}, u32[]{:S(2)}) %collective-permute-start.40) | collective-permute-done | bytes 49184 | tf_op jit(solution)/shard_map/ppermute | solution.py:336
  125.2 39.4 %inverse_factor.1.low_ref = f32[256,256]{1,0:T(8,128)S(1)} custom-call(f32[256,256]{1,0:T(8,128)S(1)} %get-tuple-element.49.near_ref, f32[256,256]{1,0:T(8,128)S(1)} %collective-permute-done.42.far_ref), custom_call_target="tpu_custom_call" | custom-call | flops 1006632960 | tf_op jit(solution)/shard_map/inverse_factor/pallas_call | solution.py:251
  164.6 41.7 %finish.1 = (f32[768,256]{1,0:T(8,128)}, f32[256,256]{1,0:T(8,128)}) custom-call(s32[33]{0:T(128)S(1)} %pad_add_fusion.places_ref, f32[768,256]{1,0:T(8,128)S(1)} %get-tuple-element.46.p_ref, f32[4,96,128]{2,1,0:T(8,128)S(1)} %pad_maximum_fusion.mine_ref, f32[4,96,128]{2,1,0:T(8,128)S(1)} %collective-permute-done.41.other_ref, ...), custom_call_target="tpu_custom_call" | custom-call | tf_op jit(solution)/shard_map/finish/pallas_call | solution.py:291
  (105 shorter events, 38.1 us)
Async XLA Ops:
  1.8 17.1 %collective-permute-start.19 = (bf16[768,256]{1,0:T(8,128)(2,1)S(1)}, bf16[768,256]{1,0:T(8,128)(2,1)S(1)}, u32[]{:S(2)}, u32[]{:S(2)}) collective-permute-start(bf16[768,256]{1,0:T(8,128)(2,1)S(1)} %convert_element_type.3.rest_0_.b_ref), channel_id=1, source_target_pairs={{0,8},{2,10},{4,12},{6,14},{8,0},{10,2},{12,4},{14,6},{16,24},{18,... | collective-permute-start | bytes 1179656 | tf_op jit(solution)/shard_map/ppermute | solution.py:336
  4.9 16.6 %collective-permute-start.30 = (bf16[768,256]{1,0:T(8,128)(2,1)S(1)}, bf16[768,256]{1,0:T(8,128)(2,1)S(1)}, u32[]{:S(2)}, u32[]{:S(2)}) collective-permute-start(bf16[768,256]{1,0:T(8,128)(2,1)S(1)} %convert_element_type.3.rest_0_.b_ref), channel_id=1, source_target_pairs={{0,1},{1,0},{2,3},{3,2},{4,5},{5,4},{6,7},{7,6},{8,9},{9,8},{10,11... | collective-permute-start | bytes 1179656 | tf_op jit(solution)/shard_map/ppermute | solution.py:339
  4.9 19.9 %collective-permute-start.16 = (bf16[768,256]{1,0:T(8,128)(2,1)S(1)}, bf16[768,256]{1,0:T(8,128)(2,1)}, u32[]{:S(2)}, u32[]{:S(2)}) collective-permute-start(bf16[768,256]{1,0:T(8,128)(2,1)S(1)} %convert_element_type.3.rest_0_.b_ref), channel_id=1, source_target_pairs={{0,4},{2,6},{4,0},{6,2},{8,12},{10,14},{12,8},{14,10},{16,20},{18,... | collective-permute-start | bytes 1179656 | tf_op jit(solution)/shard_map/ppermute | solution.py:336
  6.4 19.2 %collective-permute-start.27 = (bf16[768,256]{1,0:T(8,128)(2,1)S(1)}, bf16[768,256]{1,0:T(8,128)(2,1)S(1)}, u32[]{:S(2)}, u32[]{:S(2)}) collective-permute-start(bf16[768,256]{1,0:T(8,128)(2,1)S(1)} %convert_element_type.3.rest_0_.b_ref), channel_id=1, source_target_pairs={{0,2},{2,0},{4,6},{6,4},{8,10},{10,8},{12,14},{14,12},{16,18},{18,... | collective-permute-start | bytes 1179656 | tf_op jit(solution)/shard_map/ppermute | solution.py:336
  7.9 20.3 %collective-permute-start = (bf16[768,256]{1,0:T(8,128)(2,1)S(1)}, bf16[768,256]{1,0:T(8,128)(2,1)S(1)}, u32[]{:S(2)}, u32[]{:S(2)}) collective-permute-start(bf16[768,256]{1,0:T(8,128)(2,1)S(1)} %convert_element_type.3.rest_0_.b_ref), channel_id=1, source_target_pairs={{0,16},{2,18},{4,20},{6,22},{8,24},{10,26},{12,28},{14,30},{16,0},... | collective-permute-start | bytes 1179656 | tf_op jit(solution)/shard_map/ppermute | solution.py:336
  33.6 15.6 %collective-permute-start.6 = (bf16[768,256]{1,0:T(8,128)(2,1)S(1)}, bf16[768,256]{1,0:T(8,128)(2,1)S(1)}, u32[]{:S(2)}, u32[]{:S(2)}) collective-permute-start(bf16[768,256]{1,0:T(8,128)(2,1)S(1)} %collective-permute-done.rest_0_), channel_id=1, source_target_pairs={{0,2},{2,0},{4,6},{6,4},{8,10},{10,8},{12,14},{14,12},{16,18},{18,... | collective-permute-start | bytes 1179656 | tf_op jit(solution)/shard_map/ppermute | solution.py:336
  34.6 14.6 %collective-permute-start.9 = (bf16[768,256]{1,0:T(8,128)(2,1)S(1)}, bf16[768,256]{1,0:T(8,128)(2,1)S(1)}, u32[]{:S(2)}, u32[]{:S(2)}) collective-permute-start(bf16[768,256]{1,0:T(8,128)(2,1)S(1)} %collective-permute-done.rest_0_), channel_id=1, source_target_pairs={{0,4},{2,6},{4,0},{6,2},{8,12},{10,14},{12,8},{14,10},{16,20},{18,... | collective-permute-start | bytes 1179656 | tf_op jit(solution)/shard_map/ppermute | solution.py:336
  37.1 12.6 %collective-permute-start.15 = (bf16[768,256]{1,0:T(8,128)(2,1)S(1)}, bf16[768,256]{1,0:T(8,128)(2,1)S(1)}, u32[]{:S(2)}, u32[]{:S(2)}) collective-permute-start(bf16[768,256]{1,0:T(8,128)(2,1)S(1)} %collective-permute-done.rest_0_), channel_id=1, source_target_pairs={{0,1},{1,0},{2,3},{3,2},{4,5},{5,4},{6,7},{7,6},{8,9},{9,8},{10,11... | collective-permute-start | bytes 1179656 | tf_op jit(solution)/shard_map/ppermute | solution.py:339
  42.0 15.1 %collective-permute-start.21 = (bf16[768,256]{1,0:T(8,128)(2,1)S(1)}, bf16[768,256]{1,0:T(8,128)(2,1)S(1)}, u32[]{:S(2)}, u32[]{:S(2)}) collective-permute-start(bf16[768,256]{1,0:T(8,128)(2,1)S(1)} %collective-permute-done.20.rest_0_), channel_id=1, source_target_pairs={{0,4},{2,6},{4,0},{6,2},{8,12},{10,14},{12,8},{14,10},{16,20},{18,... | collective-permute-start | bytes 1179656 | tf_op jit(solution)/shard_map/ppermute | solution.py:336
  44.5 14.1 %collective-permute-start.23 = (bf16[768,256]{1,0:T(8,128)(2,1)S(1)}, bf16[768,256]{1,0:T(8,128)(2,1)S(1)}, u32[]{:S(2)}, u32[]{:S(2)}) collective-permute-start(bf16[768,256]{1,0:T(8,128)(2,1)S(1)} %collective-permute-done.20.rest_0_), channel_id=1, source_target_pairs={{0,1},{1,0},{2,3},{3,2},{4,5},{5,4},{6,7},{7,6},{8,9},{9,8},{10,11... | collective-permute-start | bytes 1179656 | tf_op jit(solution)/shard_map/ppermute | solution.py:339
  49.2 13.5 %collective-permute-start.25 = (bf16[768,256]{1,0:T(8,128)(2,1)S(1)}, bf16[768,256]{1,0:T(8,128)(2,1)S(1)}, u32[]{:S(2)}, u32[]{:S(2)}) collective-permute-start(bf16[768,256]{1,0:T(8,128)(2,1)S(1)} %collective-permute-done.24.rest_1_), channel_id=1, source_target_pairs={{0,1},{1,0},{2,3},{3,2},{4,5},{5,4},{6,7},{7,6},{8,9},{9,8},{10,11... | collective-permute-start | bytes 1179656 | tf_op jit(solution)/shard_map/ppermute | solution.py:339
  49.2 13.6 %collective-permute-start.18 = (bf16[768,256]{1,0:T(8,128)(2,1)S(1)}, bf16[768,256]{1,0:T(8,128)(2,1)S(1)}, u32[]{:S(2)}, u32[]{:S(2)}) collective-permute-start(bf16[768,256]{1,0:T(8,128)(2,1)S(1)} %collective-permute-done.17.rest_1_), channel_id=1, source_target_pairs={{0,1},{1,0},{2,3},{3,2},{4,5},{5,4},{6,7},{7,6},{8,9},{9,8},{10,11... | collective-permute-start | bytes 1179656 | tf_op jit(solution)/shard_map/ppermute | solution.py:339
  49.7 13.6 %collective-permute-start.2 = (bf16[768,256]{1,0:T(8,128)(2,1)S(1)}, bf16[768,256]{1,0:T(8,128)(2,1)S(1)}, u32[]{:S(2)}, u32[]{:S(2)}) collective-permute-start(bf16[768,256]{1,0:T(8,128)(2,1)S(1)} %collective-permute-done.1.rest_0_), channel_id=1, source_target_pairs={{0,4},{2,6},{4,0},{6,2},{8,12},{10,14},{12,8},{14,10},{16,20},{18,... | collective-permute-start | bytes 1179656 | tf_op jit(solution)/shard_map/ppermute | solution.py:336
  57.2 12.2 %collective-permute-start.10 = (bf16[768,256]{1,0:T(8,128)(2,1)S(1)}, bf16[768,256]{1,0:T(8,128)(2,1)S(1)}, u32[]{:S(2)}, u32[]{:S(2)}) collective-permute-start(bf16[768,256]{1,0:T(8,128)(2,1)S(1)} %collective-permute-done.9.rest_2_), channel_id=1, source_target_pairs={{0,2},{2,0},{4,6},{6,4},{8,10},{10,8},{12,14},{14,12},{16,18},{18,... | collective-permute-start | bytes 1179656 | tf_op jit(solution)/shard_map/ppermute | solution.py:336
  62.7 13.9 %collective-permute-start.12 = (bf16[768,256]{1,0:T(8,128)(2,1)S(1)}, bf16[768,256]{1,0:T(8,128)(2,1)S(1)}, u32[]{:S(2)}, u32[]{:S(2)}) collective-permute-start(bf16[768,256]{1,0:T(8,128)(2,1)S(1)} %collective-permute-done.1.rest_0_), channel_id=1, source_target_pairs={{0,1},{1,0},{2,3},{3,2},{4,5},{5,4},{6,7},{7,6},{8,9},{9,8},{10,11... | collective-permute-start | bytes 1179656 | tf_op jit(solution)/shard_map/ppermute | solution.py:339
  62.8 13.9 %collective-permute-start.13 = (bf16[768,256]{1,0:T(8,128)(2,1)S(1)}, bf16[768,256]{1,0:T(8,128)(2,1)S(1)}, u32[]{:S(2)}, u32[]{:S(2)}) collective-permute-start(bf16[768,256]{1,0:T(8,128)(2,1)S(1)} %collective-permute-done.6.rest_1_), channel_id=1, source_target_pairs={{0,1},{1,0},{2,3},{3,2},{4,5},{5,4},{6,7},{7,6},{8,9},{9,8},{10,11... | collective-permute-start | bytes 1179656 | tf_op jit(solution)/shard_map/ppermute | solution.py:339
  63.3 13.9 %collective-permute-start.22 = (bf16[768,256]{1,0:T(8,128)(2,1)S(1)}, bf16[768,256]{1,0:T(8,128)(2,1)S(1)}, u32[]{:S(2)}, u32[]{:S(2)}) collective-permute-start(bf16[768,256]{1,0:T(8,128)(2,1)S(1)} %collective-permute-done.21.rest_2_), channel_id=1, source_target_pairs={{0,1},{1,0},{2,3},{3,2},{4,5},{5,4},{6,7},{7,6},{8,9},{9,8},{10,11... | collective-permute-start | bytes 1179656 | tf_op jit(solution)/shard_map/ppermute | solution.py:339
  69.4 15.5 %collective-permute-start.14 = (bf16[768,256]{1,0:T(8,128)(2,1)S(1)}, bf16[768,256]{1,0:T(8,128)(2,1)S(1)}, u32[]{:S(2)}, u32[]{:S(2)}) collective-permute-start(bf16[768,256]{1,0:T(8,128)(2,1)S(1)} %collective-permute-done.9.rest_2_), channel_id=1, source_target_pairs={{0,1},{1,0},{2,3},{3,2},{4,5},{5,4},{6,7},{7,6},{8,9},{9,8},{10,11... | collective-permute-start | bytes 1179656 | tf_op jit(solution)/shard_map/ppermute | solution.py:339
  69.9 14.5 %collective-permute-start.3 = (bf16[768,256]{1,0:T(8,128)(2,1)S(1)}, bf16[768,256]{1,0:T(8,128)(2,1)S(1)}, u32[]{:S(2)}, u32[]{:S(2)}) collective-permute-start(bf16[768,256]{1,0:T(8,128)(2,1)S(1)} %collective-permute-done.2.rest_0_), channel_id=1, source_target_pairs={{0,2},{2,0},{4,6},{6,4},{8,10},{10,8},{12,14},{14,12},{16,18},{18,... | collective-permute-start | bytes 1179656 | tf_op jit(solution)/shard_map/ppermute | solution.py:336
  76.6 15.4 %collective-permute-start.5 = (bf16[768,256]{1,0:T(8,128)(2,1)S(1)}, bf16[768,256]{1,0:T(8,128)(2,1)S(1)}, u32[]{:S(2)}, u32[]{:S(2)}) collective-permute-start(bf16[768,256]{1,0:T(8,128)(2,1)S(1)} %collective-permute-done.2.rest_0_), channel_id=1, source_target_pairs={{0,1},{1,0},{2,3},{3,2},{4,5},{5,4},{6,7},{7,6},{8,9},{9,8},{10,11... | collective-permute-start | bytes 1179656 | tf_op jit(solution)/shard_map/ppermute | solution.py:339
  76.7 15.3 %collective-permute-start.11 = (bf16[768,256]{1,0:T(8,128)(2,1)S(1)}, bf16[768,256]{1,0:T(8,128)(2,1)S(1)}, u32[]{:S(2)}, u32[]{:S(2)}) collective-permute-start(bf16[768,256]{1,0:T(8,128)(2,1)S(1)} %collective-permute-done.10.rest_2_), channel_id=1, source_target_pairs={{0,1},{1,0},{2,3},{3,2},{4,5},{5,4},{6,7},{7,6},{8,9},{9,8},{10,11... | collective-permute-start | bytes 1179656 | tf_op jit(solution)/shard_map/ppermute | solution.py:339
  77.2 14.8 %collective-permute-start.8 = (bf16[768,256]{1,0:T(8,128)(2,1)S(1)}, bf16[768,256]{1,0:T(8,128)(2,1)S(1)}, u32[]{:S(2)}, u32[]{:S(2)}) collective-permute-start(bf16[768,256]{1,0:T(8,128)(2,1)S(1)} %collective-permute-done.7.rest_1_), channel_id=1, source_target_pairs={{0,1},{1,0},{2,3},{3,2},{4,5},{5,4},{6,7},{7,6},{8,9},{9,8},{10,11... | collective-permute-start | bytes 1179656 | tf_op jit(solution)/shard_map/ppermute | solution.py:339
  84.4 12.7 %collective-permute-start.4 = (bf16[768,256]{1,0:T(8,128)(2,1)S(1)}, bf16[768,256]{1,0:T(8,128)(2,1)S(1)}, u32[]{:S(2)}, u32[]{:S(2)}) collective-permute-start(bf16[768,256]{1,0:T(8,128)(2,1)S(1)} %collective-permute-done.3.rest_0_), channel_id=1, source_target_pairs={{0,1},{1,0},{2,3},{3,2},{4,5},{5,4},{6,7},{7,6},{8,9},{9,8},{10,11... | collective-permute-start | bytes 1179656 | tf_op jit(solution)/shard_map/ppermute | solution.py:339
  125.1 39.5 %collective-permute-start.41 = (f32[4,96,128]{2,1,0:T(8,128)S(1)}, f32[4,96,128]{2,1,0:T(8,128)S(1)}, u32[]{:S(2)}, u32[]{:S(2)}) collective-permute-start(f32[4,96,128]{2,1,0:T(8,128)S(1)} %pad_maximum_fusion.mine_ref), channel_id=1, source_target_pairs={{0,1},{1,0},{2,3},{3,2},{4,5},{5,4},{6,7},{7,6},{8,9},{9,8},{10,11... | collective-permute-start | bytes 589832 | tf_op jit(solution)/shard_map/ppermute | solution.py:339
  (31 other events, 162.6 us)

commit v6 on v5

--- a/solution.py
+++ b/solution.py
@@ -85,7 +85,7 @@
     )(places, product, basis)
 
 
-BUFFERS = 5
+BUFFERS = 6
 
 
 def stage_call(hamiltonian, units, near, places, offset, ready, ahead, acc):
@@ -365,9 +365,18 @@
     product = acc[1]
     keep, send = cut_call(product, basis, places)
     a = keep + from_core(send)
-    b = a[0] + from_chip(a[1], 1) + from_chip(a[2], 2) + from_chip(a[3], 3)
-    b = b + from_chip(b, 4) + from_chip(b, 8) + from_chip(b, 12)
-    mine4 = jnp.stack([b, from_chip(b, 1), from_chip(b, 2), from_chip(b, 3)])
+
+    def from_three(arrays, steps):
+        got = {}
+        for a, step in zip(arrays, steps):
+            got[step] = from_chip(a, step)
+        return [got[step] for step in sorted(steps)]
+
+    x, y, xy = from_three((a[3], a[2], a[1]), (3, 2, 1))
+    b = a[0] + x + y + xy
+    z = from_three((b, b, b), (12, 8, 4))
+    b = b + z[0] + z[1] + z[2]
+    mine4 = jnp.stack([b, *from_three((b, b, b), (3, 2, 1))])
     other4 = from_core(mine4)
     low = inverse_call(correlation, correlation_far)
     return finish_call(product, mine4, other4, low, places, float(hamiltonian.shape[1]) ** 0.5)

time: 207 us -> 207 us (level)
  no operation moved by 1% of the time
where the time goes in v6:
time: 207 us; the launch traced here: 206 us
  Pallas kernels  125 us (60%)
  starting transfers between devices  38.6 us (19%)
  waiting for transfers between devices  34.5 us (17%)
  local copies, waits for them, and re-layouts  5.56 us (3%)
    pallas_call x8, Pallas kernels, stage_call(): pl.pallas_call(body, name='stage_product', out_shape=(jax.ShapeDtypeStruc...  42.2 us
    pallas_call x1, Pallas kernels, finish_call(): pl.pallas_call(body, name='finish', out_shape=(jax.ShapeDtypeStruct((rows...  41.7 us
    pallas_call x1, Pallas kernels, inverse_call(): pl.pallas_call(body, name='inverse_factor', out_shape=jax.ShapeDtypeStruc...  39.4 us
    ppermute x24, starting transfers between devices, from_chip(): return lax.ppermute(a, 'rows', [(s, s ^ m) for s in range(chips)])  35.1 us
    ppermute x24, waiting for transfers between devices, from_chip(): return lax.ppermute(a, 'rows', [(s, s ^ m) for s in range(chips)])  33.1 us
    unnamed x24, local copies, waits for them, and re-layouts  5.55 us
  transfers between devices with their start and end apart: 43, of which 16 were waited for; matrix products, arithmetic and copies ran while one was open for 0% of the time, Pallas kernels for 39%

profile of v6, /device:TPU:0, one launch (start us, length us, event | category | flops | bytes accessed | tf_op | source)
XLA Modules:
  0.0 206.5 jit_solution(4408534850654542657)
XLA Ops:
  1.8 3.1 %collective-permute-start.19 = (bf16[768,256]{1,0:T(8,128)(2,1)S(1)}, bf16[768,256]{1,0:T(8,128)(2,1)S(1)}, u32[]{:S(2)}, u32[]{:S(2)}) collective-permute-start(bf16[768,256]{1,0:T(8,128)(2,1)S(1)} %convert_element_type.3.rest_0_.b_ref), channel_id=1, source_target_pairs={{0,8},{2,10},{4,12},{6,14},{8,0},{10,2},{12,4},{14,6},{16,24},{18,... | collective-permute-start | bytes 1179656 | tf_op jit(solution)/shard_map/ppermute | solution.py:336
  7.9 2.6 %collective-permute-start = (bf16[768,256]{1,0:T(8,128)(2,1)S(1)}, bf16[768,256]{1,0:T(8,128)(2,1)S(1)}, u32[]{:S(2)}, u32[]{:S(2)}) collective-permute-start(bf16[768,256]{1,0:T(8,128)(2,1)S(1)} %convert_element_type.3.rest_0_.b_ref), channel_id=1, source_target_pairs={{0,16},{2,18},{4,20},{6,22},{8,24},{10,26},{12,28},{14,30},{16,0},... | collective-permute-start | bytes 1179656 | tf_op jit(solution)/shard_map/ppermute | solution.py:336
  10.5 8.4 %collective-permute-done.19.rest_0_ = bf16[768,256]{1,0:T(8,128)(2,1)S(1)} collective-permute-done((bf16[768,256]{1,0:T(8,128)(2,1)S(1)}, bf16[768,256]{1,0:T(8,128)(2,1)S(1)}, u32[]{:S(2)}, u32[]{:S(2)}) %collective-permute-start.19) | collective-permute-done | bytes 393248 | tf_op jit(solution)/shard_map/ppermute | solution.py:336
  18.9 2.6 %collective-permute-start.20 = (bf16[768,256]{1,0:T(8,128)(2,1)S(1)}, bf16[768,256]{1,0:T(8,128)(2,1)S(1)}, u32[]{:S(2)}, u32[]{:S(2)}) collective-permute-start(bf16[768,256]{1,0:T(8,128)(2,1)S(1)} %collective-permute-done.19.rest_0_), channel_id=1, source_target_pairs={{0,2},{2,0},{4,6},{6,4},{8,10},{10,8},{12,14},{14,12},{16,18},{18,... | collective-permute-start | bytes 1179656 | tf_op jit(solution)/shard_map/ppermute | solution.py:336
  22.3 2.5 %collective-permute-start.24 = (bf16[768,256]{1,0:T(8,128)(2,1)S(1)}, bf16[768,256]{1,0:T(8,128)(2,1)S(1)}, u32[]{:S(2)}, u32[]{:S(2)}) collective-permute-start(bf16[768,256]{1,0:T(8,128)(2,1)S(1)} %collective-permute-done.19.rest_0_), channel_id=1, source_target_pairs={{0,4},{2,6},{4,0},{6,2},{8,12},{10,14},{12,8},{14,10},{16,20},{18,... | collective-permute-start | bytes 1179656 | tf_op jit(solution)/shard_map/ppermute | solution.py:336
  26.1 2.1 %collective-permute-done.rest_0_ = bf16[768,256]{1,0:T(8,128)(2,1)S(1)} collective-permute-done((bf16[768,256]{1,0:T(8,128)(2,1)S(1)}, bf16[768,256]{1,0:T(8,128)(2,1)S(1)}, u32[]{:S(2)}, u32[]{:S(2)}) %collective-permute-start) | collective-permute-done | bytes 393248 | tf_op jit(solution)/shard_map/ppermute | solution.py:336
  34.6 1.7 collective-permute-start.9
  37.1 4.9 %collective-permute-done.17.rest_1_ = bf16[768,256]{1,0:T(8,128)(2,1)S(1)} collective-permute-done((bf16[768,256]{1,0:T(8,128)(2,1)}, bf16[768,256]{1,0:T(8,128)(2,1)S(1)}, u32[]{:S(2)}, u32[]{:S(2)}) %collective-permute-start.17) | collective-permute-done | bytes 393248 | tf_op jit(solution)/shard_map/ppermute | solution.py:336
  42.0 2.5 %collective-permute-start.21 = (bf16[768,256]{1,0:T(8,128)(2,1)S(1)}, bf16[768,256]{1,0:T(8,128)(2,1)S(1)}, u32[]{:S(2)}, u32[]{:S(2)}) collective-permute-start(bf16[768,256]{1,0:T(8,128)(2,1)S(1)} %collective-permute-done.20.rest_0_), channel_id=1, source_target_pairs={{0,4},{2,6},{4,0},{6,2},{8,12},{10,14},{12,8},{14,10},{16,20},{18,... | collective-permute-start | bytes 1179656 | tf_op jit(solution)/shard_map/ppermute | solution.py:336
  45.2 4.0 %collective-permute-done.6.rest_1_ = bf16[768,256]{1,0:T(8,128)(2,1)S(1)} collective-permute-done((bf16[768,256]{1,0:T(8,128)(2,1)S(1)}, bf16[768,256]{1,0:T(8,128)(2,1)S(1)}, u32[]{:S(2)}, u32[]{:S(2)}) %collective-permute-start.6) | collective-permute-done | bytes 393248 | tf_op jit(solution)/shard_map/ppermute | solution.py:336
  52.0 5.1 %stage_product.8 = (f32[6,768,768]{2,1,0:T(8,128)S(1)}, f32[768,256]{1,0:T(8,128)S(1)}, f32[256,256]{1,0:T(8,128)S(1)}) custom-call(s32[33]{0:T(128)S(1)} %pad_add_fusion.places_ref, f32[768,24576]{1,0:T(8,128)} %h_ref.15, bf16[768,256]{1,0:T(8,128)(2,1)S(1)} %convert_element_type.3.rest_0_.b_ref, bf16[768,256]{1,0:T(8,128)(2,1)S(1)} %copy-done.11), custom_call_target="tpu_custom_call" | custom-call | flops 1207959552 | bytes 4718592 | tf_op jit(solution)/shard_map/stage_product/pallas_call | solution.py:161
  58.8 4.0 %stage_product.9 = (f32[6,768,768]{2,1,0:T(8,128)S(1)}, f32[768,256]{1,0:T(8,128)S(1)}, f32[256,256]{1,0:T(8,128)S(1)}) custom-call(s32[33]{0:T(128)S(1)} %pad_add_fusion.places_ref, f32[768,24576]{1,0:T(8,128)} %h_ref.15, bf16[768,256]{1,0:T(8,128)(2,1)S(1)} %copy-done.1, ...), custom_call_target="tpu_custom_call", output_to_operand_aliasing={{0}: (5, {}), {1}: (6, {}), {2}: (7, {})} | custom-call | flops 1811939328 | bytes 7077888 | tf_op jit(solution)/shard_map/stage_product/pallas_call | solution.py:161
  63.4 6.0 %stage_product.10 = (f32[6,768,768]{2,1,0:T(8,128)S(1)}, f32[768,256]{1,0:T(8,128)S(1)}, f32[256,256]{1,0:T(8,128)S(1)}) custom-call(s32[33]{0:T(128)S(1)} %pad_add_fusion.places_ref, f32[768,24576]{1,0:T(8,128)} %h_ref.15, bf16[768,256]{1,0:T(8,128)(2,1)S(1)} %collective-permute-done.20.rest_0_, ...), custom_call_target="tpu_custom_call", output_to_operand_aliasing={{0}: (7, {}), {1}: (8, {}), {2}: (9, {})} | custom-call | flops 3019898880 | bytes 11796480 | tf_op jit(solution)/shard_map/stage_product/pallas_call | solution.py:161
  70.5 6.1 %stage_product.11 = (f32[6,768,768]{2,1,0:T(8,128)S(1)}, f32[768,256]{1,0:T(8,128)S(1)}, f32[256,256]{1,0:T(8,128)S(1)}) custom-call(s32[33]{0:T(128)S(1)} %pad_add_fusion.places_ref, f32[768,24576]{1,0:T(8,128)} %h_ref.15, bf16[768,256]{1,0:T(8,128)(2,1)S(1)} %collective-permute-done.rest_0_, ...), custom_call_target="tpu_custom_call", output_to_operand_aliasing={{0}: (7, {}), {1}: (8, {}), {2}: (9, {})} | custom-call | flops 3019898880 | bytes 11796480 | tf_op jit(solution)/shard_map/stage_product/pallas_call | solution.py:161
  77.3 7.1 %stage_product.12 = (f32[6,768,768]{2,1,0:T(8,128)S(1)}, f32[768,256]{1,0:T(8,128)S(1)}, f32[256,256]{1,0:T(8,128)S(1)}) custom-call(s32[33]{0:T(128)S(1)} %pad_add_fusion.places_ref, f32[768,24576]{1,0:T(8,128)} %h_ref.15, bf16[768,256]{1,0:T(8,128)(2,1)S(1)} %collective-permute-done.1.rest_0_, ...), custom_call_target="tpu_custom_call", output_to_operand_aliasing={{0}: (8, {}), {1}: (9, {}), {2}: (10, {})} | custom-call | flops 3623878656 | bytes 14155776 | tf_op jit(solution)/shard_map/stage_product/pallas_call | solution.py:161
  84.9 7.1 %stage_product.13 = (f32[6,768,768]{2,1,0:T(8,128)S(1)}, f32[768,256]{1,0:T(8,128)S(1)}, f32[256,256]{1,0:T(8,128)S(1)}) custom-call(s32[33]{0:T(128)S(1)} %pad_add_fusion.places_ref, f32[768,24576]{1,0:T(8,128)} %h_ref.15, bf16[768,256]{1,0:T(8,128)(2,1)S(1)} %collective-permute-done.2.rest_0_, ...), custom_call_target="tpu_custom_call", output_to_operand_aliasing={{0}: (8, {}), {1}: (9, {}), {2}: (10, {})} | custom-call | flops 3623878656 | bytes 14155776 | tf_op jit(solution)/shard_map/stage_product/pallas_call | solution.py:161
  92.1 5.0 %stage_product.14 = (f32[6,768,768]{2,1,0:T(8,128)S(1)}, f32[768,256]{1,0:T(8,128)S(1)}, f32[256,256]{1,0:T(8,128)S(1)}) custom-call(s32[33]{0:T(128)S(1)} %pad_add_fusion.places_ref, f32[768,24576]{1,0:T(8,128)} %h_ref.15, bf16[768,256]{1,0:T(8,128)(2,1)S(1)} %collective-permute-done.3.rest_0_, ...), custom_call_target="tpu_custom_call", output_to_operand_aliasing={{0}: (6, {}), {1}: (7, {}), {2}: (8, {})} | custom-call | flops 2415919104 | bytes 9437184 | tf_op jit(solution)/shard_map/stage_product/pallas_call | solution.py:161
  103.4 2.0 collective-permute-start.34
  106.0 1.8 collective-permute-done.33
  108.4 2.1 collective-permute-start.35
  113.0 3.2 %collective-permute-done.36 = f32[96,128]{1,0:T(8,128)S(1)} collective-permute-done((f32[96,128]{1,0:T(8,128)S(1)}, f32[96,128]{1,0:T(8,128)S(1)}, u32[]{:S(2)}, u32[]{:S(2)}) %collective-permute-start.36) | collective-permute-done | bytes 49184 | tf_op jit(solution)/shard_map/ppermute | solution.py:336
  123.1 2.1 %collective-permute-done.40 = f32[96,128]{1,0:T(8,128)S(1)} collective-permute-done((f32[96,128]{1,0:T(8,128)S(1)}, f32[96,128]{1,0:T(8,128)S(1)}, u32[]{:S(2)}, u32[]{:S(2)}) %collective-permute-start.40) | collective-permute-done | bytes 49184 | tf_op jit(solution)/shard_map/ppermute | solution.py:336
  125.3 39.4 %inverse_factor.1.low_ref = f32[256,256]{1,0:T(8,128)S(1)} custom-call(f32[256,256]{1,0:T(8,128)S(1)} %get-tuple-element.49.near_ref, f32[256,256]{1,0:T(8,128)S(1)} %collective-permute-done.42.far_ref), custom_call_target="tpu_custom_call" | custom-call | flops 1006632960 | tf_op jit(solution)/shard_map/inverse_factor/pallas_call | solution.py:251
  164.7 41.7 %finish.1 = (f32[768,256]{1,0:T(8,128)}, f32[256,256]{1,0:T(8,128)}) custom-call(s32[33]{0:T(128)S(1)} %pad_add_fusion.places_ref, f32[768,256]{1,0:T(8,128)S(1)} %get-tuple-element.46.p_ref, f32[4,96,128]{2,1,0:T(8,128)S(1)} %pad_maximum_fusion.mine_ref, f32[4,96,128]{2,1,0:T(8,128)S(1)} %collective-permute-done.41.other_ref, ...), custom_call_target="tpu_custom_call" | custom-call | tf_op jit(solution)/shard_map/finish/pallas_call | solution.py:291
  (105 shorter events, 38.1 us)
Async XLA Ops:
  1.8 17.1 %collective-permute-start.19 = (bf16[768,256]{1,0:T(8,128)(2,1)S(1)}, bf16[768,256]{1,0:T(8,128)(2,1)S(1)}, u32[]{:S(2)}, u32[]{:S(2)}) collective-permute-start(bf16[768,256]{1,0:T(8,128)(2,1)S(1)} %convert_element_type.3.rest_0_.b_ref), channel_id=1, source_target_pairs={{0,8},{2,10},{4,12},{6,14},{8,0},{10,2},{12,4},{14,6},{16,24},{18,... | collective-permute-start | bytes 1179656 | tf_op jit(solution)/shard_map/ppermute | solution.py:336
  4.9 16.6 %collective-permute-start.30 = (bf16[768,256]{1,0:T(8,128)(2,1)S(1)}, bf16[768,256]{1,0:T(8,128)(2,1)S(1)}, u32[]{:S(2)}, u32[]{:S(2)}) collective-permute-start(bf16[768,256]{1,0:T(8,128)(2,1)S(1)} %convert_element_type.3.rest_0_.b_ref), channel_id=1, source_target_pairs={{0,1},{1,0},{2,3},{3,2},{4,5},{5,4},{6,7},{7,6},{8,9},{9,8},{10,11... | collective-permute-start | bytes 1179656 | tf_op jit(solution)/shard_map/ppermute | solution.py:339
  4.9 19.9 %collective-permute-start.16 = (bf16[768,256]{1,0:T(8,128)(2,1)S(1)}, bf16[768,256]{1,0:T(8,128)(2,1)}, u32[]{:S(2)}, u32[]{:S(2)}) collective-permute-start(bf16[768,256]{1,0:T(8,128)(2,1)S(1)} %convert_element_type.3.rest_0_.b_ref), channel_id=1, source_target_pairs={{0,4},{2,6},{4,0},{6,2},{8,12},{10,14},{12,8},{14,10},{16,20},{18,... | collective-permute-start | bytes 1179656 | tf_op jit(solution)/shard_map/ppermute | solution.py:336
  6.4 19.2 %collective-permute-start.27 = (bf16[768,256]{1,0:T(8,128)(2,1)S(1)}, bf16[768,256]{1,0:T(8,128)(2,1)S(1)}, u32[]{:S(2)}, u32[]{:S(2)}) collective-permute-start(bf16[768,256]{1,0:T(8,128)(2,1)S(1)} %convert_element_type.3.rest_0_.b_ref), channel_id=1, source_target_pairs={{0,2},{2,0},{4,6},{6,4},{8,10},{10,8},{12,14},{14,12},{16,18},{18,... | collective-permute-start | bytes 1179656 | tf_op jit(solution)/shard_map/ppermute | solution.py:336
  7.9 20.3 %collective-permute-start = (bf16[768,256]{1,0:T(8,128)(2,1)S(1)}, bf16[768,256]{1,0:T(8,128)(2,1)S(1)}, u32[]{:S(2)}, u32[]{:S(2)}) collective-permute-start(bf16[768,256]{1,0:T(8,128)(2,1)S(1)} %convert_element_type.3.rest_0_.b_ref), channel_id=1, source_target_pairs={{0,16},{2,18},{4,20},{6,22},{8,24},{10,26},{12,28},{14,30},{16,0},... | collective-permute-start | bytes 1179656 | tf_op jit(solution)/shard_map/ppermute | solution.py:336
  33.6 15.6 %collective-permute-start.6 = (bf16[768,256]{1,0:T(8,128)(2,1)S(1)}, bf16[768,256]{1,0:T(8,128)(2,1)S(1)}, u32[]{:S(2)}, u32[]{:S(2)}) collective-permute-start(bf16[768,256]{1,0:T(8,128)(2,1)S(1)} %collective-permute-done.rest_0_), channel_id=1, source_target_pairs={{0,2},{2,0},{4,6},{6,4},{8,10},{10,8},{12,14},{14,12},{16,18},{18,... | collective-permute-start | bytes 1179656 | tf_op jit(solution)/shard_map/ppermute | solution.py:336
  34.6 14.6 %collective-permute-start.9 = (bf16[768,256]{1,0:T(8,128)(2,1)S(1)}, bf16[768,256]{1,0:T(8,128)(2,1)S(1)}, u32[]{:S(2)}, u32[]{:S(2)}) collective-permute-start(bf16[768,256]{1,0:T(8,128)(2,1)S(1)} %collective-permute-done.rest_0_), channel_id=1, source_target_pairs={{0,4},{2,6},{4,0},{6,2},{8,12},{10,14},{12,8},{14,10},{16,20},{18,... | collective-permute-start | bytes 1179656 | tf_op jit(solution)/shard_map/ppermute | solution.py:336
  37.1 12.6 %collective-permute-start.15 = (bf16[768,256]{1,0:T(8,128)(2,1)S(1)}, bf16[768,256]{1,0:T(8,128)(2,1)S(1)}, u32[]{:S(2)}, u32[]{:S(2)}) collective-permute-start(bf16[768,256]{1,0:T(8,128)(2,1)S(1)} %collective-permute-done.rest_0_), channel_id=1, source_target_pairs={{0,1},{1,0},{2,3},{3,2},{4,5},{5,4},{6,7},{7,6},{8,9},{9,8},{10,11... | collective-permute-start | bytes 1179656 | tf_op jit(solution)/shard_map/ppermute | solution.py:339
  42.0 15.2 %collective-permute-start.21 = (bf16[768,256]{1,0:T(8,128)(2,1)S(1)}, bf16[768,256]{1,0:T(8,128)(2,1)S(1)}, u32[]{:S(2)}, u32[]{:S(2)}) collective-permute-start(bf16[768,256]{1,0:T(8,128)(2,1)S(1)} %collective-permute-done.20.rest_0_), channel_id=1, source_target_pairs={{0,4},{2,6},{4,0},{6,2},{8,12},{10,14},{12,8},{14,10},{16,20},{18,... | collective-permute-start | bytes 1179656 | tf_op jit(solution)/shard_map/ppermute | solution.py:336
  44.5 14.2 %collective-permute-start.23 = (bf16[768,256]{1,0:T(8,128)(2,1)S(1)}, bf16[768,256]{1,0:T(8,128)(2,1)S(1)}, u32[]{:S(2)}, u32[]{:S(2)}) collective-permute-start(bf16[768,256]{1,0:T(8,128)(2,1)S(1)} %collective-permute-done.20.rest_0_), channel_id=1, source_target_pairs={{0,1},{1,0},{2,3},{3,2},{4,5},{5,4},{6,7},{7,6},{8,9},{9,8},{10,11... | collective-permute-start | bytes 1179656 | tf_op jit(solution)/shard_map/ppermute | solution.py:339
  49.2 13.5 %collective-permute-start.25 = (bf16[768,256]{1,0:T(8,128)(2,1)S(1)}, bf16[768,256]{1,0:T(8,128)(2,1)S(1)}, u32[]{:S(2)}, u32[]{:S(2)}) collective-permute-start(bf16[768,256]{1,0:T(8,128)(2,1)S(1)} %collective-permute-done.24.rest_1_), channel_id=1, source_target_pairs={{0,1},{1,0},{2,3},{3,2},{4,5},{5,4},{6,7},{7,6},{8,9},{9,8},{10,11... | collective-permute-start | bytes 1179656 | tf_op jit(solution)/shard_map/ppermute | solution.py:339
  49.2 13.6 %collective-permute-start.18 = (bf16[768,256]{1,0:T(8,128)(2,1)S(1)}, bf16[768,256]{1,0:T(8,128)(2,1)S(1)}, u32[]{:S(2)}, u32[]{:S(2)}) collective-permute-start(bf16[768,256]{1,0:T(8,128)(2,1)S(1)} %collective-permute-done.17.rest_1_), channel_id=1, source_target_pairs={{0,1},{1,0},{2,3},{3,2},{4,5},{5,4},{6,7},{7,6},{8,9},{9,8},{10,11... | collective-permute-start | bytes 1179656 | tf_op jit(solution)/shard_map/ppermute | solution.py:339
  49.7 13.6 %collective-permute-start.2 = (bf16[768,256]{1,0:T(8,128)(2,1)S(1)}, bf16[768,256]{1,0:T(8,128)(2,1)S(1)}, u32[]{:S(2)}, u32[]{:S(2)}) collective-permute-start(bf16[768,256]{1,0:T(8,128)(2,1)S(1)} %collective-permute-done.1.rest_0_), channel_id=1, source_target_pairs={{0,4},{2,6},{4,0},{6,2},{8,12},{10,14},{12,8},{14,10},{16,20},{18,... | collective-permute-start | bytes 1179656 | tf_op jit(solution)/shard_map/ppermute | solution.py:336
  57.2 12.3 %collective-permute-start.10 = (bf16[768,256]{1,0:T(8,128)(2,1)S(1)}, bf16[768,256]{1,0:T(8,128)(2,1)S(1)}, u32[]{:S(2)}, u32[]{:S(2)}) collective-permute-start(bf16[768,256]{1,0:T(8,128)(2,1)S(1)} %collective-permute-done.9.rest_2_), channel_id=1, source_target_pairs={{0,2},{2,0},{4,6},{6,4},{8,10},{10,8},{12,14},{14,12},{16,18},{18,... | collective-permute-start | bytes 1179656 | tf_op jit(solution)/shard_map/ppermute | solution.py:336
  62.7 13.9 %collective-permute-start.12 = (bf16[768,256]{1,0:T(8,128)(2,1)S(1)}, bf16[768,256]{1,0:T(8,128)(2,1)S(1)}, u32[]{:S(2)}, u32[]{:S(2)}) collective-permute-start(bf16[768,256]{1,0:T(8,128)(2,1)S(1)} %collective-permute-done.1.rest_0_), channel_id=1, source_target_pairs={{0,1},{1,0},{2,3},{3,2},{4,5},{5,4},{6,7},{7,6},{8,9},{9,8},{10,11... | collective-permute-start | bytes 1179656 | tf_op jit(solution)/shard_map/ppermute | solution.py:339
  62.8 13.9 %collective-permute-start.13 = (bf16[768,256]{1,0:T(8,128)(2,1)S(1)}, bf16[768,256]{1,0:T(8,128)(2,1)S(1)}, u32[]{:S(2)}, u32[]{:S(2)}) collective-permute-start(bf16[768,256]{1,0:T(8,128)(2,1)S(1)} %collective-permute-done.6.rest_1_), channel_id=1, source_target_pairs={{0,1},{1,0},{2,3},{3,2},{4,5},{5,4},{6,7},{7,6},{8,9},{9,8},{10,11... | collective-permute-start | bytes 1179656 | tf_op jit(solution)/shard_map/ppermute | solution.py:339
  63.3 13.9 %collective-permute-start.22 = (bf16[768,256]{1,0:T(8,128)(2,1)S(1)}, bf16[768,256]{1,0:T(8,128)(2,1)S(1)}, u32[]{:S(2)}, u32[]{:S(2)}) collective-permute-start(bf16[768,256]{1,0:T(8,128)(2,1)S(1)} %collective-permute-done.21.rest_2_), channel_id=1, source_target_pairs={{0,1},{1,0},{2,3},{3,2},{4,5},{5,4},{6,7},{7,6},{8,9},{9,8},{10,11... | collective-permute-start | bytes 1179656 | tf_op jit(solution)/shard_map/ppermute | solution.py:339
  69.4 15.5 %collective-permute-start.14 = (bf16[768,256]{1,0:T(8,128)(2,1)S(1)}, bf16[768,256]{1,0:T(8,128)(2,1)S(1)}, u32[]{:S(2)}, u32[]{:S(2)}) collective-permute-start(bf16[768,256]{1,0:T(8,128)(2,1)S(1)} %collective-permute-done.9.rest_2_), channel_id=1, source_target_pairs={{0,1},{1,0},{2,3},{3,2},{4,5},{5,4},{6,7},{7,6},{8,9},{9,8},{10,11... | collective-permute-start | bytes 1179656 | tf_op jit(solution)/shard_map/ppermute | solution.py:339
  69.9 14.5 %collective-permute-start.3 = (bf16[768,256]{1,0:T(8,128)(2,1)S(1)}, bf16[768,256]{1,0:T(8,128)(2,1)S(1)}, u32[]{:S(2)}, u32[]{:S(2)}) collective-permute-start(bf16[768,256]{1,0:T(8,128)(2,1)S(1)} %collective-permute-done.2.rest_0_), channel_id=1, source_target_pairs={{0,2},{2,0},{4,6},{6,4},{8,10},{10,8},{12,14},{14,12},{16,18},{18,... | collective-permute-start | bytes 1179656 | tf_op jit(solution)/shard_map/ppermute | solution.py:336
  76.6 15.4 %collective-permute-start.5 = (bf16[768,256]{1,0:T(8,128)(2,1)S(1)}, bf16[768,256]{1,0:T(8,128)(2,1)S(1)}, u32[]{:S(2)}, u32[]{:S(2)}) collective-permute-start(bf16[768,256]{1,0:T(8,128)(2,1)S(1)} %collective-permute-done.2.rest_0_), channel_id=1, source_target_pairs={{0,1},{1,0},{2,3},{3,2},{4,5},{5,4},{6,7},{7,6},{8,9},{9,8},{10,11... | collective-permute-start | bytes 1179656 | tf_op jit(solution)/shard_map/ppermute | solution.py:339
  76.7 15.4 %collective-permute-start.11 = (bf16[768,256]{1,0:T(8,128)(2,1)S(1)}, bf16[768,256]{1,0:T(8,128)(2,1)S(1)}, u32[]{:S(2)}, u32[]{:S(2)}) collective-permute-start(bf16[768,256]{1,0:T(8,128)(2,1)S(1)} %collective-permute-done.10.rest_2_), channel_id=1, source_target_pairs={{0,1},{1,0},{2,3},{3,2},{4,5},{5,4},{6,7},{7,6},{8,9},{9,8},{10,11... | collective-permute-start | bytes 1179656 | tf_op jit(solution)/shard_map/ppermute | solution.py:339
  77.2 14.9 %collective-permute-start.8 = (bf16[768,256]{1,0:T(8,128)(2,1)S(1)}, bf16[768,256]{1,0:T(8,128)(2,1)S(1)}, u32[]{:S(2)}, u32[]{:S(2)}) collective-permute-start(bf16[768,256]{1,0:T(8,128)(2,1)S(1)} %collective-permute-done.7.rest_1_), channel_id=1, source_target_pairs={{0,1},{1,0},{2,3},{3,2},{4,5},{5,4},{6,7},{7,6},{8,9},{9,8},{10,11... | collective-permute-start | bytes 1179656 | tf_op jit(solution)/shard_map/ppermute | solution.py:339
  84.5 12.7 %collective-permute-start.4 = (bf16[768,256]{1,0:T(8,128)(2,1)S(1)}, bf16[768,256]{1,0:T(8,128)(2,1)S(1)}, u32[]{:S(2)}, u32[]{:S(2)}) collective-permute-start(bf16[768,256]{1,0:T(8,128)(2,1)S(1)} %collective-permute-done.3.rest_0_), channel_id=1, source_target_pairs={{0,1},{1,0},{2,3},{3,2},{4,5},{5,4},{6,7},{7,6},{8,9},{9,8},{10,11... | collective-permute-start | bytes 1179656 | tf_op jit(solution)/shard_map/ppermute | solution.py:339
  125.2 39.5 %collective-permute-start.41 = (f32[4,96,128]{2,1,0:T(8,128)S(1)}, f32[4,96,128]{2,1,0:T(8,128)S(1)}, u32[]{:S(2)}, u32[]{:S(2)}) collective-permute-start(f32[4,96,128]{2,1,0:T(8,128)S(1)} %pad_maximum_fusion.mine_ref), channel_id=1, source_target_pairs={{0,1},{1,0},{2,3},{3,2},{4,5},{5,4},{6,7},{7,6},{8,9},{9,8},{10,11... | collective-permute-start | bytes 589832 | tf_op jit(solution)/shard_map/ppermute | solution.py:339
  (31 other events, 162.7 us)
